TPU v7x, 512 devices: a whole 4x4x16 slice. The times are simulated.
512 devices in a mesh: state: 16 (over x, y_lo, core), snap: 32 (over y_hi, z).
Axes of the slice: x: 4, y: 4 (y_hi: 2, y_lo: 2; y = y_hi * 2 + y_lo), z: 16, core: 2. Of those that a mesh axis runs over, the one named last changes fastest.
Arguments:
- direct: float32 [8192, 4096], P('state', 'snap'), may hold values from -6 to 6
- adjoint: float32 [8192, 4096], P('state', 'snap'), may hold values from -6 to 6
- cell_weight: float32 [8192], P('state'), may hold values from 0.003314563 to 0.03314563
- right_vecs: float32 [4096, 256], P('snap'), may hold values from -0.09375 to 0.09375
- left_vecs: float32 [4096, 256], P('snap'), may hold values from -0.09375 to 0.09375
- inv_root: float32 [256], replicated, may hold values from 0.5 to 2
Outputs:
- gram: float32 [4096, 4096], P('state', 'snap')
- bal_modes: float32 [8192, 256], P(('state', 'snap'))
- adj_modes: float32 [8192, 256], P(('state', 'snap'))
All inputs are finite; a program needn't handle non-finite values.
Results may differ from a plain program's by a relative error of at most 0.00013.
Values sent between devices are 32-bit elements; how exact they have to be, the bound alone decides.
No kernel may reach another device: no remote copies, remote signals or barrier semaphores. Data moves between devices by JAX's collectives and lax.ppermute only.
A program may use at most 64 MiB of HBM per device.

v0:
```python
import jax
import jax.numpy as jnp
from jax import lax
from jax.sharding import Mesh, PartitionSpec as P


AXES = ("x", "l", "c", "h", "g", "q")
SIZES = (4, 2, 2, 2, 8, 2)
PREC = lax.Precision.HIGH
SWAP = [(0, 1), (1, 0)]


def _ring_pairs(up):
    pairs = []
    for g in range(8):
        if up:
            pairs.append((g, (g + 1) % 8))
        pairs.append((8 + g, 8 + (g - 1) % 8))
    return pairs


def _home_pairs():
    pairs = []
    for x in range(4):
        for l in range(2):
            for c in range(2):
                for h in range(2):
                    for g in range(8):
                        low = (g - x if c == 0 else g + 1 + x) % 8
                        here = (((x * 2 + l) * 2 + c) * 2 + h) * 8 + g
                        pairs.append((here, ((h * 8 + low) * 2 + l) * 8 + g))
    return pairs


def _dot(a, b):
    return jnp.dot(a, b, precision=PREC, preferred_element_type=jnp.float32)


def _cross(a, b):
    return lax.dot_general(a, b, (((0,), (0,)), ((), ())), precision=PREC, preferred_element_type=jnp.float32)


def _beside(index, mine, theirs):
    return jnp.where(
        index == 0, jnp.concatenate([mine, theirs], axis=1), jnp.concatenate([theirs, mine], axis=1)
    )


def local(direct, adjoint, cell_weight, right_vecs, left_vecs, inv_root):
    c, h, q = lax.axis_index("c"), lax.axis_index("h"), lax.axis_index("q")
    cells, cols = direct.shape
    modes = right_vecs.shape[1]

    other = lax.ppermute(adjoint, "c", SWAP)
    next_own = lax.ppermute(adjoint, ("c", "g"), _ring_pairs(False))
    next_other = lax.ppermute(other, ("c", "g"), _ring_pairs(False))
    own = jnp.where(c == 0, adjoint, next_own)
    other = jnp.where(c == 0, other, next_other)

    scale = inv_root[None, :]
    terms = jnp.concatenate([_dot(direct, right_vecs * scale), _dot(adjoint, left_vecs * scale)], axis=1)
    terms = terms.reshape(2, 16, cells // 32, 2 * modes).transpose(1, 0, 2, 3).reshape(cells, 2 * modes)
    own, other, terms = lax.optimization_barrier((own, other, terms))
    part = lax.psum_scatter(terms, ("g", "q"), scatter_dimension=0, tiled=True).reshape(2, cells // 32, 2 * modes)

    pair = _beside(q, direct, lax.ppermute(direct, "q", SWAP)) * cell_weight[:, None]
    both = _beside(h, pair, lax.ppermute(pair, "h", SWAP))
    other_both = lax.ppermute(both, "c", SWAP)

    pieces = []
    for step in range(4):
        product = _cross(own, both) + _cross(other, other_both)
        piece = jnp.stack([product[:, k * cols : (k + 1) * cols] for k in range(4)])
        if step < 3:
            own = lax.ppermute(own, ("c", "g"), _ring_pairs(True))
            other = lax.ppermute(other, ("c", "g"), _ring_pairs(True))
        pieces.append(lax.optimization_barrier(piece))

    got = lax.all_to_all(jnp.concatenate(pieces), ("x", "l", "q"), 0, 0, tiled=True)
    block = got.reshape(8, 2 * cols, cols).sum(0)
    gram = lax.ppermute(block, ("x", "l", "c", "h", "g"), _home_pairs())

    keep = lax.dynamic_index_in_dim(part, h, 0, keepdims=False)
    away = lax.dynamic_index_in_dim(part, 1 - h, 0, keepdims=False)
    summed = keep + lax.ppermute(away, "h", SWAP)
    return (gram, summed[:, :modes], summed[:, modes:])


def solution(mesh):
    fine = Mesh(mesh.devices.reshape(SIZES), AXES)
    state, snap = ("x", "l", "c"), ("h", "g", "q")
    in_specs = (P(state, snap), P(state, snap), P(state), P(snap, None), P(snap, None), P())
    out_specs = (P(state, snap), P(state + snap, None), P(state + snap, None))


    return jax.shard_map(local, mesh=fine, in_specs=in_specs, out_specs=out_specs, check_vma=False)
```

profile of v0, /device:TPU:4, one launch (start us, length us, event | category | flops | bytes accessed | tf_op | source)
XLA Modules:
  0.0 200.2 jit_solution(15087341004207037435)
XLA Ops:
  7.2 3.8 %collective-permute-start.3 = (f32[512,128]{1,0:T(8,128)}, f32[512,128]{1,0:T(8,128)S(1)}, u32[]{:S(2)}, u32[]{:S(2)}) collective-permute-start(f32[512,128]{1,0:T(8,128)} %param.6), channel_id=1, source_target_pairs={{0,1},{1,0},{2,3},{3,2},{4,5},{5,4},{6,7},{7,6},{8,9},{9,8},{10,11... | collective-permute-start | bytes 786440 | tf_op jit(solution)/shard_map/ppermute | solution.py:66
  11.1 6.4 %collective-permute-done.3 = f32[512,128]{1,0:T(8,128)S(1)} collective-permute-done((f32[512,128]{1,0:T(8,128)}, f32[512,128]{1,0:T(8,128)S(1)}, u32[]{:S(2)}, u32[]{:S(2)}) %collective-permute-start.3) | collective-permute-done | bytes 262176 | tf_op jit(solution)/shard_map/ppermute | solution.py:66
  17.5 1.2 fusion
  18.7 0.0 copy-start.4
  18.7 5.2 %collective-permute-start.4 = (f32[512,256]{1,0:T(8,128)S(1)}, f32[512,256]{1,0:T(8,128)S(1)}, u32[]{:S(2)}, u32[]{:S(2)}) collective-permute-start(f32[512,256]{1,0:T(8,128)S(1)} %fusion), channel_id=1, source_target_pairs={{0,16},{16,0},{1,17},{17,1},{2,18},{18,2},{3,19},{19,3},{4,20},{20... | collective-permute-start | bytes 1572872 | tf_op jit(solution)/shard_map/ppermute | solution.py:67
  24.0 1.4 collective-permute-start
  25.3 10.6 %collective-permute-start.1 = (f32[512,128]{1,0:T(8,128)S(1)}, f32[512,128]{1,0:T(8,128)}, u32[]{:S(2)}, u32[]{:S(2)}) collective-permute-start(f32[512,128]{1,0:T(8,128)S(1)} %copy-done.2), channel_id=1, source_target_pairs={{0,32},{32,0},{1,33},{33,1},{2,34},{34,2},{3,35},{35,3},{4,36},{36... | collective-permute-start | bytes 786440 | tf_op jit(solution)/shard_map/ppermute | solution.py:54
  36.0 1.2 convolution_bitcast_fusion.1
  37.2 0.4 convolution_bitcast_fusion
  37.7 1.5 collective-permute-start.2
  39.2 0.2 maximum_select_fusion
  39.4 3.7 %collective-permute-start.5 = (f32[512,512]{1,0:T(8,128)S(1)}, f32[512,512]{1,0:T(8,128)S(1)}, u32[]{:S(2)}, u32[]{:S(2)}) collective-permute-start(f32[512,512]{1,0:T(8,128)S(1)} %maximum_select_fusion), channel_id=1, source_target_pairs={{0,32},{32,0},{1,33},{33,1},{2,34},{34,2},{3,35},{35,3},{4,36},{36... | collective-permute-start | bytes 3145736 | tf_op jit(solution)/shard_map/ppermute | solution.py:68
  43.1 0.1 pad_maximum_fusion
  43.2 1.3 copy.9
  44.5 2.4 %copy.10 = f32[16,2,16,512]{3,2,1,0:T(8,128)} copy(f32[16,2,16,512]{3,2,0,1:T(8,128)} %bitcast.68) | data formatting | bytes 2097152 | tf_op jit(solution)/shard_map/transpose | solution.py:62
  46.9 1.0 broadcast_select_fusion
  47.9 3.3 %collective-permute-start.6 = (f32[512,128]{1,0:T(8,128)S(1)}, f32[512,128]{1,0:T(8,128)S(1)}, u32[]{:S(2)}, u32[]{:S(2)}) collective-permute-start(f32[512,128]{1,0:T(8,128)S(1)} %broadcast_select_fusion.1), channel_id=1, source_target_pairs={{0,2},{32,46},{2,4},{34,32},{4,6},{36,34},{6,8},{38,36},{8,10},{40... | collective-permute-start | bytes 786440 | tf_op jit(solution)/shard_map/ppermute | solution.py:75
  51.2 2.5 %collective-permute-start.7 = (f32[512,128]{1,0:T(8,128)S(1)}, f32[512,128]{1,0:T(8,128)S(1)}, u32[]{:S(2)}, u32[]{:S(2)}) collective-permute-start(f32[512,128]{1,0:T(8,128)S(1)} %broadcast_select_fusion), channel_id=1, source_target_pairs={{0,2},{32,46},{2,4},{34,32},{4,6},{36,34},{6,8},{38,36},{8,10},{40... | collective-permute-start | bytes 786440 | tf_op jit(solution)/shard_map/ppermute | solution.py:76
  53.7 5.1 %collective-permute-done.6 = f32[512,128]{1,0:T(8,128)S(1)} collective-permute-done((f32[512,128]{1,0:T(8,128)S(1)}, f32[512,128]{1,0:T(8,128)S(1)}, u32[]{:S(2)}, u32[]{:S(2)}) %collective-permute-start.6) | collective-permute-done | bytes 262176 | tf_op jit(solution)/shard_map/ppermute | solution.py:75
  58.8 2.2 %collective-permute-start.8 = (f32[512,128]{1,0:T(8,128)S(1)}, f32[512,128]{1,0:T(8,128)S(1)}, u32[]{:S(2)}, u32[]{:S(2)}) collective-permute-start(f32[512,128]{1,0:T(8,128)S(1)} %collective-permute-done.6), channel_id=1, source_target_pairs={{0,2},{32,46},{2,4},{34,32},{4,6},{36,34},{6,8},{38,36},{8,10},{40... | collective-permute-start | bytes 786440 | tf_op jit(solution)/shard_map/ppermute | solution.py:75
  61.0 2.5 %collective-permute-done.7 = f32[512,128]{1,0:T(8,128)S(1)} collective-permute-done((f32[512,128]{1,0:T(8,128)S(1)}, f32[512,128]{1,0:T(8,128)S(1)}, u32[]{:S(2)}, u32[]{:S(2)}) %collective-permute-start.7) | collective-permute-done | bytes 262176 | tf_op jit(solution)/shard_map/ppermute | solution.py:76
  63.5 1.9 collective-permute-start.9
  65.4 5.0 %collective-permute-done.8 = f32[512,128]{1,0:T(8,128)S(1)} collective-permute-done((f32[512,128]{1,0:T(8,128)S(1)}, f32[512,128]{1,0:T(8,128)S(1)}, u32[]{:S(2)}, u32[]{:S(2)}) %collective-permute-start.8) | collective-permute-done | bytes 262176 | tf_op jit(solution)/shard_map/ppermute | solution.py:75
  70.4 2.8 %collective-permute-start.10 = (f32[512,128]{1,0:T(8,128)S(1)}, f32[512,128]{1,0:T(8,128)S(1)}, u32[]{:S(2)}, u32[]{:S(2)}) collective-permute-start(f32[512,128]{1,0:T(8,128)S(1)} %collective-permute-done.8), channel_id=1, source_target_pairs={{0,2},{32,46},{2,4},{34,32},{4,6},{36,34},{6,8},{38,36},{8,10},{40... | collective-permute-start | bytes 786440 | tf_op jit(solution)/shard_map/ppermute | solution.py:75
  73.2 6.9 %collective-permute-done.9 = f32[512,128]{1,0:T(8,128)S(1)} collective-permute-done((f32[512,128]{1,0:T(8,128)S(1)}, f32[512,128]{1,0:T(8,128)S(1)}, u32[]{:S(2)}, u32[]{:S(2)}) %collective-permute-start.9) | collective-permute-done | bytes 262176 | tf_op jit(solution)/shard_map/ppermute | solution.py:76
  80.1 1.9 collective-permute-start.11
  82.0 0.4 fusion.6
  82.5 0.4 convolution_add_fusion.3
  82.9 0.5 fusion.7
  83.4 0.5 convolution_add_fusion.2
  84.0 0.5 fusion.8
  84.5 0.5 convolution_add_fusion.1
  85.0 7.7 %collective-permute-done.11 = f32[512,128]{1,0:T(8,128)S(1)} collective-permute-done((f32[512,128]{1,0:T(8,128)S(1)}, f32[512,128]{1,0:T(8,128)S(1)}, u32[]{:S(2)}, u32[]{:S(2)}) %collective-permute-start.11) | collective-permute-done | bytes 262176 | tf_op jit(solution)/shard_map/ppermute | solution.py:76
  92.7 0.5 fusion.9
  93.2 0.5 convolution_add_fusion
  93.7 1.1 pad_maximum_fusion.1
  94.8 6.4 %all-to-all-start = ((f32[16,128,128]{2,1,0:T(8,128)}), f32[16,128,128]{2,1,0:T(8,128)S(1)}, u32[]{:S(2)}, u32[]{:S(2)}) async-start(f32[16,128,128]{2,1,0:T(8,128)} %pad_maximum_fusion.1), calls=%async_computation | async-start | bytes 2097152 | tf_op jit(solution)/shard_map/all_to_all | solution.py:79
  101.2 0.0 reduce-scatter.2.cloned.1.call-start
  101.2 0.7 reduce-scatter.2.cloned.1.call-update
  101.9 71.8 %reduce-scatter.2.cloned.1.call-done = f32[32,512]{1,0:T(8,128)} async-done(((f32[512,512]{1,0:T(8,128)}), f32[32,512]{1,0:T(8,128)}) %reduce-scatter.2.cloned.1.call-update) | async-done | bytes 65552 | tf_op jit(solution)/shard_map/reduce_scatter | solution.py:64
  173.7 0.8 dynamic-slice_bitcast_fusion
  174.6 4.9 %collective-permute-start.13 = (f32[16,512]{1,0:T(8,128)S(1)}, f32[16,512]{1,0:T(8,128)S(1)}, u32[]{:S(2)}, u32[]{:S(2)}) collective-permute-start(f32[16,512]{1,0:T(8,128)S(1)} %dynamic-slice_bitcast_fusion), channel_id=1, source_target_pairs={{0,16},{16,0},{1,17},{17,1},{2,18},{18,2},{3,19},{19,3},{4,20},{20... | collective-permute-start | bytes 98312 | tf_op jit(solution)/shard_map/ppermute | solution.py:85
  179.5 2.4 %collective-permute-done.13 = f32[16,512]{1,0:T(8,128)S(1)} collective-permute-done((f32[16,512]{1,0:T(8,128)S(1)}, f32[16,512]{1,0:T(8,128)S(1)}, u32[]{:S(2)}, u32[]{:S(2)}) %collective-permute-start.13) | collective-permute-done | bytes 32800 | tf_op jit(solution)/shard_map/ppermute | solution.py:85
  181.9 0.1 bitcast_reduce_fusion
  182.0 3.4 %collective-permute-start.12 = (f32[256,128]{1,0:T(8,128)S(1)}, f32[256,128]{1,0:T(8,128)S(1)}, u32[]{:S(2)}, u32[]{:S(2)}) collective-permute-start(f32[256,128]{1,0:T(8,128)S(1)} %bitcast_reduce_fusion), channel_id=1, source_target_pairs={{0,0},{2,34},{4,68},{6,102},{8,136},{10,170},{12,204},{14,238},{16... | collective-permute-start | bytes 393224 | tf_op jit(solution)/shard_map/ppermute | solution.py:81
  185.4 0.6 fusion.5
  186.0 6.7 %collective-permute-done.12 = f32[256,128]{1,0:T(8,128)S(1)} collective-permute-done((f32[256,128]{1,0:T(8,128)S(1)}, f32[256,128]{1,0:T(8,128)S(1)}, u32[]{:S(2)}, u32[]{:S(2)}) %collective-permute-start.12) | collective-permute-done | bytes 131104 | tf_op jit(solution)/shard_map/ppermute | solution.py:81
  192.7 0.7 copy.12
  (32 shorter events, 0.2 us)
Async XLA Ops:
  7.2 10.3 %collective-permute-start.3 = (f32[512,128]{1,0:T(8,128)}, f32[512,128]{1,0:T(8,128)S(1)}, u32[]{:S(2)}, u32[]{:S(2)}) collective-permute-start(f32[512,128]{1,0:T(8,128)} %param.6), channel_id=1, source_target_pairs={{0,1},{1,0},{2,3},{3,2},{4,5},{5,4},{6,7},{7,6},{8,9},{9,8},{10,11... | collective-permute-start | bytes 786440 | tf_op jit(solution)/shard_map/ppermute | solution.py:66
  11.0 6.5 %copy-start.7 = (f32[512]{0:T(512)S(1)}, f32[512]{0:T(512)}, u32[]{:S(2)}) copy-start(f32[512]{0:T(512)} %param.8) | copy-start | bytes 6148
  11.0 13.0 %copy-start.2 = (f32[512,128]{1,0:T(8,128)S(1)}, f32[512,128]{1,0:T(8,128)}, u32[]{:S(2)}) copy-start(f32[512,128]{1,0:T(8,128)} %param.7) | copy-start | bytes 786436
  11.0 25.0 %copy-start.1 = (f32[512,128]{1,0:T(8,128)S(1)}, f32[512,128]{1,0:T(8,128)}, u32[]{:S(2)}) copy-start(f32[512,128]{1,0:T(8,128)} %param.6) | copy-start | bytes 786436
  11.0 25.0 %copy-start.3 = (f32[128,256]{1,0:T(8,128)S(1)}, f32[128,256]{1,0:T(8,128)}, u32[]{:S(2)}) copy-start(f32[128,256]{1,0:T(8,128)} %param.9) | copy-start | bytes 393220
  11.0 25.0 %copy-start.6 = (f32[256]{0:T(256)S(1)}, f32[256]{0:T(256)}, u32[]{:S(2)}) copy-start(f32[256]{0:T(256)} %param.11) | copy-start | bytes 3076
  18.7 18.5 %copy-start.4 = (f32[128,256]{1,0:T(8,128)S(1)}, f32[128,256]{1,0:T(8,128)}, u32[]{:S(2)}) copy-start(f32[128,256]{1,0:T(8,128)} %param.10) | copy-start | bytes 393220
  18.7 20.5 %collective-permute-start.4 = (f32[512,256]{1,0:T(8,128)S(1)}, f32[512,256]{1,0:T(8,128)S(1)}, u32[]{:S(2)}, u32[]{:S(2)}) collective-permute-start(f32[512,256]{1,0:T(8,128)S(1)} %fusion), channel_id=1, source_target_pairs={{0,16},{16,0},{1,17},{17,1},{2,18},{18,2},{3,19},{19,3},{4,20},{20... | collective-permute-start | bytes 1572872 | tf_op jit(solution)/shard_map/ppermute | solution.py:67
  24.0 22.9 %collective-permute-start = (f32[512,128]{1,0:T(8,128)S(1)}, f32[512,128]{1,0:T(8,128)}, u32[]{:S(2)}, u32[]{:S(2)}) collective-permute-start(f32[512,128]{1,0:T(8,128)S(1)} %copy-done.2), channel_id=1, source_target_pairs={{32,46},{34,32},{36,34},{38,36},{40,38},{42,40},{44,42},{46,44},{3... | collective-permute-start | bytes 786440 | tf_op jit(solution)/shard_map/ppermute | solution.py:55
  25.3 12.3 %collective-permute-start.1 = (f32[512,128]{1,0:T(8,128)S(1)}, f32[512,128]{1,0:T(8,128)}, u32[]{:S(2)}, u32[]{:S(2)}) collective-permute-start(f32[512,128]{1,0:T(8,128)S(1)} %copy-done.2), channel_id=1, source_target_pairs={{0,32},{32,0},{1,33},{33,1},{2,34},{34,2},{3,35},{35,3},{4,36},{36... | collective-permute-start | bytes 786440 | tf_op jit(solution)/shard_map/ppermute | solution.py:54
  37.7 5.4 %copy-start = (f32[512,256]{0,1:T(8,128)S(1)}, f32[512,256]{0,1:T(8,128)}, u32[]{:S(2)}) copy-start(f32[512,256]{0,1:T(8,128)} %convolution_bitcast_fusion.1) | copy-start | bytes 1572868
  37.7 9.2 %collective-permute-start.2 = (f32[512,128]{1,0:T(8,128)}, f32[512,128]{1,0:T(8,128)}, u32[]{:S(2)}, u32[]{:S(2)}) collective-permute-start(f32[512,128]{1,0:T(8,128)} %collective-permute-done.1), channel_id=1, source_target_pairs={{32,46},{34,32},{36,34},{38,36},{40,38},{42,40},{44,42},{46,44},{3... | collective-permute-start | bytes 786440 | tf_op jit(solution)/shard_map/ppermute | solution.py:56
  39.4 42.7 %collective-permute-start.5 = (f32[512,512]{1,0:T(8,128)S(1)}, f32[512,512]{1,0:T(8,128)S(1)}, u32[]{:S(2)}, u32[]{:S(2)}) collective-permute-start(f32[512,512]{1,0:T(8,128)S(1)} %maximum_select_fusion), channel_id=1, source_target_pairs={{0,32},{32,0},{1,33},{33,1},{2,34},{34,2},{3,35},{35,3},{4,36},{36... | collective-permute-start | bytes 3145736 | tf_op jit(solution)/shard_map/ppermute | solution.py:68
  47.9 11.0 %collective-permute-start.6 = (f32[512,128]{1,0:T(8,128)S(1)}, f32[512,128]{1,0:T(8,128)S(1)}, u32[]{:S(2)}, u32[]{:S(2)}) collective-permute-start(f32[512,128]{1,0:T(8,128)S(1)} %broadcast_select_fusion.1), channel_id=1, source_target_pairs={{0,2},{32,46},{2,4},{34,32},{4,6},{36,34},{6,8},{38,36},{8,10},{40... | collective-permute-start | bytes 786440 | tf_op jit(solution)/shard_map/ppermute | solution.py:75
  51.2 12.3 %collective-permute-start.7 = (f32[512,128]{1,0:T(8,128)S(1)}, f32[512,128]{1,0:T(8,128)S(1)}, u32[]{:S(2)}, u32[]{:S(2)}) collective-permute-start(f32[512,128]{1,0:T(8,128)S(1)} %broadcast_select_fusion), channel_id=1, source_target_pairs={{0,2},{32,46},{2,4},{34,32},{4,6},{36,34},{6,8},{38,36},{8,10},{40... | collective-permute-start | bytes 786440 | tf_op jit(solution)/shard_map/ppermute | solution.py:76
  58.8 11.6 %collective-permute-start.8 = (f32[512,128]{1,0:T(8,128)S(1)}, f32[512,128]{1,0:T(8,128)S(1)}, u32[]{:S(2)}, u32[]{:S(2)}) collective-permute-start(f32[512,128]{1,0:T(8,128)S(1)} %collective-permute-done.6), channel_id=1, source_target_pairs={{0,2},{32,46},{2,4},{34,32},{4,6},{36,34},{6,8},{38,36},{8,10},{40... | collective-permute-start | bytes 786440 | tf_op jit(solution)/shard_map/ppermute | solution.py:75
  63.5 16.6 %collective-permute-start.9 = (f32[512,128]{1,0:T(8,128)S(1)}, f32[512,128]{1,0:T(8,128)S(1)}, u32[]{:S(2)}, u32[]{:S(2)}) collective-permute-start(f32[512,128]{1,0:T(8,128)S(1)} %collective-permute-done.7), channel_id=1, source_target_pairs={{0,2},{32,46},{2,4},{34,32},{4,6},{36,34},{6,8},{38,36},{8,10},{40... | collective-permute-start | bytes 786440 | tf_op jit(solution)/shard_map/ppermute | solution.py:76
  70.4 22.7 %collective-permute-start.10 = (f32[512,128]{1,0:T(8,128)S(1)}, f32[512,128]{1,0:T(8,128)S(1)}, u32[]{:S(2)}, u32[]{:S(2)}) collective-permute-start(f32[512,128]{1,0:T(8,128)S(1)} %collective-permute-done.8), channel_id=1, source_target_pairs={{0,2},{32,46},{2,4},{34,32},{4,6},{36,34},{6,8},{38,36},{8,10},{40... | collective-permute-start | bytes 786440 | tf_op jit(solution)/shard_map/ppermute | solution.py:75
  80.1 12.6 %collective-permute-start.11 = (f32[512,128]{1,0:T(8,128)S(1)}, f32[512,128]{1,0:T(8,128)S(1)}, u32[]{:S(2)}, u32[]{:S(2)}) collective-permute-start(f32[512,128]{1,0:T(8,128)S(1)} %collective-permute-done.9), channel_id=1, source_target_pairs={{0,2},{32,46},{2,4},{34,32},{4,6},{36,34},{6,8},{38,36},{8,10},{40... | collective-permute-start | bytes 786440 | tf_op jit(solution)/shard_map/ppermute | solution.py:76
  94.8 87.1 %all-to-all-start = ((f32[16,128,128]{2,1,0:T(8,128)}), f32[16,128,128]{2,1,0:T(8,128)S(1)}, u32[]{:S(2)}, u32[]{:S(2)}) async-start(f32[16,128,128]{2,1,0:T(8,128)} %pad_maximum_fusion.1), calls=%async_computation | async-start | bytes 2097152 | tf_op jit(solution)/shard_map/all_to_all | solution.py:79
  101.2 72.6 %reduce-scatter.2.cloned.1.call-start = ((), (), s32[]{:S(2)}) async-start(), calls=%async_computation.2 | async-start | bytes 1114112 | tf_op jit(solution)/shard_map/reduce_scatter | solution.py:64
  173.7 8.1 %copy-start.5 = (f32[32,512]{1,0:T(8,128)S(1)}, f32[32,512]{1,0:T(8,128)}, u32[]{:S(2)}) copy-start(f32[32,512]{1,0:T(8,128)} %reduce-scatter.2.cloned.1.call-done) | copy-start | bytes 196612
  174.6 7.3 %collective-permute-start.13 = (f32[16,512]{1,0:T(8,128)S(1)}, f32[16,512]{1,0:T(8,128)S(1)}, u32[]{:S(2)}, u32[]{:S(2)}) collective-permute-start(f32[16,512]{1,0:T(8,128)S(1)} %dynamic-slice_bitcast_fusion), channel_id=1, source_target_pairs={{0,16},{16,0},{1,17},{17,1},{2,18},{18,2},{3,19},{19,3},{4,20},{20... | collective-permute-start | bytes 98312 | tf_op jit(solution)/shard_map/ppermute | solution.py:85
  182.0 10.8 %collective-permute-start.12 = (f32[256,128]{1,0:T(8,128)S(1)}, f32[256,128]{1,0:T(8,128)S(1)}, u32[]{:S(2)}, u32[]{:S(2)}) collective-permute-start(f32[256,128]{1,0:T(8,128)S(1)} %bitcast_reduce_fusion), channel_id=1, source_target_pairs={{0,0},{2,34},{4,68},{6,102},{8,136},{10,170},{12,204},{14,238},{16... | collective-permute-start | bytes 393224 | tf_op jit(solution)/shard_map/ppermute | solution.py:81
Sparse Core Ops, SparseCore 0:
  104.8 68.9 reduce-scatter.1
where the time goes:
time: 201 us; the launch traced here: 200 us
  waiting for transfers between devices  115 us (57%)
  starting transfers between devices  55.7 us (28%)
  between operations  14.5 us (7%)
  local copies, waits for them, and re-layouts  5.87 us (3%)
  matrix products  5.35 us (3%)
  other arithmetic  3.66 us (2%)
    reduce_scatter x1, waiting for transfers between devices, local(): lax.psum_scatter(terms, ('g', 'q'), scatter_dimension=0, tiled=True)  71.8 us
    ppermute x3, waiting for transfers between devices, local(): other = lax.ppermute(other, ('c', 'g'), _ring_pairs(True))  17 us
    ppermute x1, starting transfers between devices, local(): other = lax.ppermute(adjoint, 'c', SWAP)  10.6 us
    ppermute x3, waiting for transfers between devices, local(): own = lax.ppermute(own, ('c', 'g'), _ring_pairs(True))  10.1 us
    ppermute x3, starting transfers between devices, local(): own = lax.ppermute(own, ('c', 'g'), _ring_pairs(True))  8.32 us
    ppermute x1, waiting for transfers between devices, local(): gram = lax.ppermute(block, ('x', 'l', 'c', 'h', 'g'), _home_pairs())  6.75 us
    ppermute x1, waiting for transfers between devices, local(): lax.ppermute(direct, 'q', SWAP)  6.44 us
    all_to_all x1, starting transfers between devices, local(): lax.all_to_all(jnp.concatenate(pieces), ('x', 'l', 'q'), 0, 0, tiled=True)  6.39 us
  transfers between devices with their start and end apart: 16, of which 9 were waited for; matrix products, arithmetic and copies ran while one was open for 6% of the time, Pallas kernels for 0%

commit v1 on v0

--- a/solution.py
+++ b/solution.py
@@ -19,16 +19,17 @@
     return pairs
 
 
-def _home_pairs():
+def _home_pairs(turn):
     pairs = []
-    for x in range(4):
-        for l in range(2):
-            for c in range(2):
-                for h in range(2):
-                    for g in range(8):
-                        low = (g - x if c == 0 else g + 1 + x) % 8
-                        here = (((x * 2 + l) * 2 + c) * 2 + h) * 8 + g
-                        pairs.append((here, ((h * 8 + low) * 2 + l) * 8 + g))
+    for here in range(512):
+        rest, q = divmod(here, 2)
+        rest, g = divmod(rest, 8)
+        rest, h = divmod(rest, 2)
+        rest, c = divmod(rest, 2)
+        x, l = divmod(rest, 2)
+        arrival = 2 * (turn ^ q) + x // 2
+        low = (g - arrival if c == 0 else g + 1 + arrival) % 8
+        pairs.append((here, (((h * 8 + low) * 2 + x % 2) * 8 + g) * 2 + l))
     return pairs
 
 
@@ -51,19 +52,21 @@
     cells, cols = direct.shape
     modes = right_vecs.shape[1]
 
+    next_direct = lax.ppermute(direct, "q", SWAP)
+    next_own = lax.ppermute(adjoint, ("c", "g"), _ring_pairs(False))
     other = lax.ppermute(adjoint, "c", SWAP)
-    next_own = lax.ppermute(adjoint, ("c", "g"), _ring_pairs(False))
     next_other = lax.ppermute(other, ("c", "g"), _ring_pairs(False))
     own = jnp.where(c == 0, adjoint, next_own)
     other = jnp.where(c == 0, other, next_other)
 
     scale = inv_root[None, :]
     terms = jnp.concatenate([_dot(direct, right_vecs * scale), _dot(adjoint, left_vecs * scale)], axis=1)
-    terms = terms.reshape(2, 16, cells // 32, 2 * modes).transpose(1, 0, 2, 3).reshape(cells, 2 * modes)
-    own, other, terms = lax.optimization_barrier((own, other, terms))
-    part = lax.psum_scatter(terms, ("g", "q"), scatter_dimension=0, tiled=True).reshape(2, cells // 32, 2 * modes)
+    half = cells // 2
+    keep = lax.dynamic_slice_in_dim(terms, h * half, half, 0)
+    away = lax.dynamic_slice_in_dim(terms, (1 - h) * half, half, 0)
+    summed = lax.psum_scatter(keep + lax.ppermute(away, "h", SWAP), ("g", "q"), scatter_dimension=0, tiled=True)
 
-    pair = _beside(q, direct, lax.ppermute(direct, "q", SWAP)) * cell_weight[:, None]
+    pair = _beside(q, direct, next_direct) * cell_weight[:, None]
     both = _beside(h, pair, lax.ppermute(pair, "h", SWAP))
     other_both = lax.ppermute(both, "c", SWAP)
 
@@ -76,13 +79,17 @@
             other = lax.ppermute(other, ("c", "g"), _ring_pairs(True))
         pieces.append(lax.optimization_barrier(piece))
 
-    got = lax.all_to_all(jnp.concatenate(pieces), ("x", "l", "q"), 0, 0, tiled=True)
-    block = got.reshape(8, 2 * cols, cols).sum(0)
-    gram = lax.ppermute(block, ("x", "l", "c", "h", "g"), _home_pairs())
+    sums = []
+    for chunk in range(2):
+        chunk_pieces = jnp.concatenate(pieces[2 * chunk : 2 * chunk + 2])
+        sums.append(lax.all_to_all(chunk_pieces, ("x", "l"), 0, 0, tiled=True).sum(0))
+    home0 = lax.ppermute(jnp.where(q == 0, sums[0], sums[1]), AXES, _home_pairs(0))
+    home1 = lax.ppermute(jnp.where(q == 0, sums[1], sums[0]), AXES, _home_pairs(1))
 
-    keep = lax.dynamic_index_in_dim(part, h, 0, keepdims=False)
-    away = lax.dynamic_index_in_dim(part, 1 - h, 0, keepdims=False)
-    summed = keep + lax.ppermute(away, "h", SWAP)
+    low = (lax.axis_index("x") % 2) * 4 + lax.axis_index("l") * 2 + c
+    behind = (lax.axis_index("g") - low) % 8
+    arrival = jnp.where(behind < 4, behind, 7 - behind)
+    gram = jnp.where(arrival < 2, jnp.concatenate([home0, home1]), jnp.concatenate([home1, home0]))
     return (gram, summed[:, :modes], summed[:, modes:])
 
 

time: 201 us -> 153 us (0.76)
  the two profiles are of different devices: /device:TPU:4 before, /device:TPU:10 now
where the time goes in v1:
time: 153 us; the launch traced here: 152 us
  starting transfers between devices  64.2 us (42%)
  waiting for transfers between devices  52.6 us (34%)
  between operations  14.5 us (9%)
  other arithmetic  8.57 us (6%)
  matrix products  8.23 us (5%)
  local copies, waits for them, and re-layouts  4.43 us (3%)
    unnamed x2, waiting for transfers between devices  18.4 us
    ppermute x3, starting transfers between devices, local(): own = lax.ppermute(own, ('c', 'g'), _ring_pairs(True))  11.9 us
    all_to_all x2, waiting for transfers between devices, local(): lax.all_to_all(chunk_pieces, ('x', 'l'), 0, 0, tiled=True).sum(0)  11.7 us
    all_to_all x2, starting transfers between devices, local(): lax.all_to_all(chunk_pieces, ('x', 'l'), 0, 0, tiled=True).sum(0)  10.7 us
    ppermute x3, starting transfers between devices, local(): other = lax.ppermute(other, ('c', 'g'), _ring_pairs(True))  9.55 us
    ppermute x1, starting transfers between devices, local(): other_both = lax.ppermute(both, 'c', SWAP)  7.57 us
    dot_general x8, matrix products, _cross(): lax.dot_general(a, b, (((0,), (0,)), ((), ())), precision=PREC, preferred...  7.39 us
    ppermute x1, waiting for transfers between devices, local(): both = _beside(h, pair, lax.ppermute(pair, 'h', SWAP))  6.61 us
  transfers between devices with their start and end apart: 18, of which 8 were waited for; matrix products, arithmetic and copies ran while one was open for 12% of the time, Pallas kernels for 0%

profile of v1, /device:TPU:10, one launch (start us, length us, event | category | flops | bytes accessed | tf_op | source)
XLA Modules:
  0.0 152.4 jit_solution(3267177003658258918)
XLA Ops:
  7.2 0.0 reduce-scatter.4.cloned.1.call-start
  7.2 3.8 %collective-permute-start.1 = (f32[512,128]{1,0:T(8,128)}, f32[512,128]{1,0:T(8,128)S(1)}, u32[]{:S(2)}, u32[]{:S(2)}) collective-permute-start(f32[512,128]{1,0:T(8,128)} %param.6), channel_id=1, source_target_pairs={{0,1},{1,0},{2,3},{3,2},{4,5},{5,4},{6,7},{7,6},{8,9},{9,8},{10,11... | collective-permute-start | bytes 786440 | tf_op jit(solution)/shard_map/ppermute | solution.py:55
  11.1 6.4 %collective-permute-done.1 = f32[512,128]{1,0:T(8,128)S(1)} collective-permute-done((f32[512,128]{1,0:T(8,128)}, f32[512,128]{1,0:T(8,128)S(1)}, u32[]{:S(2)}, u32[]{:S(2)}) %collective-permute-start.1) | collective-permute-done | bytes 262176 | tf_op jit(solution)/shard_map/ppermute | solution.py:55
  17.5 1.2 fusion.3
  18.7 4.3 %collective-permute-start.2 = (f32[512,256]{1,0:T(8,128)S(1)}, f32[512,256]{1,0:T(8,128)S(1)}, u32[]{:S(2)}, u32[]{:S(2)}) collective-permute-start(f32[512,256]{1,0:T(8,128)S(1)} %fusion.3), channel_id=1, source_target_pairs={{0,16},{16,0},{1,17},{17,1},{2,18},{18,2},{3,19},{19,3},{4,20},{20... | collective-permute-start | bytes 1572872 | tf_op jit(solution)/shard_map/ppermute | solution.py:70
  23.1 1.9 %collective-permute-start.3 = (f32[512,128]{1,0:T(8,128)S(1)}, f32[512,128]{1,0:T(8,128)}, u32[]{:S(2)}, u32[]{:S(2)}) collective-permute-start(f32[512,128]{1,0:T(8,128)S(1)} %copy-done.1), channel_id=1, source_target_pairs={{0,32},{32,0},{1,33},{33,1},{2,34},{34,2},{3,35},{35,3},{4,36},{36... | collective-permute-start | bytes 786440 | tf_op jit(solution)/shard_map/ppermute | solution.py:57
  25.0 1.4 collective-permute-start
  26.4 0.4 convolution_bitcast_fusion.1
  26.8 0.4 convolution_bitcast_fusion
  27.3 1.4 collective-permute-start.4
  28.6 6.6 %collective-permute-done.2 = f32[512,256]{1,0:T(8,128)S(1)} collective-permute-done((f32[512,256]{1,0:T(8,128)S(1)}, f32[512,256]{1,0:T(8,128)S(1)}, u32[]{:S(2)}, u32[]{:S(2)}) %collective-permute-start.2) | collective-permute-done | bytes 524320 | tf_op jit(solution)/shard_map/ppermute | solution.py:70
  35.2 0.2 maximum_select_fusion
  35.4 7.6 %collective-permute-start.5 = (f32[512,512]{1,0:T(8,128)S(1)}, f32[512,512]{1,0:T(8,128)S(1)}, u32[]{:S(2)}, u32[]{:S(2)}) collective-permute-start(f32[512,512]{1,0:T(8,128)S(1)} %maximum_select_fusion), channel_id=1, source_target_pairs={{0,32},{32,0},{1,33},{33,1},{2,34},{34,2},{3,35},{35,3},{4,36},{36... | collective-permute-start | bytes 3145736 | tf_op jit(solution)/shard_map/ppermute | solution.py:71
  43.0 0.8 fusion
  43.8 3.1 %collective-permute-start.14 = (f32[256,512]{0,1:T(8,128)}, f32[256,512]{0,1:T(8,128)}, u32[]{:S(2)}, u32[]{:S(2)}) collective-permute-start(f32[256,512]{0,1:T(8,128)} %fusion), channel_id=1, source_target_pairs={{0,16},{16,0},{1,17},{17,1},{2,18},{18,2},{3,19},{19,3},{4,20},{20... | collective-permute-start | bytes 1572872 | tf_op jit(solution)/shard_map/ppermute | solution.py:67
  47.0 1.0 broadcast_select_fusion.1
  48.0 3.4 %collective-permute-start.6 = (f32[512,128]{1,0:T(8,128)S(1)}, f32[512,128]{1,0:T(8,128)}, u32[]{:S(2)}, u32[]{:S(2)}) collective-permute-start(f32[512,128]{1,0:T(8,128)S(1)} %broadcast_select_fusion.1), channel_id=1, source_target_pairs={{0,2},{32,46},{2,4},{34,32},{4,6},{36,34},{6,8},{38,36},{8,10},{40... | collective-permute-start | bytes 786440 | tf_op jit(solution)/shard_map/ppermute | solution.py:78
  51.4 1.0 broadcast_select_fusion
  52.4 3.6 %collective-permute-start.7 = (f32[512,128]{1,0:T(8,128)S(1)}, f32[512,128]{1,0:T(8,128)}, u32[]{:S(2)}, u32[]{:S(2)}) collective-permute-start(f32[512,128]{1,0:T(8,128)S(1)} %broadcast_select_fusion), channel_id=1, source_target_pairs={{0,2},{32,46},{2,4},{34,32},{4,6},{36,34},{6,8},{38,36},{8,10},{40... | collective-permute-start | bytes 786440 | tf_op jit(solution)/shard_map/ppermute | solution.py:79
  56.0 3.9 %collective-permute-done.6 = f32[512,128]{1,0:T(8,128)} collective-permute-done((f32[512,128]{1,0:T(8,128)S(1)}, f32[512,128]{1,0:T(8,128)}, u32[]{:S(2)}, u32[]{:S(2)}) %collective-permute-start.6) | collective-permute-done | bytes 262176 | tf_op jit(solution)/shard_map/ppermute | solution.py:78
  59.9 1.9 %collective-permute-start.8 = (f32[512,128]{1,0:T(8,128)}, f32[512,128]{1,0:T(8,128)}, u32[]{:S(2)}, u32[]{:S(2)}) collective-permute-start(f32[512,128]{1,0:T(8,128)} %collective-permute-done.6), channel_id=1, source_target_pairs={{0,2},{32,46},{2,4},{34,32},{4,6},{36,34},{6,8},{38,36},{8,10},{40... | collective-permute-start | bytes 786440 | tf_op jit(solution)/shard_map/ppermute | solution.py:78
  61.8 2.7 %collective-permute-done.7 = f32[512,128]{1,0:T(8,128)} collective-permute-done((f32[512,128]{1,0:T(8,128)S(1)}, f32[512,128]{1,0:T(8,128)}, u32[]{:S(2)}, u32[]{:S(2)}) %collective-permute-start.7) | collective-permute-done | bytes 262176 | tf_op jit(solution)/shard_map/ppermute | solution.py:79
  64.5 3.5 %collective-permute-start.9 = (f32[512,128]{1,0:T(8,128)}, f32[512,128]{1,0:T(8,128)}, u32[]{:S(2)}, u32[]{:S(2)}) collective-permute-start(f32[512,128]{1,0:T(8,128)} %collective-permute-done.7), channel_id=1, source_target_pairs={{0,2},{32,46},{2,4},{34,32},{4,6},{36,34},{6,8},{38,36},{8,10},{40... | collective-permute-start | bytes 786440 | tf_op jit(solution)/shard_map/ppermute | solution.py:79
  68.0 1.9 %fusion.2 = f32[256,512]{0,1:T(8,128)} fusion(f32[256,512]{0,1:T(8,128)} %collective-permute-done.14, s32[]{:T(128)S(6)} %select_n.83, f32[512,256]{0,1:T(8,128)S(1)} %convolution_bitcast_fusion.1, f32[512,256]{0,1:T(8,128)S(1)} %convolution_bitcast_fusion), kind=kLoop, calls=%fused_computation.13 | loop fusion | flops 262144 | bytes 2097156 | tf_op jit(solution)/shard_map/add | solution.py:67
  70.0 2.1 %copy.13 = f32[256,512]{1,0:T(8,128)} copy(f32[256,512]{0,1:T(8,128)} %fusion.2) | data formatting | bytes 1048576
  72.1 6.6 %collective-permute-start.10 = (f32[512,128]{1,0:T(8,128)}, f32[512,128]{1,0:T(8,128)S(1)}, u32[]{:S(2)}, u32[]{:S(2)}) collective-permute-start(f32[512,128]{1,0:T(8,128)} %collective-permute-done.8), channel_id=1, source_target_pairs={{0,2},{32,46},{2,4},{34,32},{4,6},{36,34},{6,8},{38,36},{8,10},{40... | collective-permute-start | bytes 786440 | tf_op jit(solution)/shard_map/ppermute | solution.py:78
  78.6 2.8 %collective-permute-done.9 = f32[512,128]{1,0:T(8,128)} collective-permute-done((f32[512,128]{1,0:T(8,128)}, f32[512,128]{1,0:T(8,128)}, u32[]{:S(2)}, u32[]{:S(2)}) %collective-permute-start.9) | collective-permute-done | bytes 262176 | tf_op jit(solution)/shard_map/ppermute | solution.py:79
  81.4 2.4 %collective-permute-start.11 = (f32[512,128]{1,0:T(8,128)}, f32[512,128]{1,0:T(8,128)S(1)}, u32[]{:S(2)}, u32[]{:S(2)}) collective-permute-start(f32[512,128]{1,0:T(8,128)} %collective-permute-done.9), channel_id=1, source_target_pairs={{0,2},{32,46},{2,4},{34,32},{4,6},{36,34},{6,8},{38,36},{8,10},{40... | collective-permute-start | bytes 786440 | tf_op jit(solution)/shard_map/ppermute | solution.py:79
  83.8 1.4 fusion.10
  85.2 1.4 convolution_add_fusion.2
  86.7 0.9 copy-done.3
  87.6 0.5 fusion.9
  88.1 0.4 convolution_add_fusion.3
  88.6 0.8 pad_maximum_fusion
  89.4 5.8 %all-to-all-start = ((f32[8,128,128]{2,1,0:T(8,128)}), f32[8,128,128]{2,1,0:T(8,128)S(1)}, u32[]{:S(2)}, u32[]{:S(2)}) async-start(f32[8,128,128]{2,1,0:T(8,128)} %pad_maximum_fusion), calls=%async_computation | async-start | bytes 1048576 | tf_op jit(solution)/shard_map/all_to_all | solution.py:85
  95.3 0.4 fusion.12
  95.7 0.4 convolution_add_fusion
  96.2 1.4 fusion.11
  97.6 1.4 convolution_add_fusion.1
  99.1 0.8 pad_maximum_fusion.1
  99.9 4.0 %all-to-all-done = f32[8,128,128]{2,1,0:T(8,128)S(1)} async-done(((f32[8,128,128]{2,1,0:T(8,128)}), f32[8,128,128]{2,1,0:T(8,128)S(1)}, u32[]{:S(2)}, u32[]{:S(2)}) %all-to-all-start) | async-done | bytes 524320 | tf_op jit(solution)/shard_map/all_to_all | solution.py:85
  103.9 4.9 %all-to-all-start.1 = ((f32[8,128,128]{2,1,0:T(8,128)}), f32[8,128,128]{2,1,0:T(8,128)S(1)}, u32[]{:S(2)}, u32[]{:S(2)}) async-start(f32[8,128,128]{2,1,0:T(8,128)} %pad_maximum_fusion.1), calls=%async_computation.1 | async-start | bytes 1048576 | tf_op jit(solution)/shard_map/all_to_all | solution.py:85
  108.8 7.8 %all-to-all-done.1 = f32[8,128,128]{2,1,0:T(8,128)S(1)} async-done(((f32[8,128,128]{2,1,0:T(8,128)}), f32[8,128,128]{2,1,0:T(8,128)S(1)}, u32[]{:S(2)}, u32[]{:S(2)}) %all-to-all-start.1) | async-done | bytes 524320 | tf_op jit(solution)/shard_map/all_to_all | solution.py:85
  116.6 3.9 %collective-permute-start.13 = (f32[128,128]{1,0:T(8,128)S(1)}, f32[128,128]{1,0:T(8,128)S(1)}, u32[]{:S(2)}, u32[]{:S(2)}) collective-permute-start(f32[128,128]{1,0:T(8,128)S(1)} %get-tuple-element.26), channel_id=1, source_target_pairs={{0,192},{1,0},{2,226},{3,34},{4,4},{5,68},{6,38},{7,102},{8,72},{9... | collective-permute-start | bytes 196616 | tf_op jit(solution)/shard_map/ppermute | solution.py:87
  120.6 4.6 %collective-permute-start.12 = (f32[128,128]{1,0:T(8,128)S(1)}, f32[128,128]{1,0:T(8,128)S(1)}, u32[]{:S(2)}, u32[]{:S(2)}) collective-permute-start(f32[128,128]{1,0:T(8,128)S(1)} %get-tuple-element.25), channel_id=1, source_target_pairs={{0,0},{1,192},{2,34},{3,226},{4,68},{5,4},{6,102},{7,38},{8,136},{... | collective-permute-start | bytes 196616 | tf_op jit(solution)/shard_map/ppermute | solution.py:86
  125.2 18.4 %reduce-scatter.4.cloned.1.call-done = f32[16,512]{1,0:T(8,128)} async-done(((f32[256,512]{1,0:T(8,128)}), f32[16,512]{1,0:T(8,128)}) %reduce-scatter.4.cloned.1.call-update) | async-done | bytes 32784
  143.6 1.3 fusion.8
  144.9 0.7 maximum_select_fusion.2
  (37 shorter events, 0.3 us)
Async XLA Ops:
  7.2 136.4 %reduce-scatter.4.cloned.1.call-start = ((), (), s32[]{:S(2)}) async-start(), calls=%async_computation.3 | async-start | bytes 557056
  7.2 10.3 %collective-permute-start.1 = (f32[512,128]{1,0:T(8,128)}, f32[512,128]{1,0:T(8,128)S(1)}, u32[]{:S(2)}, u32[]{:S(2)}) collective-permute-start(f32[512,128]{1,0:T(8,128)} %param.6), channel_id=1, source_target_pairs={{0,1},{1,0},{2,3},{3,2},{4,5},{5,4},{6,7},{7,6},{8,9},{9,8},{10,11... | collective-permute-start | bytes 786440 | tf_op jit(solution)/shard_map/ppermute | solution.py:55
  11.0 6.5 %copy-start.7 = (f32[512]{0:T(512)S(1)}, f32[512]{0:T(512)}, u32[]{:S(2)}) copy-start(f32[512]{0:T(512)} %param.8) | copy-start | bytes 6148
  11.1 12.0 %copy-start.1 = (f32[512,128]{1,0:T(8,128)S(1)}, f32[512,128]{1,0:T(8,128)}, u32[]{:S(2)}) copy-start(f32[512,128]{1,0:T(8,128)} %param.7) | copy-start | bytes 786436
  11.1 15.3 %copy-start = (f32[512,128]{1,0:T(8,128)S(1)}, f32[512,128]{1,0:T(8,128)}, u32[]{:S(2)}) copy-start(f32[512,128]{1,0:T(8,128)} %param.6) | copy-start | bytes 786436
  11.1 15.3 %copy-start.4 = (f32[128,256]{1,0:T(8,128)S(1)}, f32[128,256]{1,0:T(8,128)}, u32[]{:S(2)}) copy-start(f32[128,256]{1,0:T(8,128)} %param.9) | copy-start | bytes 393220
  11.1 15.3 %copy-start.6 = (f32[256]{0:T(256)S(1)}, f32[256]{0:T(256)}, u32[]{:S(2)}) copy-start(f32[256]{0:T(256)} %param.11) | copy-start | bytes 3076
  18.7 8.1 %copy-start.5 = (f32[128,256]{1,0:T(8,128)S(1)}, f32[128,256]{1,0:T(8,128)}, u32[]{:S(2)}) copy-start(f32[128,256]{1,0:T(8,128)} %param.10) | copy-start | bytes 393220
  18.7 16.5 %collective-permute-start.2 = (f32[512,256]{1,0:T(8,128)S(1)}, f32[512,256]{1,0:T(8,128)S(1)}, u32[]{:S(2)}, u32[]{:S(2)}) collective-permute-start(f32[512,256]{1,0:T(8,128)S(1)} %fusion.3), channel_id=1, source_target_pairs={{0,16},{16,0},{1,17},{17,1},{2,18},{18,2},{3,19},{19,3},{4,20},{20... | collective-permute-start | bytes 1572872 | tf_op jit(solution)/shard_map/ppermute | solution.py:70
  23.1 4.2 %collective-permute-start.3 = (f32[512,128]{1,0:T(8,128)S(1)}, f32[512,128]{1,0:T(8,128)}, u32[]{:S(2)}, u32[]{:S(2)}) collective-permute-start(f32[512,128]{1,0:T(8,128)S(1)} %copy-done.1), channel_id=1, source_target_pairs={{0,32},{32,0},{1,33},{33,1},{2,34},{34,2},{3,35},{35,3},{4,36},{36... | collective-permute-start | bytes 786440 | tf_op jit(solution)/shard_map/ppermute | solution.py:57
  25.0 22.0 %collective-permute-start = (f32[512,128]{1,0:T(8,128)S(1)}, f32[512,128]{1,0:T(8,128)}, u32[]{:S(2)}, u32[]{:S(2)}) collective-permute-start(f32[512,128]{1,0:T(8,128)S(1)} %copy-done.1), channel_id=1, source_target_pairs={{32,46},{34,32},{36,34},{38,36},{40,38},{42,40},{44,42},{46,44},{3... | collective-permute-start | bytes 786440 | tf_op jit(solution)/shard_map/ppermute | solution.py:56
  27.3 24.1 %collective-permute-start.4 = (f32[512,128]{1,0:T(8,128)}, f32[512,128]{1,0:T(8,128)}, u32[]{:S(2)}, u32[]{:S(2)}) collective-permute-start(f32[512,128]{1,0:T(8,128)} %collective-permute-done.3), channel_id=1, source_target_pairs={{32,46},{34,32},{36,34},{38,36},{40,38},{42,40},{44,42},{46,44},{3... | collective-permute-start | bytes 786440 | tf_op jit(solution)/shard_map/ppermute | solution.py:58
  35.4 48.4 %collective-permute-start.5 = (f32[512,512]{1,0:T(8,128)S(1)}, f32[512,512]{1,0:T(8,128)S(1)}, u32[]{:S(2)}, u32[]{:S(2)}) collective-permute-start(f32[512,512]{1,0:T(8,128)S(1)} %maximum_select_fusion), channel_id=1, source_target_pairs={{0,32},{32,0},{1,33},{33,1},{2,34},{34,2},{3,35},{35,3},{4,36},{36... | collective-permute-start | bytes 3145736 | tf_op jit(solution)/shard_map/ppermute | solution.py:71
  43.8 24.2 %collective-permute-start.14 = (f32[256,512]{0,1:T(8,128)}, f32[256,512]{0,1:T(8,128)}, u32[]{:S(2)}, u32[]{:S(2)}) collective-permute-start(f32[256,512]{0,1:T(8,128)} %fusion), channel_id=1, source_target_pairs={{0,16},{16,0},{1,17},{17,1},{2,18},{18,2},{3,19},{19,3},{4,20},{20... | collective-permute-start | bytes 1572872 | tf_op jit(solution)/shard_map/ppermute | solution.py:67
  48.0 11.9 %collective-permute-start.6 = (f32[512,128]{1,0:T(8,128)S(1)}, f32[512,128]{1,0:T(8,128)}, u32[]{:S(2)}, u32[]{:S(2)}) collective-permute-start(f32[512,128]{1,0:T(8,128)S(1)} %broadcast_select_fusion.1), channel_id=1, source_target_pairs={{0,2},{32,46},{2,4},{34,32},{4,6},{36,34},{6,8},{38,36},{8,10},{40... | collective-permute-start | bytes 786440 | tf_op jit(solution)/shard_map/ppermute | solution.py:78
  52.4 7.5 %copy-start.2 = (f32[512,128]{1,0:T(8,128)}, f32[512,128]{1,0:T(8,128)S(1)}, u32[]{:S(2)}) copy-start(f32[512,128]{1,0:T(8,128)S(1)} %broadcast_select_fusion) | copy-start | bytes 786436
  52.4 12.1 %collective-permute-start.7 = (f32[512,128]{1,0:T(8,128)S(1)}, f32[512,128]{1,0:T(8,128)}, u32[]{:S(2)}, u32[]{:S(2)}) collective-permute-start(f32[512,128]{1,0:T(8,128)S(1)} %broadcast_select_fusion), channel_id=1, source_target_pairs={{0,2},{32,46},{2,4},{34,32},{4,6},{36,34},{6,8},{38,36},{8,10},{40... | collective-permute-start | bytes 786440 | tf_op jit(solution)/shard_map/ppermute | solution.py:79
  59.9 12.1 %collective-permute-start.8 = (f32[512,128]{1,0:T(8,128)}, f32[512,128]{1,0:T(8,128)}, u32[]{:S(2)}, u32[]{:S(2)}) collective-permute-start(f32[512,128]{1,0:T(8,128)} %collective-permute-done.6), channel_id=1, source_target_pairs={{0,2},{32,46},{2,4},{34,32},{4,6},{36,34},{6,8},{38,36},{8,10},{40... | collective-permute-start | bytes 786440 | tf_op jit(solution)/shard_map/ppermute | solution.py:78
  64.5 16.9 %collective-permute-start.9 = (f32[512,128]{1,0:T(8,128)}, f32[512,128]{1,0:T(8,128)}, u32[]{:S(2)}, u32[]{:S(2)}) collective-permute-start(f32[512,128]{1,0:T(8,128)} %collective-permute-done.7), channel_id=1, source_target_pairs={{0,2},{32,46},{2,4},{34,32},{4,6},{36,34},{6,8},{38,36},{8,10},{40... | collective-permute-start | bytes 786440 | tf_op jit(solution)/shard_map/ppermute | solution.py:79
  72.1 23.7 %collective-permute-start.10 = (f32[512,128]{1,0:T(8,128)}, f32[512,128]{1,0:T(8,128)S(1)}, u32[]{:S(2)}, u32[]{:S(2)}) collective-permute-start(f32[512,128]{1,0:T(8,128)} %collective-permute-done.8), channel_id=1, source_target_pairs={{0,2},{32,46},{2,4},{34,32},{4,6},{36,34},{6,8},{38,36},{8,10},{40... | collective-permute-start | bytes 786440 | tf_op jit(solution)/shard_map/ppermute | solution.py:78
  81.4 13.9 %collective-permute-start.11 = (f32[512,128]{1,0:T(8,128)}, f32[512,128]{1,0:T(8,128)S(1)}, u32[]{:S(2)}, u32[]{:S(2)}) collective-permute-start(f32[512,128]{1,0:T(8,128)} %collective-permute-done.9), channel_id=1, source_target_pairs={{0,2},{32,46},{2,4},{34,32},{4,6},{36,34},{6,8},{38,36},{8,10},{40... | collective-permute-start | bytes 786440 | tf_op jit(solution)/shard_map/ppermute | solution.py:79
  86.6 1.0 copy-start.3
  89.4 14.5 %all-to-all-start = ((f32[8,128,128]{2,1,0:T(8,128)}), f32[8,128,128]{2,1,0:T(8,128)S(1)}, u32[]{:S(2)}, u32[]{:S(2)}) async-start(f32[8,128,128]{2,1,0:T(8,128)} %pad_maximum_fusion), calls=%async_computation | async-start | bytes 1048576 | tf_op jit(solution)/shard_map/all_to_all | solution.py:85
  103.9 12.7 %all-to-all-start.1 = ((f32[8,128,128]{2,1,0:T(8,128)}), f32[8,128,128]{2,1,0:T(8,128)S(1)}, u32[]{:S(2)}, u32[]{:S(2)}) async-start(f32[8,128,128]{2,1,0:T(8,128)} %pad_maximum_fusion.1), calls=%async_computation.1 | async-start | bytes 1048576 | tf_op jit(solution)/shard_map/all_to_all | solution.py:85
  116.6 28.3 %collective-permute-start.13 = (f32[128,128]{1,0:T(8,128)S(1)}, f32[128,128]{1,0:T(8,128)S(1)}, u32[]{:S(2)}, u32[]{:S(2)}) collective-permute-start(f32[128,128]{1,0:T(8,128)S(1)} %get-tuple-element.26), channel_id=1, source_target_pairs={{0,192},{1,0},{2,226},{3,34},{4,4},{5,68},{6,38},{7,102},{8,72},{9... | collective-permute-start | bytes 196616 | tf_op jit(solution)/shard_map/ppermute | solution.py:87
  120.6 24.3 %collective-permute-start.12 = (f32[128,128]{1,0:T(8,128)S(1)}, f32[128,128]{1,0:T(8,128)S(1)}, u32[]{:S(2)}, u32[]{:S(2)}) collective-permute-start(f32[128,128]{1,0:T(8,128)S(1)} %get-tuple-element.25), channel_id=1, source_target_pairs={{0,0},{1,192},{2,34},{3,226},{4,68},{5,4},{6,102},{7,38},{8,136},{... | collective-permute-start | bytes 196616 | tf_op jit(solution)/shard_map/ppermute | solution.py:86
Sparse Core Ops, SparseCore 0:
  72.2 71.3 reduce-scatter.3

commit v2 on v1

--- a/solution.py
+++ b/solution.py
@@ -52,6 +52,10 @@
     cells, cols = direct.shape
     modes = right_vecs.shape[1]
 
+    scale = inv_root[None, :]
+    terms = jnp.concatenate([_dot(direct, right_vecs * scale), _dot(adjoint, left_vecs * scale)], axis=1)
+    half = cells // 2
+    away = lax.ppermute(lax.dynamic_slice_in_dim(terms, (1 - h) * half, half, 0), "h", SWAP)
     next_direct = lax.ppermute(direct, "q", SWAP)
     next_own = lax.ppermute(adjoint, ("c", "g"), _ring_pairs(False))
     other = lax.ppermute(adjoint, "c", SWAP)
@@ -59,12 +63,8 @@
     own = jnp.where(c == 0, adjoint, next_own)
     other = jnp.where(c == 0, other, next_other)
 
-    scale = inv_root[None, :]
-    terms = jnp.concatenate([_dot(direct, right_vecs * scale), _dot(adjoint, left_vecs * scale)], axis=1)
-    half = cells // 2
-    keep = lax.dynamic_slice_in_dim(terms, h * half, half, 0)
-    away = lax.dynamic_slice_in_dim(terms, (1 - h) * half, half, 0)
-    summed = lax.psum_scatter(keep + lax.ppermute(away, "h", SWAP), ("g", "q"), scatter_dimension=0, tiled=True)
+    terms = away + lax.dynamic_slice_in_dim(terms, h * half, half, 0)
+    summed = lax.psum_scatter(terms, ("g", "q"), scatter_dimension=0, tiled=True)
 
     pair = _beside(q, direct, next_direct) * cell_weight[:, None]
     both = _beside(h, pair, lax.ppermute(pair, "h", SWAP))
@@ -78,13 +78,13 @@
             own = lax.ppermute(own, ("c", "g"), _ring_pairs(True))
             other = lax.ppermute(other, ("c", "g"), _ring_pairs(True))
         pieces.append(lax.optimization_barrier(piece))
+        if step == 2:
+            early = lax.all_to_all(jnp.concatenate(pieces[:2]), ("x", "l"), 0, 0, tiled=True).sum(0)
+            own, other, pieces, early = lax.optimization_barrier((own, other, pieces, early))
 
-    sums = []
-    for chunk in range(2):
-        chunk_pieces = jnp.concatenate(pieces[2 * chunk : 2 * chunk + 2])
-        sums.append(lax.all_to_all(chunk_pieces, ("x", "l"), 0, 0, tiled=True).sum(0))
-    home0 = lax.ppermute(jnp.where(q == 0, sums[0], sums[1]), AXES, _home_pairs(0))
-    home1 = lax.ppermute(jnp.where(q == 0, sums[1], sums[0]), AXES, _home_pairs(1))
+    late = lax.all_to_all(jnp.concatenate(pieces[2:]), ("x", "l"), 0, 0, tiled=True).sum(0)
+    home0 = lax.ppermute(jnp.where(q == 0, early, late), AXES, _home_pairs(0))
+    home1 = lax.ppermute(jnp.where(q == 0, late, early), AXES, _home_pairs(1))
 
     low = (lax.axis_index("x") % 2) * 4 + lax.axis_index("l") * 2 + c
     behind = (lax.axis_index("g") - low) % 8

time: 153 us -> 155 us (1.013)
  the two profiles are of different devices: /device:TPU:10 before, /device:TPU:12 now
where the time goes in v2:
time: 155 us; the launch traced here: 154 us
  starting transfers between devices  68 us (44%)
  waiting for transfers between devices  48.9 us (32%)
  between operations  14.5 us (9%)
  other arithmetic  9.77 us (6%)
  matrix products  8.23 us (5%)
  local copies, waits for them, and re-layouts  4.44 us (3%)
    unnamed x2, waiting for transfers between devices  16.8 us
    ppermute x3, starting transfers between devices, local(): own = lax.ppermute(own, ('c', 'g'), _ring_pairs(True))  11.9 us
    ppermute x3, starting transfers between devices, local(): other = lax.ppermute(other, ('c', 'g'), _ring_pairs(True))  10.5 us
    ppermute x1, starting transfers between devices, local(): home1 = lax.ppermute(jnp.where(q == 0, late, early), AXES, _home_pairs(1))  8.18 us
    ppermute x1, starting transfers between devices, local(): other_both = lax.ppermute(both, 'c', SWAP)  7.47 us
    dot_general x8, matrix products, _cross(): lax.dot_general(a, b, (((0,), (0,)), ((), ())), precision=PREC, preferred...  7.39 us
    ppermute x1, waiting for transfers between devices, local(): both = _beside(h, pair, lax.ppermute(pair, 'h', SWAP))  6.71 us
    ppermute x1, waiting for transfers between devices, local(): next_direct = lax.ppermute(direct, 'q', SWAP)  6.45 us
  transfers between devices with their start and end apart: 18, of which 8 were waited for; matrix products, arithmetic and copies ran while one was open for 13% of the time, Pallas kernels for 0%

profile of v2, /device:TPU:12, one launch (start us, length us, event | category | flops | bytes accessed | tf_op | source)
XLA Modules:
  0.0 153.9 jit_solution(7792210366488091167)
XLA Ops:
  7.2 0.0 reduce-scatter.4.cloned.1.call-start
  7.2 3.8 %collective-permute-start.9 = (f32[512,128]{1,0:T(8,128)}, f32[512,128]{1,0:T(8,128)S(1)}, u32[]{:S(2)}, u32[]{:S(2)}) collective-permute-start(f32[512,128]{1,0:T(8,128)} %param.6), channel_id=1, source_target_pairs={{0,1},{1,0},{2,3},{3,2},{4,5},{5,4},{6,7},{7,6},{8,9},{9,8},{10,11... | collective-permute-start | bytes 786440 | tf_op jit(solution)/shard_map/ppermute | solution.py:59
  11.1 6.5 %collective-permute-done.9 = f32[512,128]{1,0:T(8,128)S(1)} collective-permute-done((f32[512,128]{1,0:T(8,128)}, f32[512,128]{1,0:T(8,128)S(1)}, u32[]{:S(2)}, u32[]{:S(2)}) %collective-permute-start.9) | collective-permute-done | bytes 262176 | tf_op jit(solution)/shard_map/ppermute | solution.py:59
  17.5 1.2 fusion.3
  18.7 4.3 %collective-permute-start.10 = (f32[512,256]{1,0:T(8,128)S(1)}, f32[512,256]{1,0:T(8,128)}, u32[]{:S(2)}, u32[]{:S(2)}) collective-permute-start(f32[512,256]{1,0:T(8,128)S(1)} %fusion.3), channel_id=1, source_target_pairs={{0,16},{16,0},{1,17},{17,1},{2,18},{18,2},{3,19},{19,3},{4,20},{20... | collective-permute-start | bytes 1572872 | tf_op jit(solution)/shard_map/ppermute | solution.py:70
  23.1 1.9 %collective-permute-start.4 = (f32[512,128]{1,0:T(8,128)S(1)}, f32[512,128]{1,0:T(8,128)}, u32[]{:S(2)}, u32[]{:S(2)}) collective-permute-start(f32[512,128]{1,0:T(8,128)S(1)} %copy-done.1), channel_id=1, source_target_pairs={{0,32},{32,0},{1,33},{33,1},{2,34},{34,2},{3,35},{35,3},{4,36},{36... | collective-permute-start | bytes 786440 | tf_op jit(solution)/shard_map/ppermute | solution.py:61
  25.0 1.4 collective-permute-start
  26.4 0.4 convolution_bitcast_fusion
  26.8 0.4 convolution_bitcast_fusion.1
  27.3 1.4 collective-permute-start.5
  28.7 6.7 %collective-permute-done.10 = f32[512,256]{1,0:T(8,128)} collective-permute-done((f32[512,256]{1,0:T(8,128)S(1)}, f32[512,256]{1,0:T(8,128)}, u32[]{:S(2)}, u32[]{:S(2)}) %collective-permute-start.10) | collective-permute-done | bytes 524320 | tf_op jit(solution)/shard_map/ppermute | solution.py:70
  35.4 1.4 maximum_select_fusion
  36.7 7.5 %collective-permute-start.11 = (f32[512,512]{1,0:T(8,128)S(1)}, f32[512,512]{1,0:T(8,128)S(1)}, u32[]{:S(2)}, u32[]{:S(2)}) collective-permute-start(f32[512,512]{1,0:T(8,128)S(1)} %maximum_select_fusion), channel_id=1, source_target_pairs={{0,32},{32,0},{1,33},{33,1},{2,34},{34,2},{3,35},{35,3},{4,36},{36... | collective-permute-start | bytes 3145736 | tf_op jit(solution)/shard_map/ppermute | solution.py:71
  44.2 0.8 fusion.2
  45.0 3.1 %collective-permute-start.14 = (f32[256,512]{0,1:T(8,128)}, f32[256,512]{0,1:T(8,128)}, u32[]{:S(2)}, u32[]{:S(2)}) collective-permute-start(f32[256,512]{0,1:T(8,128)} %fusion.2), channel_id=1, source_target_pairs={{0,16},{16,0},{1,17},{17,1},{2,18},{18,2},{3,19},{19,3},{4,20},{20... | collective-permute-start | bytes 1572872 | tf_op jit(solution)/shard_map/ppermute | solution.py:58
  48.2 1.0 broadcast_select_fusion.1
  49.2 3.4 %collective-permute-start.1 = (f32[512,128]{1,0:T(8,128)S(1)}, f32[512,128]{1,0:T(8,128)}, u32[]{:S(2)}, u32[]{:S(2)}) collective-permute-start(f32[512,128]{1,0:T(8,128)S(1)} %broadcast_select_fusion.1), channel_id=1, source_target_pairs={{0,2},{32,46},{2,4},{34,32},{4,6},{36,34},{6,8},{38,36},{8,10},{40... | collective-permute-start | bytes 786440 | tf_op jit(solution)/shard_map/ppermute | solution.py:78
  52.6 1.0 broadcast_select_fusion
  53.6 3.7 %collective-permute-start.6 = (f32[512,128]{1,0:T(8,128)S(1)}, f32[512,128]{1,0:T(8,128)}, u32[]{:S(2)}, u32[]{:S(2)}) collective-permute-start(f32[512,128]{1,0:T(8,128)S(1)} %broadcast_select_fusion), channel_id=1, source_target_pairs={{0,2},{32,46},{2,4},{34,32},{4,6},{36,34},{6,8},{38,36},{8,10},{40... | collective-permute-start | bytes 786440 | tf_op jit(solution)/shard_map/ppermute | solution.py:79
  57.3 3.9 %collective-permute-done.1 = f32[512,128]{1,0:T(8,128)} collective-permute-done((f32[512,128]{1,0:T(8,128)S(1)}, f32[512,128]{1,0:T(8,128)}, u32[]{:S(2)}, u32[]{:S(2)}) %collective-permute-start.1) | collective-permute-done | bytes 262176 | tf_op jit(solution)/shard_map/ppermute | solution.py:78
  61.2 1.9 %collective-permute-start.2 = (f32[512,128]{1,0:T(8,128)}, f32[512,128]{1,0:T(8,128)}, u32[]{:S(2)}, u32[]{:S(2)}) collective-permute-start(f32[512,128]{1,0:T(8,128)} %collective-permute-done.1), channel_id=1, source_target_pairs={{0,2},{32,46},{2,4},{34,32},{4,6},{36,34},{6,8},{38,36},{8,10},{40... | collective-permute-start | bytes 786440 | tf_op jit(solution)/shard_map/ppermute | solution.py:78
  63.1 1.9 %collective-permute-done.6 = f32[512,128]{1,0:T(8,128)} collective-permute-done((f32[512,128]{1,0:T(8,128)S(1)}, f32[512,128]{1,0:T(8,128)}, u32[]{:S(2)}, u32[]{:S(2)}) %collective-permute-start.6) | collective-permute-done | bytes 262176 | tf_op jit(solution)/shard_map/ppermute | solution.py:79
  65.0 4.2 %collective-permute-start.7 = (f32[512,128]{1,0:T(8,128)}, f32[512,128]{1,0:T(8,128)}, u32[]{:S(2)}, u32[]{:S(2)}) collective-permute-start(f32[512,128]{1,0:T(8,128)} %collective-permute-done.6), channel_id=1, source_target_pairs={{0,2},{32,46},{2,4},{34,32},{4,6},{36,34},{6,8},{38,36},{8,10},{40... | collective-permute-start | bytes 786440 | tf_op jit(solution)/shard_map/ppermute | solution.py:79
  69.3 1.9 %fusion.1 = f32[256,512]{0,1:T(8,128)} fusion(f32[256,512]{0,1:T(8,128)} %collective-permute-done.14, s32[]{:T(128)S(6)} %select_n.84, f32[512,256]{0,1:T(8,128)S(1)} %convolution_bitcast_fusion.1, f32[512,256]{0,1:T(8,128)S(1)} %convolution_bitcast_fusion), kind=kLoop, calls=%fused_computation.12 | loop fusion | flops 262144 | bytes 2097156 | tf_op jit(solution)/shard_map/add | solution.py:66
  71.2 2.1 %copy.13 = f32[256,512]{1,0:T(8,128)} copy(f32[256,512]{0,1:T(8,128)} %fusion.1) | data formatting | bytes 1048576
  73.3 6.6 %collective-permute-start.3 = (f32[512,128]{1,0:T(8,128)}, f32[512,128]{1,0:T(8,128)S(1)}, u32[]{:S(2)}, u32[]{:S(2)}) collective-permute-start(f32[512,128]{1,0:T(8,128)} %collective-permute-done.2), channel_id=1, source_target_pairs={{0,2},{32,46},{2,4},{34,32},{4,6},{36,34},{6,8},{38,36},{8,10},{40... | collective-permute-start | bytes 786440 | tf_op jit(solution)/shard_map/ppermute | solution.py:78
  79.9 2.8 %collective-permute-done.7 = f32[512,128]{1,0:T(8,128)} collective-permute-done((f32[512,128]{1,0:T(8,128)}, f32[512,128]{1,0:T(8,128)}, u32[]{:S(2)}, u32[]{:S(2)}) %collective-permute-start.7) | collective-permute-done | bytes 262176 | tf_op jit(solution)/shard_map/ppermute | solution.py:79
  82.7 2.6 %collective-permute-start.8 = (f32[512,128]{1,0:T(8,128)}, f32[512,128]{1,0:T(8,128)S(1)}, u32[]{:S(2)}, u32[]{:S(2)}) collective-permute-start(f32[512,128]{1,0:T(8,128)} %collective-permute-done.7), channel_id=1, source_target_pairs={{0,2},{32,46},{2,4},{34,32},{4,6},{36,34},{6,8},{38,36},{8,10},{40... | collective-permute-start | bytes 786440 | tf_op jit(solution)/shard_map/ppermute | solution.py:79
  85.3 1.4 fusion.10
  86.7 1.4 convolution_add_fusion.2
  88.2 0.9 copy-done.3
  89.1 0.5 fusion.9
  89.6 0.4 convolution_add_fusion.3
  90.1 0.8 pad_maximum_fusion
  90.9 5.7 %all-to-all-start = ((f32[8,128,128]{2,1,0:T(8,128)}), f32[8,128,128]{2,1,0:T(8,128)S(1)}, u32[]{:S(2)}, u32[]{:S(2)}) async-start(f32[8,128,128]{2,1,0:T(8,128)} %pad_maximum_fusion), calls=%async_computation | async-start | bytes 1048576 | tf_op jit(solution)/shard_map/all_to_all | solution.py:82
  96.6 1.4 fusion.11
  98.0 1.4 convolution_add_fusion.1
  99.5 4.2 %all-to-all-done = f32[8,128,128]{2,1,0:T(8,128)S(1)} async-done(((f32[8,128,128]{2,1,0:T(8,128)}), f32[8,128,128]{2,1,0:T(8,128)S(1)}, u32[]{:S(2)}, u32[]{:S(2)}) %all-to-all-start) | async-done | bytes 524320 | tf_op jit(solution)/shard_map/all_to_all | solution.py:82
  103.7 0.4 fusion.12
  104.2 0.4 convolution_add_fusion
  104.7 0.9 pad_maximum_fusion.1
  105.5 6.4 %all-to-all-start.1 = ((f32[8,128,128]{2,1,0:T(8,128)}), f32[8,128,128]{2,1,0:T(8,128)S(1)}, u32[]{:S(2)}, u32[]{:S(2)}) async-start(f32[8,128,128]{2,1,0:T(8,128)} %pad_maximum_fusion.1), calls=%async_computation.1 | async-start | bytes 1048576 | tf_op jit(solution)/shard_map/all_to_all | solution.py:85
  111.9 6.2 %all-to-all-done.1 = f32[8,128,128]{2,1,0:T(8,128)S(1)} async-done(((f32[8,128,128]{2,1,0:T(8,128)}), f32[8,128,128]{2,1,0:T(8,128)S(1)}, u32[]{:S(2)}, u32[]{:S(2)}) %all-to-all-start.1) | async-done | bytes 524320 | tf_op jit(solution)/shard_map/all_to_all | solution.py:85
  118.2 1.9 %collective-permute-start.12 = (f32[128,128]{1,0:T(8,128)S(1)}, f32[128,128]{1,0:T(8,128)S(1)}, u32[]{:S(2)}, u32[]{:S(2)}) collective-permute-start(f32[128,128]{1,0:T(8,128)S(1)} %get-tuple-element.33), channel_id=1, source_target_pairs={{0,0},{1,192},{2,34},{3,226},{4,68},{5,4},{6,102},{7,38},{8,136},{... | collective-permute-start | bytes 196616 | tf_op jit(solution)/shard_map/ppermute | solution.py:86
  120.1 8.2 %collective-permute-start.13 = (f32[128,128]{1,0:T(8,128)S(1)}, f32[128,128]{1,0:T(8,128)S(1)}, u32[]{:S(2)}, u32[]{:S(2)}) collective-permute-start(f32[128,128]{1,0:T(8,128)S(1)} %get-tuple-element.34), channel_id=1, source_target_pairs={{0,192},{1,0},{2,226},{3,34},{4,4},{5,68},{6,38},{7,102},{8,72},{9... | collective-permute-start | bytes 196616 | tf_op jit(solution)/shard_map/ppermute | solution.py:87
  128.3 16.8 %reduce-scatter.4.cloned.1.call-done = f32[16,512]{1,0:T(8,128)} async-done(((f32[256,512]{1,0:T(8,128)}), f32[16,512]{1,0:T(8,128)}) %reduce-scatter.4.cloned.1.call-update) | async-done | bytes 32784
  145.0 1.3 fusion.8
  146.4 0.7 maximum_select_fusion.2
  (37 shorter events, 0.3 us)
Async XLA Ops:
  7.2 137.9 %reduce-scatter.4.cloned.1.call-start = ((), (), s32[]{:S(2)}) async-start(), calls=%async_computation.3 | async-start | bytes 557056
  7.2 10.3 %collective-permute-start.9 = (f32[512,128]{1,0:T(8,128)}, f32[512,128]{1,0:T(8,128)S(1)}, u32[]{:S(2)}, u32[]{:S(2)}) collective-permute-start(f32[512,128]{1,0:T(8,128)} %param.6), channel_id=1, source_target_pairs={{0,1},{1,0},{2,3},{3,2},{4,5},{5,4},{6,7},{7,6},{8,9},{9,8},{10,11... | collective-permute-start | bytes 786440 | tf_op jit(solution)/shard_map/ppermute | solution.py:59
  11.1 6.5 %copy-start.7 = (f32[512]{0:T(512)S(1)}, f32[512]{0:T(512)}, u32[]{:S(2)}) copy-start(f32[512]{0:T(512)} %param.8) | copy-start | bytes 6148
  11.1 12.0 %copy-start.1 = (f32[512,128]{1,0:T(8,128)S(1)}, f32[512,128]{1,0:T(8,128)}, u32[]{:S(2)}) copy-start(f32[512,128]{1,0:T(8,128)} %param.7) | copy-start | bytes 786436
  11.1 15.3 %copy-start.4 = (f32[128,256]{1,0:T(8,128)S(1)}, f32[128,256]{1,0:T(8,128)}, u32[]{:S(2)}) copy-start(f32[128,256]{1,0:T(8,128)} %param.10) | copy-start | bytes 393220
  11.1 15.3 %copy-start.6 = (f32[256]{0:T(256)S(1)}, f32[256]{0:T(256)}, u32[]{:S(2)}) copy-start(f32[256]{0:T(256)} %param.11) | copy-start | bytes 3076
  18.7 8.1 %copy-start = (f32[512,128]{1,0:T(8,128)S(1)}, f32[512,128]{1,0:T(8,128)}, u32[]{:S(2)}) copy-start(f32[512,128]{1,0:T(8,128)} %param.6) | copy-start | bytes 786436
  18.7 8.1 %copy-start.5 = (f32[128,256]{1,0:T(8,128)S(1)}, f32[128,256]{1,0:T(8,128)}, u32[]{:S(2)}) copy-start(f32[128,256]{1,0:T(8,128)} %param.9) | copy-start | bytes 393220
  18.7 16.6 %collective-permute-start.10 = (f32[512,256]{1,0:T(8,128)S(1)}, f32[512,256]{1,0:T(8,128)}, u32[]{:S(2)}, u32[]{:S(2)}) collective-permute-start(f32[512,256]{1,0:T(8,128)S(1)} %fusion.3), channel_id=1, source_target_pairs={{0,16},{16,0},{1,17},{17,1},{2,18},{18,2},{3,19},{19,3},{4,20},{20... | collective-permute-start | bytes 1572872 | tf_op jit(solution)/shard_map/ppermute | solution.py:70
  23.1 4.2 %collective-permute-start.4 = (f32[512,128]{1,0:T(8,128)S(1)}, f32[512,128]{1,0:T(8,128)}, u32[]{:S(2)}, u32[]{:S(2)}) collective-permute-start(f32[512,128]{1,0:T(8,128)S(1)} %copy-done.1), channel_id=1, source_target_pairs={{0,32},{32,0},{1,33},{33,1},{2,34},{34,2},{3,35},{35,3},{4,36},{36... | collective-permute-start | bytes 786440 | tf_op jit(solution)/shard_map/ppermute | solution.py:61
  25.0 23.2 %collective-permute-start = (f32[512,128]{1,0:T(8,128)S(1)}, f32[512,128]{1,0:T(8,128)}, u32[]{:S(2)}, u32[]{:S(2)}) collective-permute-start(f32[512,128]{1,0:T(8,128)S(1)} %copy-done.1), channel_id=1, source_target_pairs={{32,46},{34,32},{36,34},{38,36},{40,38},{42,40},{44,42},{46,44},{3... | collective-permute-start | bytes 786440 | tf_op jit(solution)/shard_map/ppermute | solution.py:60
  27.3 25.3 %collective-permute-start.5 = (f32[512,128]{1,0:T(8,128)}, f32[512,128]{1,0:T(8,128)}, u32[]{:S(2)}, u32[]{:S(2)}) collective-permute-start(f32[512,128]{1,0:T(8,128)} %collective-permute-done.4), channel_id=1, source_target_pairs={{32,46},{34,32},{36,34},{38,36},{40,38},{42,40},{44,42},{46,44},{3... | collective-permute-start | bytes 786440 | tf_op jit(solution)/shard_map/ppermute | solution.py:62
  36.7 48.6 %collective-permute-start.11 = (f32[512,512]{1,0:T(8,128)S(1)}, f32[512,512]{1,0:T(8,128)S(1)}, u32[]{:S(2)}, u32[]{:S(2)}) collective-permute-start(f32[512,512]{1,0:T(8,128)S(1)} %maximum_select_fusion), channel_id=1, source_target_pairs={{0,32},{32,0},{1,33},{33,1},{2,34},{34,2},{3,35},{35,3},{4,36},{36... | collective-permute-start | bytes 3145736 | tf_op jit(solution)/shard_map/ppermute | solution.py:71
  45.0 24.2 %collective-permute-start.14 = (f32[256,512]{0,1:T(8,128)}, f32[256,512]{0,1:T(8,128)}, u32[]{:S(2)}, u32[]{:S(2)}) collective-permute-start(f32[256,512]{0,1:T(8,128)} %fusion.2), channel_id=1, source_target_pairs={{0,16},{16,0},{1,17},{17,1},{2,18},{18,2},{3,19},{19,3},{4,20},{20... | collective-permute-start | bytes 1572872 | tf_op jit(solution)/shard_map/ppermute | solution.py:58
  49.2 12.0 %collective-permute-start.1 = (f32[512,128]{1,0:T(8,128)S(1)}, f32[512,128]{1,0:T(8,128)}, u32[]{:S(2)}, u32[]{:S(2)}) collective-permute-start(f32[512,128]{1,0:T(8,128)S(1)} %broadcast_select_fusion.1), channel_id=1, source_target_pairs={{0,2},{32,46},{2,4},{34,32},{4,6},{36,34},{6,8},{38,36},{8,10},{40... | collective-permute-start | bytes 786440 | tf_op jit(solution)/shard_map/ppermute | solution.py:78
  53.6 7.6 %copy-start.2 = (f32[512,128]{1,0:T(8,128)}, f32[512,128]{1,0:T(8,128)S(1)}, u32[]{:S(2)}) copy-start(f32[512,128]{1,0:T(8,128)S(1)} %broadcast_select_fusion) | copy-start | bytes 786436
  53.6 11.4 %collective-permute-start.6 = (f32[512,128]{1,0:T(8,128)S(1)}, f32[512,128]{1,0:T(8,128)}, u32[]{:S(2)}, u32[]{:S(2)}) collective-permute-start(f32[512,128]{1,0:T(8,128)S(1)} %broadcast_select_fusion), channel_id=1, source_target_pairs={{0,2},{32,46},{2,4},{34,32},{4,6},{36,34},{6,8},{38,36},{8,10},{40... | collective-permute-start | bytes 786440 | tf_op jit(solution)/shard_map/ppermute | solution.py:79
  61.2 12.0 %collective-permute-start.2 = (f32[512,128]{1,0:T(8,128)}, f32[512,128]{1,0:T(8,128)}, u32[]{:S(2)}, u32[]{:S(2)}) collective-permute-start(f32[512,128]{1,0:T(8,128)} %collective-permute-done.1), channel_id=1, source_target_pairs={{0,2},{32,46},{2,4},{34,32},{4,6},{36,34},{6,8},{38,36},{8,10},{40... | collective-permute-start | bytes 786440 | tf_op jit(solution)/shard_map/ppermute | solution.py:78
  65.0 17.7 %collective-permute-start.7 = (f32[512,128]{1,0:T(8,128)}, f32[512,128]{1,0:T(8,128)}, u32[]{:S(2)}, u32[]{:S(2)}) collective-permute-start(f32[512,128]{1,0:T(8,128)} %collective-permute-done.6), channel_id=1, source_target_pairs={{0,2},{32,46},{2,4},{34,32},{4,6},{36,34},{6,8},{38,36},{8,10},{40... | collective-permute-start | bytes 786440 | tf_op jit(solution)/shard_map/ppermute | solution.py:79
  73.3 30.4 %collective-permute-start.3 = (f32[512,128]{1,0:T(8,128)}, f32[512,128]{1,0:T(8,128)S(1)}, u32[]{:S(2)}, u32[]{:S(2)}) collective-permute-start(f32[512,128]{1,0:T(8,128)} %collective-permute-done.2), channel_id=1, source_target_pairs={{0,2},{32,46},{2,4},{34,32},{4,6},{36,34},{6,8},{38,36},{8,10},{40... | collective-permute-start | bytes 786440 | tf_op jit(solution)/shard_map/ppermute | solution.py:78
  82.7 21.0 %collective-permute-start.8 = (f32[512,128]{1,0:T(8,128)}, f32[512,128]{1,0:T(8,128)S(1)}, u32[]{:S(2)}, u32[]{:S(2)}) collective-permute-start(f32[512,128]{1,0:T(8,128)} %collective-permute-done.7), channel_id=1, source_target_pairs={{0,2},{32,46},{2,4},{34,32},{4,6},{36,34},{6,8},{38,36},{8,10},{40... | collective-permute-start | bytes 786440 | tf_op jit(solution)/shard_map/ppermute | solution.py:79
  88.1 1.0 copy-start.3
  90.9 12.8 %all-to-all-start = ((f32[8,128,128]{2,1,0:T(8,128)}), f32[8,128,128]{2,1,0:T(8,128)S(1)}, u32[]{:S(2)}, u32[]{:S(2)}) async-start(f32[8,128,128]{2,1,0:T(8,128)} %pad_maximum_fusion), calls=%async_computation | async-start | bytes 1048576 | tf_op jit(solution)/shard_map/all_to_all | solution.py:82
  105.5 12.6 %all-to-all-start.1 = ((f32[8,128,128]{2,1,0:T(8,128)}), f32[8,128,128]{2,1,0:T(8,128)S(1)}, u32[]{:S(2)}, u32[]{:S(2)}) async-start(f32[8,128,128]{2,1,0:T(8,128)} %pad_maximum_fusion.1), calls=%async_computation.1 | async-start | bytes 1048576 | tf_op jit(solution)/shard_map/all_to_all | solution.py:85
  118.2 28.2 %collective-permute-start.12 = (f32[128,128]{1,0:T(8,128)S(1)}, f32[128,128]{1,0:T(8,128)S(1)}, u32[]{:S(2)}, u32[]{:S(2)}) collective-permute-start(f32[128,128]{1,0:T(8,128)S(1)} %get-tuple-element.33), channel_id=1, source_target_pairs={{0,0},{1,192},{2,34},{3,226},{4,68},{5,4},{6,102},{7,38},{8,136},{... | collective-permute-start | bytes 196616 | tf_op jit(solution)/shard_map/ppermute | solution.py:86
  120.1 26.3 %collective-permute-start.13 = (f32[128,128]{1,0:T(8,128)S(1)}, f32[128,128]{1,0:T(8,128)S(1)}, u32[]{:S(2)}, u32[]{:S(2)}) collective-permute-start(f32[128,128]{1,0:T(8,128)S(1)} %get-tuple-element.34), channel_id=1, source_target_pairs={{0,192},{1,0},{2,226},{3,34},{4,4},{5,68},{6,38},{7,102},{8,72},{9... | collective-permute-start | bytes 196616 | tf_op jit(solution)/shard_map/ppermute | solution.py:87
Sparse Core Ops, SparseCore 0:
  73.4 71.6 reduce-scatter.3

commit v3 on v2

--- a/solution.py
+++ b/solution.py
@@ -52,17 +52,20 @@
     cells, cols = direct.shape
     modes = right_vecs.shape[1]
 
-    scale = inv_root[None, :]
-    terms = jnp.concatenate([_dot(direct, right_vecs * scale), _dot(adjoint, left_vecs * scale)], axis=1)
-    half = cells // 2
-    away = lax.ppermute(lax.dynamic_slice_in_dim(terms, (1 - h) * half, half, 0), "h", SWAP)
     next_direct = lax.ppermute(direct, "q", SWAP)
     next_own = lax.ppermute(adjoint, ("c", "g"), _ring_pairs(False))
     other = lax.ppermute(adjoint, "c", SWAP)
+    other, direct_after, adjoint_after = lax.optimization_barrier((other, direct, adjoint))
     next_other = lax.ppermute(other, ("c", "g"), _ring_pairs(False))
     own = jnp.where(c == 0, adjoint, next_own)
     other = jnp.where(c == 0, other, next_other)
 
+    scale = inv_root[None, :]
+    terms = jnp.concatenate(
+        [_dot(direct_after, right_vecs * scale), _dot(adjoint_after, left_vecs * scale)], axis=1
+    )
+    half = cells // 2
+    away = lax.ppermute(lax.dynamic_slice_in_dim(terms, (1 - h) * half, half, 0), "h", SWAP)
     terms = away + lax.dynamic_slice_in_dim(terms, h * half, half, 0)
     summed = lax.psum_scatter(terms, ("g", "q"), scatter_dimension=0, tiled=True)
 

time: 155 us -> 154 us (level)
  the two profiles are of different devices: /device:TPU:12 before, /device:TPU:2 now
where the time goes in v3:
time: 154 us; the launch traced here: 152 us
  starting transfers between devices  66.3 us (43%)
  waiting for transfers between devices  49 us (32%)
  between operations  14.5 us (9%)
  matrix products  9.17 us (6%)
  other arithmetic  8.98 us (6%)
  local copies, waits for them, and re-layouts  4.43 us (3%)
    ppermute x3, starting transfers between devices, local(): other = lax.ppermute(other, ('c', 'g'), _ring_pairs(True))  16.4 us
    unnamed x2, waiting for transfers between devices  15.6 us
    ppermute x3, starting transfers between devices, local(): own = lax.ppermute(own, ('c', 'g'), _ring_pairs(True))  12.9 us
    all_to_all x1, waiting for transfers between devices, local(): lax.all_to_all(jnp.concatenate(pieces[2:]), ('x', 'l'), 0, 0, tiled=True)  9.2 us
    dot_general x8, matrix products, _cross(): lax.dot_general(a, b, (((0,), (0,)), ((), ())), precision=PREC, preferred...  8.35 us
    ppermute x1, waiting for transfers between devices, local(): both = _beside(h, pair, lax.ppermute(pair, 'h', SWAP))  8.29 us
    all_to_all x1, waiting for transfers between devices, local(): lax.all_to_all(jnp.concatenate(pieces[:2]), ('x', 'l'), 0, 0, tiled=True)  5.6 us
    ppermute x1, starting transfers between devices, local(): both = _beside(h, pair, lax.ppermute(pair, 'h', SWAP))  5.1 us
  transfers between devices with their start and end apart: 18, of which 7 were waited for; matrix products, arithmetic and copies ran while one was open for 14% of the time, Pallas kernels for 0%

profile of v3, /device:TPU:2, one launch (start us, length us, event | category | flops | bytes accessed | tf_op | source)
XLA Modules:
  0.0 152.4 jit_solution(18379440895272894533)
XLA Ops:
  7.2 0.0 reduce-scatter.4.cloned.1.call-start
  7.2 3.8 %collective-permute-start.9 = (f32[512,128]{1,0:T(8,128)}, f32[512,128]{1,0:T(8,128)S(1)}, u32[]{:S(2)}, u32[]{:S(2)}) collective-permute-start(f32[512,128]{1,0:T(8,128)} %param.6), channel_id=1, source_target_pairs={{0,1},{1,0},{2,3},{3,2},{4,5},{5,4},{6,7},{7,6},{8,9},{9,8},{10,11... | collective-permute-start | bytes 786440 | tf_op jit(solution)/shard_map/ppermute | solution.py:55
  11.0 1.9 %collective-permute-start.4 = (f32[512,128]{1,0:T(8,128)}, f32[512,128]{1,0:T(8,128)}, u32[]{:S(2)}, u32[]{:S(2)}) collective-permute-start(f32[512,128]{1,0:T(8,128)} %param.7), channel_id=1, source_target_pairs={{0,32},{32,0},{1,33},{33,1},{2,34},{34,2},{3,35},{35,3},{4,36},{36... | collective-permute-start | bytes 786440 | tf_op jit(solution)/shard_map/ppermute | solution.py:57
  13.0 4.5 %collective-permute-done.9 = f32[512,128]{1,0:T(8,128)S(1)} collective-permute-done((f32[512,128]{1,0:T(8,128)}, f32[512,128]{1,0:T(8,128)S(1)}, u32[]{:S(2)}, u32[]{:S(2)}) %collective-permute-start.9) | collective-permute-done | bytes 262176 | tf_op jit(solution)/shard_map/ppermute | solution.py:55
  17.5 1.2 fusion.3
  18.8 5.1 %collective-permute-start.10 = (f32[512,256]{1,0:T(8,128)S(1)}, f32[512,256]{1,0:T(8,128)}, u32[]{:S(2)}, u32[]{:S(2)}) collective-permute-start(f32[512,256]{1,0:T(8,128)S(1)} %fusion.3), channel_id=1, source_target_pairs={{0,16},{16,0},{1,17},{17,1},{2,18},{18,2},{3,19},{19,3},{4,20},{20... | collective-permute-start | bytes 1572872 | tf_op jit(solution)/shard_map/ppermute | solution.py:73
  23.9 1.4 collective-permute-start
  25.3 0.8 collective-permute-start.5
  26.1 0.4 fusion.4
  26.5 0.4 fusion.6
  27.0 8.3 %collective-permute-done.10 = f32[512,256]{1,0:T(8,128)} collective-permute-done((f32[512,256]{1,0:T(8,128)S(1)}, f32[512,256]{1,0:T(8,128)}, u32[]{:S(2)}, u32[]{:S(2)}) %collective-permute-start.10) | collective-permute-done | bytes 524320 | tf_op jit(solution)/shard_map/ppermute | solution.py:73
  35.3 1.4 maximum_select_fusion
  36.7 0.0 copy-start.2
  36.7 4.9 %collective-permute-start.11 = (f32[512,512]{1,0:T(8,128)S(1)}, f32[512,512]{1,0:T(8,128)S(1)}, u32[]{:S(2)}, u32[]{:S(2)}) collective-permute-start(f32[512,512]{1,0:T(8,128)S(1)} %maximum_select_fusion), channel_id=1, source_target_pairs={{0,32},{32,0},{1,33},{33,1},{2,34},{34,2},{3,35},{35,3},{4,36},{36... | collective-permute-start | bytes 3145736 | tf_op jit(solution)/shard_map/ppermute | solution.py:74
  41.6 0.9 fusion.2
  42.5 2.2 %collective-permute-start.14 = (f32[256,512]{0,1:T(8,128)}, f32[256,512]{0,1:T(8,128)}, u32[]{:S(2)}, u32[]{:S(2)}) collective-permute-start(f32[256,512]{0,1:T(8,128)} %fusion.2), channel_id=1, source_target_pairs={{0,16},{16,0},{1,17},{17,1},{2,18},{18,2},{3,19},{19,3},{4,20},{20... | collective-permute-start | bytes 1572872 | tf_op jit(solution)/shard_map/ppermute | solution.py:68
  44.8 5.2 %collective-permute-start.1 = (f32[512,128]{1,0:T(8,128)S(1)}, f32[512,128]{1,0:T(8,128)}, u32[]{:S(2)}, u32[]{:S(2)}) collective-permute-start(f32[512,128]{1,0:T(8,128)S(1)} %broadcast_select_fusion.1), channel_id=1, source_target_pairs={{0,2},{32,46},{2,4},{34,32},{4,6},{36,34},{6,8},{38,36},{8,10},{40... | collective-permute-start | bytes 786440 | tf_op jit(solution)/shard_map/ppermute | solution.py:81
  50.0 1.0 broadcast_select_fusion
  51.0 6.4 %collective-permute-start.6 = (f32[512,128]{1,0:T(8,128)S(1)}, f32[512,128]{1,0:T(8,128)}, u32[]{:S(2)}, u32[]{:S(2)}) collective-permute-start(f32[512,128]{1,0:T(8,128)S(1)} %broadcast_select_fusion), channel_id=1, source_target_pairs={{0,2},{32,46},{2,4},{34,32},{4,6},{36,34},{6,8},{38,36},{8,10},{40... | collective-permute-start | bytes 786440 | tf_op jit(solution)/shard_map/ppermute | solution.py:82
  57.4 3.9 %collective-permute-done.1 = f32[512,128]{1,0:T(8,128)} collective-permute-done((f32[512,128]{1,0:T(8,128)S(1)}, f32[512,128]{1,0:T(8,128)}, u32[]{:S(2)}, u32[]{:S(2)}) %collective-permute-start.1) | collective-permute-done | bytes 262176 | tf_op jit(solution)/shard_map/ppermute | solution.py:81
  61.3 1.9 %collective-permute-start.2 = (f32[512,128]{1,0:T(8,128)}, f32[512,128]{1,0:T(8,128)}, u32[]{:S(2)}, u32[]{:S(2)}) collective-permute-start(f32[512,128]{1,0:T(8,128)} %collective-permute-done.1), channel_id=1, source_target_pairs={{0,2},{32,46},{2,4},{34,32},{4,6},{36,34},{6,8},{38,36},{8,10},{40... | collective-permute-start | bytes 786440 | tf_op jit(solution)/shard_map/ppermute | solution.py:81
  63.2 1.8 %collective-permute-done.6 = f32[512,128]{1,0:T(8,128)} collective-permute-done((f32[512,128]{1,0:T(8,128)S(1)}, f32[512,128]{1,0:T(8,128)}, u32[]{:S(2)}, u32[]{:S(2)}) %collective-permute-start.6) | collective-permute-done | bytes 262176 | tf_op jit(solution)/shard_map/ppermute | solution.py:82
  65.0 4.6 %collective-permute-start.7 = (f32[512,128]{1,0:T(8,128)}, f32[512,128]{1,0:T(8,128)}, u32[]{:S(2)}, u32[]{:S(2)}) collective-permute-start(f32[512,128]{1,0:T(8,128)} %collective-permute-done.6), channel_id=1, source_target_pairs={{0,2},{32,46},{2,4},{34,32},{4,6},{36,34},{6,8},{38,36},{8,10},{40... | collective-permute-start | bytes 786440 | tf_op jit(solution)/shard_map/ppermute | solution.py:82
  69.7 1.9 %fusion.1 = f32[256,512]{0,1:T(8,128)} fusion(f32[256,512]{0,1:T(8,128)} %collective-permute-done.14, s32[]{:T(128)S(6)} %select_n.84, f32[512,256]{0,1:T(8,128)S(1)} %fusion.6, f32[512,256]{0,1:T(8,128)S(1)} %fusion.4), kind=kLoop, calls=%fused_computation.10 | loop fusion | flops 262144 | bytes 2097156 | tf_op jit(solution)/shard_map/add | solution.py:69
  71.6 2.1 %copy.13 = f32[256,512]{1,0:T(8,128)} copy(f32[256,512]{0,1:T(8,128)} %fusion.1) | data formatting | bytes 1048576
  73.7 0.0 reduce-scatter.4.cloned.1.call-update
  73.7 5.9 %collective-permute-start.3 = (f32[512,128]{1,0:T(8,128)}, f32[512,128]{1,0:T(8,128)S(1)}, u32[]{:S(2)}, u32[]{:S(2)}) collective-permute-start(f32[512,128]{1,0:T(8,128)} %collective-permute-done.2), channel_id=1, source_target_pairs={{0,2},{32,46},{2,4},{34,32},{4,6},{36,34},{6,8},{38,36},{8,10},{40... | collective-permute-start | bytes 786440 | tf_op jit(solution)/shard_map/ppermute | solution.py:81
  79.6 5.4 %collective-permute-start.8 = (f32[512,128]{1,0:T(8,128)}, f32[512,128]{1,0:T(8,128)}, u32[]{:S(2)}, u32[]{:S(2)}) collective-permute-start(f32[512,128]{1,0:T(8,128)} %collective-permute-done.7), channel_id=1, source_target_pairs={{0,2},{32,46},{2,4},{34,32},{4,6},{36,34},{6,8},{38,36},{8,10},{40... | collective-permute-start | bytes 786440 | tf_op jit(solution)/shard_map/ppermute | solution.py:82
  85.0 1.4 fusion.12
  86.4 1.4 convolution_add_fusion.2
  87.9 0.9 copy-done.4
  88.8 0.5 fusion.11
  89.3 0.4 convolution_add_fusion.3
  89.8 0.9 pad_maximum_fusion
  90.7 4.9 %all-to-all-start = ((f32[8,128,128]{2,1,0:T(8,128)}), f32[8,128,128]{2,1,0:T(8,128)S(1)}, u32[]{:S(2)}, u32[]{:S(2)}) async-start(f32[8,128,128]{2,1,0:T(8,128)} %pad_maximum_fusion), calls=%async_computation | async-start | bytes 1048576 | tf_op jit(solution)/shard_map/all_to_all | solution.py:85
  95.6 1.4 fusion.13
  97.0 1.4 convolution_add_fusion.1
  98.5 5.6 %all-to-all-done = f32[8,128,128]{2,1,0:T(8,128)S(1)} async-done(((f32[8,128,128]{2,1,0:T(8,128)}), f32[8,128,128]{2,1,0:T(8,128)S(1)}, u32[]{:S(2)}, u32[]{:S(2)}) %all-to-all-start) | async-done | bytes 524320 | tf_op jit(solution)/shard_map/all_to_all | solution.py:85
  104.1 1.4 fusion.14
  105.5 0.4 convolution_add_fusion
  106.0 0.9 pad_maximum_fusion.1
  106.9 5.1 %all-to-all-start.1 = ((f32[8,128,128]{2,1,0:T(8,128)}), f32[8,128,128]{2,1,0:T(8,128)S(1)}, u32[]{:S(2)}, u32[]{:S(2)}) async-start(f32[8,128,128]{2,1,0:T(8,128)} %pad_maximum_fusion.1), calls=%async_computation.1 | async-start | bytes 1048576 | tf_op jit(solution)/shard_map/all_to_all | solution.py:88
  112.0 9.2 %all-to-all-done.1 = f32[8,128,128]{2,1,0:T(8,128)S(1)} async-done(((f32[8,128,128]{2,1,0:T(8,128)}), f32[8,128,128]{2,1,0:T(8,128)S(1)}, u32[]{:S(2)}, u32[]{:S(2)}) %all-to-all-start.1) | async-done | bytes 524320 | tf_op jit(solution)/shard_map/all_to_all | solution.py:88
  121.2 4.8 %collective-permute-start.12 = (f32[128,128]{1,0:T(8,128)S(1)}, f32[128,128]{1,0:T(8,128)S(1)}, u32[]{:S(2)}, u32[]{:S(2)}) collective-permute-start(f32[128,128]{1,0:T(8,128)S(1)} %get-tuple-element.39), channel_id=1, source_target_pairs={{0,0},{1,192},{2,34},{3,226},{4,68},{5,4},{6,102},{7,38},{8,136},{... | collective-permute-start | bytes 196616 | tf_op jit(solution)/shard_map/ppermute | solution.py:89
  126.0 1.9 %collective-permute-start.13 = (f32[128,128]{1,0:T(8,128)S(1)}, f32[128,128]{1,0:T(8,128)S(1)}, u32[]{:S(2)}, u32[]{:S(2)}) collective-permute-start(f32[128,128]{1,0:T(8,128)S(1)} %get-tuple-element.40), channel_id=1, source_target_pairs={{0,192},{1,0},{2,226},{3,34},{4,4},{5,68},{6,38},{7,102},{8,72},{9... | collective-permute-start | bytes 196616 | tf_op jit(solution)/shard_map/ppermute | solution.py:90
  128.0 15.6 %reduce-scatter.4.cloned.1.call-done = f32[16,512]{1,0:T(8,128)} async-done(((f32[256,512]{1,0:T(8,128)}), f32[16,512]{1,0:T(8,128)}) %reduce-scatter.4.cloned.1.call-update) | async-done | bytes 32784
  143.5 1.3 fusion.10
  144.9 0.7 maximum_select_fusion.2
  (39 shorter events, 0.3 us)
Async XLA Ops:
  7.2 136.4 %reduce-scatter.4.cloned.1.call-start = ((), (), s32[]{:S(2)}) async-start(), calls=%async_computation.3 | async-start | bytes 557056
  7.2 10.3 %collective-permute-start.9 = (f32[512,128]{1,0:T(8,128)}, f32[512,128]{1,0:T(8,128)S(1)}, u32[]{:S(2)}, u32[]{:S(2)}) collective-permute-start(f32[512,128]{1,0:T(8,128)} %param.6), channel_id=1, source_target_pairs={{0,1},{1,0},{2,3},{3,2},{4,5},{5,4},{6,7},{7,6},{8,9},{9,8},{10,11... | collective-permute-start | bytes 786440 | tf_op jit(solution)/shard_map/ppermute | solution.py:55
  11.0 14.2 %collective-permute-start.4 = (f32[512,128]{1,0:T(8,128)}, f32[512,128]{1,0:T(8,128)}, u32[]{:S(2)}, u32[]{:S(2)}) collective-permute-start(f32[512,128]{1,0:T(8,128)} %param.7), channel_id=1, source_target_pairs={{0,32},{32,0},{1,33},{33,1},{2,34},{34,2},{3,35},{35,3},{4,36},{36... | collective-permute-start | bytes 786440 | tf_op jit(solution)/shard_map/ppermute | solution.py:57
  13.0 4.6 %copy-start.8 = (f32[512]{0:T(512)S(1)}, f32[512]{0:T(512)}, u32[]{:S(2)}) copy-start(f32[512]{0:T(512)} %param.8) | copy-start | bytes 6148
  13.0 10.9 %copy-start.1 = (f32[512,128]{1,0:T(8,128)S(1)}, f32[512,128]{1,0:T(8,128)}, u32[]{:S(2)}) copy-start(f32[512,128]{1,0:T(8,128)} %param.7) | copy-start | bytes 786436
  13.0 13.1 %copy-start.5 = (f32[128,256]{1,0:T(8,128)S(1)}, f32[128,256]{1,0:T(8,128)}, u32[]{:S(2)}) copy-start(f32[128,256]{1,0:T(8,128)} %param.10) | copy-start | bytes 393220
  18.8 16.5 %collective-permute-start.10 = (f32[512,256]{1,0:T(8,128)S(1)}, f32[512,256]{1,0:T(8,128)}, u32[]{:S(2)}, u32[]{:S(2)}) collective-permute-start(f32[512,256]{1,0:T(8,128)S(1)} %fusion.3), channel_id=1, source_target_pairs={{0,16},{16,0},{1,17},{17,1},{2,18},{18,2},{3,19},{19,3},{4,20},{20... | collective-permute-start | bytes 1572872 | tf_op jit(solution)/shard_map/ppermute | solution.py:73
  23.9 20.8 %collective-permute-start = (f32[512,128]{1,0:T(8,128)S(1)}, f32[512,128]{1,0:T(8,128)}, u32[]{:S(2)}, u32[]{:S(2)}) collective-permute-start(f32[512,128]{1,0:T(8,128)S(1)} %copy-done.1), channel_id=1, source_target_pairs={{32,46},{34,32},{36,34},{38,36},{40,38},{42,40},{44,42},{46,44},{3... | collective-permute-start | bytes 786440 | tf_op jit(solution)/shard_map/ppermute | solution.py:56
  25.3 0.8 copy-start.7
  25.3 1.3 copy-start
  25.3 1.3 copy-start.6
  25.3 24.7 %collective-permute-start.5 = (f32[512,128]{1,0:T(8,128)}, f32[512,128]{1,0:T(8,128)S(1)}, u32[]{:S(2)}, u32[]{:S(2)}) collective-permute-start(f32[512,128]{1,0:T(8,128)} %collective-permute-done.4), channel_id=1, source_target_pairs={{32,46},{34,32},{36,34},{38,36},{40,38},{42,40},{44,42},{46,44},{3... | collective-permute-start | bytes 786440 | tf_op jit(solution)/shard_map/ppermute | solution.py:59
  36.7 8.1 %copy-start.2 = (f32[512,128]{1,0:T(8,128)S(1)}, f32[512,128]{1,0:T(8,128)}, u32[]{:S(2)}) copy-start(f32[512,128]{1,0:T(8,128)} %param.7) | copy-start | bytes 786436
  36.7 48.3 %collective-permute-start.11 = (f32[512,512]{1,0:T(8,128)S(1)}, f32[512,512]{1,0:T(8,128)S(1)}, u32[]{:S(2)}, u32[]{:S(2)}) collective-permute-start(f32[512,512]{1,0:T(8,128)S(1)} %maximum_select_fusion), channel_id=1, source_target_pairs={{0,32},{32,0},{1,33},{33,1},{2,34},{34,2},{3,35},{35,3},{4,36},{36... | collective-permute-start | bytes 3145736 | tf_op jit(solution)/shard_map/ppermute | solution.py:74
  42.5 27.2 %collective-permute-start.14 = (f32[256,512]{0,1:T(8,128)}, f32[256,512]{0,1:T(8,128)}, u32[]{:S(2)}, u32[]{:S(2)}) collective-permute-start(f32[256,512]{0,1:T(8,128)} %fusion.2), channel_id=1, source_target_pairs={{0,16},{16,0},{1,17},{17,1},{2,18},{18,2},{3,19},{19,3},{4,20},{20... | collective-permute-start | bytes 1572872 | tf_op jit(solution)/shard_map/ppermute | solution.py:68
  44.8 16.5 %collective-permute-start.1 = (f32[512,128]{1,0:T(8,128)S(1)}, f32[512,128]{1,0:T(8,128)}, u32[]{:S(2)}, u32[]{:S(2)}) collective-permute-start(f32[512,128]{1,0:T(8,128)S(1)} %broadcast_select_fusion.1), channel_id=1, source_target_pairs={{0,2},{32,46},{2,4},{34,32},{4,6},{36,34},{6,8},{38,36},{8,10},{40... | collective-permute-start | bytes 786440 | tf_op jit(solution)/shard_map/ppermute | solution.py:81
  51.0 10.3 %copy-start.3 = (f32[512,128]{1,0:T(8,128)}, f32[512,128]{1,0:T(8,128)S(1)}, u32[]{:S(2)}) copy-start(f32[512,128]{1,0:T(8,128)S(1)} %broadcast_select_fusion) | copy-start | bytes 786436
  51.0 14.1 %collective-permute-start.6 = (f32[512,128]{1,0:T(8,128)S(1)}, f32[512,128]{1,0:T(8,128)}, u32[]{:S(2)}, u32[]{:S(2)}) collective-permute-start(f32[512,128]{1,0:T(8,128)S(1)} %broadcast_select_fusion), channel_id=1, source_target_pairs={{0,2},{32,46},{2,4},{34,32},{4,6},{36,34},{6,8},{38,36},{8,10},{40... | collective-permute-start | bytes 786440 | tf_op jit(solution)/shard_map/ppermute | solution.py:82
  61.3 12.4 %collective-permute-start.2 = (f32[512,128]{1,0:T(8,128)}, f32[512,128]{1,0:T(8,128)}, u32[]{:S(2)}, u32[]{:S(2)}) collective-permute-start(f32[512,128]{1,0:T(8,128)} %collective-permute-done.1), channel_id=1, source_target_pairs={{0,2},{32,46},{2,4},{34,32},{4,6},{36,34},{6,8},{38,36},{8,10},{40... | collective-permute-start | bytes 786440 | tf_op jit(solution)/shard_map/ppermute | solution.py:81
  65.0 14.6 %collective-permute-start.7 = (f32[512,128]{1,0:T(8,128)}, f32[512,128]{1,0:T(8,128)}, u32[]{:S(2)}, u32[]{:S(2)}) collective-permute-start(f32[512,128]{1,0:T(8,128)} %collective-permute-done.6), channel_id=1, source_target_pairs={{0,2},{32,46},{2,4},{34,32},{4,6},{36,34},{6,8},{38,36},{8,10},{40... | collective-permute-start | bytes 786440 | tf_op jit(solution)/shard_map/ppermute | solution.py:82
  73.7 30.4 %collective-permute-start.3 = (f32[512,128]{1,0:T(8,128)}, f32[512,128]{1,0:T(8,128)S(1)}, u32[]{:S(2)}, u32[]{:S(2)}) collective-permute-start(f32[512,128]{1,0:T(8,128)} %collective-permute-done.2), channel_id=1, source_target_pairs={{0,2},{32,46},{2,4},{34,32},{4,6},{36,34},{6,8},{38,36},{8,10},{40... | collective-permute-start | bytes 786440 | tf_op jit(solution)/shard_map/ppermute | solution.py:81
  79.6 24.5 %collective-permute-start.8 = (f32[512,128]{1,0:T(8,128)}, f32[512,128]{1,0:T(8,128)}, u32[]{:S(2)}, u32[]{:S(2)}) collective-permute-start(f32[512,128]{1,0:T(8,128)} %collective-permute-done.7), channel_id=1, source_target_pairs={{0,2},{32,46},{2,4},{34,32},{4,6},{36,34},{6,8},{38,36},{8,10},{40... | collective-permute-start | bytes 786440 | tf_op jit(solution)/shard_map/ppermute | solution.py:82
  87.9 1.0 copy-start.4
  90.7 13.4 %all-to-all-start = ((f32[8,128,128]{2,1,0:T(8,128)}), f32[8,128,128]{2,1,0:T(8,128)S(1)}, u32[]{:S(2)}, u32[]{:S(2)}) async-start(f32[8,128,128]{2,1,0:T(8,128)} %pad_maximum_fusion), calls=%async_computation | async-start | bytes 1048576 | tf_op jit(solution)/shard_map/all_to_all | solution.py:85
  106.9 14.3 %all-to-all-start.1 = ((f32[8,128,128]{2,1,0:T(8,128)}), f32[8,128,128]{2,1,0:T(8,128)S(1)}, u32[]{:S(2)}, u32[]{:S(2)}) async-start(f32[8,128,128]{2,1,0:T(8,128)} %pad_maximum_fusion.1), calls=%async_computation.1 | async-start | bytes 1048576 | tf_op jit(solution)/shard_map/all_to_all | solution.py:88
  121.2 23.7 %collective-permute-start.12 = (f32[128,128]{1,0:T(8,128)S(1)}, f32[128,128]{1,0:T(8,128)S(1)}, u32[]{:S(2)}, u32[]{:S(2)}) collective-permute-start(f32[128,128]{1,0:T(8,128)S(1)} %get-tuple-element.39), channel_id=1, source_target_pairs={{0,0},{1,192},{2,34},{3,226},{4,68},{5,4},{6,102},{7,38},{8,136},{... | collective-permute-start | bytes 196616 | tf_op jit(solution)/shard_map/ppermute | solution.py:89
  126.0 18.9 %collective-permute-start.13 = (f32[128,128]{1,0:T(8,128)S(1)}, f32[128,128]{1,0:T(8,128)S(1)}, u32[]{:S(2)}, u32[]{:S(2)}) collective-permute-start(f32[128,128]{1,0:T(8,128)S(1)} %get-tuple-element.40), channel_id=1, source_target_pairs={{0,192},{1,0},{2,226},{3,34},{4,4},{5,68},{6,38},{7,102},{8,72},{9... | collective-permute-start | bytes 196616 | tf_op jit(solution)/shard_map/ppermute | solution.py:90
Sparse Core Ops, SparseCore 0:
  73.8 69.6 reduce-scatter.3

commit v4 on v2

--- a/solution.py
+++ b/solution.py
@@ -52,19 +52,22 @@
     cells, cols = direct.shape
     modes = right_vecs.shape[1]
 
-    scale = inv_root[None, :]
-    terms = jnp.concatenate([_dot(direct, right_vecs * scale), _dot(adjoint, left_vecs * scale)], axis=1)
-    half = cells // 2
-    away = lax.ppermute(lax.dynamic_slice_in_dim(terms, (1 - h) * half, half, 0), "h", SWAP)
     next_direct = lax.ppermute(direct, "q", SWAP)
     next_own = lax.ppermute(adjoint, ("c", "g"), _ring_pairs(False))
     other = lax.ppermute(adjoint, "c", SWAP)
+    scale = inv_root[None, :]
+    terms = jnp.concatenate([_dot(direct, right_vecs * scale), _dot(adjoint, left_vecs * scale)], axis=1)
+    rows = cells // 32
+    terms = terms.reshape(2, 8, 2, rows, 2 * modes).transpose(2, 1, 0, 3, 4).reshape(2, cells // 2, 2 * modes)
+    away = lax.dynamic_index_in_dim(terms, 1 - q, 0, keepdims=False)
+    away, other = lax.optimization_barrier((away, other))
+    away = lax.ppermute(away, "q", SWAP)
     next_other = lax.ppermute(other, ("c", "g"), _ring_pairs(False))
     own = jnp.where(c == 0, adjoint, next_own)
     other = jnp.where(c == 0, other, next_other)
 
-    terms = away + lax.dynamic_slice_in_dim(terms, h * half, half, 0)
-    summed = lax.psum_scatter(terms, ("g", "q"), scatter_dimension=0, tiled=True)
+    terms = away + lax.dynamic_index_in_dim(terms, q, 0, keepdims=False)
+    part = lax.psum_scatter(terms, "g", scatter_dimension=0, tiled=True).reshape(2, rows, 2 * modes)
 
     pair = _beside(q, direct, next_direct) * cell_weight[:, None]
     both = _beside(h, pair, lax.ppermute(pair, "h", SWAP))
@@ -90,6 +93,10 @@
     behind = (lax.axis_index("g") - low) % 8
     arrival = jnp.where(behind < 4, behind, 7 - behind)
     gram = jnp.where(arrival < 2, jnp.concatenate([home0, home1]), jnp.concatenate([home1, home0]))
+
+    keep = lax.dynamic_index_in_dim(part, h, 0, keepdims=False)
+    away = lax.dynamic_index_in_dim(part, 1 - h, 0, keepdims=False)
+    summed = keep + lax.ppermute(away, "h", SWAP)
     return (gram, summed[:, :modes], summed[:, modes:])
 
 

time: 155 us -> 171 us (1.10)
  the two profiles are of different devices: /device:TPU:12 before, /device:TPU:39 now
where the time goes in v4:
time: 171 us; the launch traced here: 170 us
  starting transfers between devices  93.2 us (55%)
  waiting for transfers between devices  40.6 us (24%)
  between operations  14.6 us (9%)
  other arithmetic  10.2 us (6%)
  matrix products  8.21 us (5%)
  local copies, waits for them, and re-layouts  3.46 us (2%)
    ppermute x3, starting transfers between devices, local(): own = lax.ppermute(own, ('c', 'g'), _ring_pairs(True))  17.9 us
    ppermute x3, starting transfers between devices, local(): other = lax.ppermute(other, ('c', 'g'), _ring_pairs(True))  14.4 us
    ppermute x3, waiting for transfers between devices, local(): own = lax.ppermute(own, ('c', 'g'), _ring_pairs(True))  13.9 us
    ppermute x1, starting transfers between devices, local(): home0 = lax.ppermute(jnp.where(q == 0, early, late), AXES, _home_pairs(0))  12.7 us
    ppermute x1, starting transfers between devices, local(): next_own = lax.ppermute(adjoint, ('c', 'g'), _ring_pairs(False))  11.4 us
    ppermute x1, waiting for transfers between devices, local(): both = _beside(h, pair, lax.ppermute(pair, 'h', SWAP))  10.4 us
    dot_general x8, matrix products, _cross(): lax.dot_general(a, b, (((0,), (0,)), ((), ())), precision=PREC, preferred...  7.37 us
    reduce_scatter x1, waiting for transfers between devices, local(): lax.psum_scatter(terms, 'g', scatter_dimension=0, tiled=True)  5.61 us
  transfers between devices with their start and end apart: 19, of which 8 were waited for; matrix products, arithmetic and copies ran while one was open for 12% of the time, Pallas kernels for 0%

profile of v4, /device:TPU:39, one launch (start us, length us, event | category | flops | bytes accessed | tf_op | source)
XLA Modules:
  0.0 170.2 jit_solution(17881106219299566493)
XLA Ops:
  7.2 1.9 %collective-permute-start.9 = (f32[512,128]{1,0:T(8,128)}, f32[512,128]{1,0:T(8,128)S(1)}, u32[]{:S(2)}, u32[]{:S(2)}) collective-permute-start(f32[512,128]{1,0:T(8,128)} %param.6), channel_id=1, source_target_pairs={{0,1},{1,0},{2,3},{3,2},{4,5},{5,4},{6,7},{7,6},{8,9},{9,8},{10,11... | collective-permute-start | bytes 786440 | tf_op jit(solution)/shard_map/ppermute | solution.py:55
  9.1 11.4 %collective-permute-start = (f32[512,128]{1,0:T(8,128)}, f32[512,128]{1,0:T(8,128)}, u32[]{:S(2)}, u32[]{:S(2)}) collective-permute-start(f32[512,128]{1,0:T(8,128)} %param.7), channel_id=1, source_target_pairs={{32,46},{34,32},{36,34},{38,36},{40,38},{42,40},{44,42},{46,44},{3... | collective-permute-start | bytes 786440 | tf_op jit(solution)/shard_map/ppermute | solution.py:56
  20.5 1.9 %collective-permute-start.4 = (f32[512,128]{1,0:T(8,128)}, f32[512,128]{1,0:T(8,128)}, u32[]{:S(2)}, u32[]{:S(2)}) collective-permute-start(f32[512,128]{1,0:T(8,128)} %param.7), channel_id=1, source_target_pairs={{0,32},{32,0},{1,33},{33,1},{2,34},{34,2},{3,35},{35,3},{4,36},{36... | collective-permute-start | bytes 786440 | tf_op jit(solution)/shard_map/ppermute | solution.py:57
  22.5 0.6 copy-done.8
  23.2 2.0 %fusion = f32[512,256]{1,0:T(8,128)} fusion(f32[512,128]{1,0:T(8,128)S(1)} %collective-permute-done.9, f32[512,128]{1,0:T(8,128)} %param.6, f32[512]{0:T(512)S(1)} %copy-done.8, pred[]{:T(512)S(6)} %eq.15), kind=kLoop, calls=%fused_computation.9 | loop fusion | flops 524288 | bytes 1050625 | tf_op jit(solution)/shard_map/mul | solution.py:72
  25.1 4.9 %collective-permute-start.10 = (f32[512,256]{1,0:T(8,128)}, f32[512,256]{1,0:T(8,128)}, u32[]{:S(2)}, u32[]{:S(2)}) collective-permute-start(f32[512,256]{1,0:T(8,128)} %fusion), channel_id=1, source_target_pairs={{0,16},{16,0},{1,17},{17,1},{2,18},{18,2},{3,19},{19,3},{4,20},{20... | collective-permute-start | bytes 1572872 | tf_op jit(solution)/shard_map/ppermute | solution.py:73
  30.1 0.4 convolution_bitcast_fusion.1
  30.5 0.4 convolution_bitcast_fusion
  31.5 10.4 %collective-permute-done.10 = f32[512,256]{1,0:T(8,128)} collective-permute-done((f32[512,256]{1,0:T(8,128)}, f32[512,256]{1,0:T(8,128)}, u32[]{:S(2)}, u32[]{:S(2)}) %collective-permute-start.10) | collective-permute-done | bytes 524320 | tf_op jit(solution)/shard_map/ppermute | solution.py:73
  41.9 1.7 %maximum_select_fusion = f32[512,512]{1,0:T(8,128)S(1)} fusion(f32[512,256]{1,0:T(8,128)} %collective-permute-done.10, f32[512,256]{1,0:T(8,128)} %fusion, pred[]{:T(512)S(6)} %eq.17), kind=kLoop, calls=%fused_computation.7 | loop fusion | flops 786432 | bytes 2097153 | tf_op jit(solution)/shard_map/jit(_where)/select_n | solution.py:45
  43.7 3.3 %collective-permute-start.11 = (f32[512,512]{1,0:T(8,128)S(1)}, f32[512,512]{1,0:T(8,128)S(1)}, u32[]{:S(2)}, u32[]{:S(2)}) collective-permute-start(f32[512,512]{1,0:T(8,128)S(1)} %maximum_select_fusion), channel_id=1, source_target_pairs={{0,32},{32,0},{1,33},{33,1},{2,34},{34,2},{3,35},{35,3},{4,36},{36... | collective-permute-start | bytes 3145736 | tf_op jit(solution)/shard_map/ppermute | solution.py:74
  46.9 0.8 dynamic-slice_bitcast_fusion
  47.8 4.0 %collective-permute-start.5 = (f32[512,128]{1,0:T(8,128)}, f32[512,128]{1,0:T(8,128)}, u32[]{:S(2)}, u32[]{:S(2)}) collective-permute-start(f32[512,128]{1,0:T(8,128)} %collective-permute-done.4), channel_id=1, source_target_pairs={{32,46},{34,32},{36,34},{38,36},{40,38},{42,40},{44,42},{46,44},{3... | collective-permute-start | bytes 786440 | tf_op jit(solution)/shard_map/ppermute | solution.py:65
  51.8 2.6 %collective-permute-start.14 = (f32[256,512]{1,0:T(8,128)}, f32[256,512]{1,0:T(8,128)}, u32[]{:S(2)}, u32[]{:S(2)}) collective-permute-start(f32[256,512]{1,0:T(8,128)} %dynamic-slice_bitcast_fusion), channel_id=1, source_target_pairs={{0,1},{1,0},{2,3},{3,2},{4,5},{5,4},{6,7},{7,6},{8,9},{9,8},{10,11... | collective-permute-start | bytes 1572872 | tf_op jit(solution)/shard_map/ppermute | solution.py:64
  54.4 1.0 broadcast_select_fusion.1
  55.4 5.9 %collective-permute-start.1 = (f32[512,128]{1,0:T(8,128)S(1)}, f32[512,128]{1,0:T(8,128)}, u32[]{:S(2)}, u32[]{:S(2)}) collective-permute-start(f32[512,128]{1,0:T(8,128)S(1)} %broadcast_select_fusion.1), channel_id=1, source_target_pairs={{0,2},{32,46},{2,4},{34,32},{4,6},{36,34},{6,8},{38,36},{8,10},{40... | collective-permute-start | bytes 786440 | tf_op jit(solution)/shard_map/ppermute | solution.py:81
  61.3 1.8 %collective-permute-done.5 = f32[512,128]{1,0:T(8,128)} collective-permute-done((f32[512,128]{1,0:T(8,128)}, f32[512,128]{1,0:T(8,128)}, u32[]{:S(2)}, u32[]{:S(2)}) %collective-permute-start.5) | collective-permute-done | bytes 262176 | tf_op jit(solution)/shard_map/ppermute | solution.py:65
  63.2 1.0 broadcast_select_fusion
  64.2 6.1 %collective-permute-start.6 = (f32[512,128]{1,0:T(8,128)S(1)}, f32[512,128]{1,0:T(8,128)}, u32[]{:S(2)}, u32[]{:S(2)}) collective-permute-start(f32[512,128]{1,0:T(8,128)S(1)} %broadcast_select_fusion), channel_id=1, source_target_pairs={{0,2},{32,46},{2,4},{34,32},{4,6},{36,34},{6,8},{38,36},{8,10},{40... | collective-permute-start | bytes 786440 | tf_op jit(solution)/shard_map/ppermute | solution.py:82
  70.2 12.7 %collective-permute-done.1 = f32[512,128]{1,0:T(8,128)} collective-permute-done((f32[512,128]{1,0:T(8,128)S(1)}, f32[512,128]{1,0:T(8,128)}, u32[]{:S(2)}, u32[]{:S(2)}) %collective-permute-start.1) | collective-permute-done | bytes 262176 | tf_op jit(solution)/shard_map/ppermute | solution.py:81
  82.9 6.0 %collective-permute-start.2 = (f32[512,128]{1,0:T(8,128)}, f32[512,128]{1,0:T(8,128)}, u32[]{:S(2)}, u32[]{:S(2)}) collective-permute-start(f32[512,128]{1,0:T(8,128)} %collective-permute-done.1), channel_id=1, source_target_pairs={{0,2},{32,46},{2,4},{34,32},{4,6},{36,34},{6,8},{38,36},{8,10},{40... | collective-permute-start | bytes 786440 | tf_op jit(solution)/shard_map/ppermute | solution.py:81
  88.9 3.6 %collective-permute-start.7 = (f32[512,128]{1,0:T(8,128)}, f32[512,128]{1,0:T(8,128)}, u32[]{:S(2)}, u32[]{:S(2)}) collective-permute-start(f32[512,128]{1,0:T(8,128)} %collective-permute-done.6), channel_id=1, source_target_pairs={{0,2},{32,46},{2,4},{34,32},{4,6},{36,34},{6,8},{38,36},{8,10},{40... | collective-permute-start | bytes 786440 | tf_op jit(solution)/shard_map/ppermute | solution.py:82
  92.6 1.9 %bitcast_add_fusion = f32[256,512]{1,0:T(8,128)} fusion(f32[256,512]{1,0:T(8,128)} %collective-permute-done.14, f32[2,256,512]{2,1,0:T(8,128)S(1)} %bitcast.69, s32[]{:T(128)S(6)} %select_n.92), kind=kLoop, calls=%fused_computation.12 | loop fusion | flops 131072 | bytes 1572868 | tf_op jit(solution)/shard_map/add | solution.py:69
  94.5 1.2 collective-permute-done.2
  95.8 6.0 %collective-permute-start.3 = (f32[512,128]{1,0:T(8,128)}, f32[512,128]{1,0:T(8,128)S(1)}, u32[]{:S(2)}, u32[]{:S(2)}) collective-permute-start(f32[512,128]{1,0:T(8,128)} %collective-permute-done.2), channel_id=1, source_target_pairs={{0,2},{32,46},{2,4},{34,32},{4,6},{36,34},{6,8},{38,36},{8,10},{40... | collective-permute-start | bytes 786440 | tf_op jit(solution)/shard_map/ppermute | solution.py:81
  101.8 4.7 %collective-permute-start.8 = (f32[512,128]{1,0:T(8,128)}, f32[512,128]{1,0:T(8,128)S(1)}, u32[]{:S(2)}, u32[]{:S(2)}) collective-permute-start(f32[512,128]{1,0:T(8,128)} %collective-permute-done.7), channel_id=1, source_target_pairs={{0,2},{32,46},{2,4},{34,32},{4,6},{36,34},{6,8},{38,36},{8,10},{40... | collective-permute-start | bytes 786440 | tf_op jit(solution)/shard_map/ppermute | solution.py:82
  106.5 0.4 fusion.6
  107.0 0.4 convolution_add_fusion.3
  107.5 1.4 fusion.7
  108.9 1.4 convolution_add_fusion.2
  110.3 0.8 pad_maximum_fusion.1
  111.2 5.2 %all-to-all-start = ((f32[8,128,128]{2,1,0:T(8,128)}), f32[8,128,128]{2,1,0:T(8,128)S(1)}, u32[]{:S(2)}, u32[]{:S(2)}) async-start(f32[8,128,128]{2,1,0:T(8,128)} %pad_maximum_fusion.1), calls=%async_computation | async-start | bytes 1048576 | tf_op jit(solution)/shard_map/all_to_all | solution.py:85
  116.4 1.4 fusion.8
  117.8 1.4 convolution_add_fusion.1
  119.3 2.7 %all-to-all-done = f32[8,128,128]{2,1,0:T(8,128)S(1)} async-done(((f32[8,128,128]{2,1,0:T(8,128)}), f32[8,128,128]{2,1,0:T(8,128)S(1)}, u32[]{:S(2)}, u32[]{:S(2)}) %all-to-all-start) | async-done | bytes 524320 | tf_op jit(solution)/shard_map/all_to_all | solution.py:85
  122.0 0.4 fusion.9
  122.5 0.4 convolution_add_fusion
  123.0 0.9 pad_maximum_fusion.2
  123.8 4.9 %all-to-all-start.1 = ((f32[8,128,128]{2,1,0:T(8,128)}), f32[8,128,128]{2,1,0:T(8,128)S(1)}, u32[]{:S(2)}, u32[]{:S(2)}) async-start(f32[8,128,128]{2,1,0:T(8,128)} %pad_maximum_fusion.2), calls=%async_computation.1 | async-start | bytes 1048576 | tf_op jit(solution)/shard_map/all_to_all | solution.py:88
  128.7 5.6 %reduce-scatter.2.cloned.1.call-done = f32[32,512]{1,0:T(8,128)} async-done(((f32[256,512]{1,0:T(8,128)}), f32[32,512]{1,0:T(8,128)}) %reduce-scatter.2.cloned.1.call-update) | async-done | bytes 65552 | tf_op jit(solution)/shard_map/reduce_scatter | solution.py:70
  134.3 0.8 dynamic-slice_bitcast_fusion.1
  135.2 4.5 %collective-permute-start.15 = (f32[16,512]{1,0:T(8,128)S(1)}, f32[16,512]{1,0:T(8,128)S(1)}, u32[]{:S(2)}, u32[]{:S(2)}) collective-permute-start(f32[16,512]{1,0:T(8,128)S(1)} %dynamic-slice_bitcast_fusion.1), channel_id=1, source_target_pairs={{0,16},{16,0},{1,17},{17,1},{2,18},{18,2},{3,19},{19,3},{4,20},{20... | collective-permute-start | bytes 98312 | tf_op jit(solution)/shard_map/ppermute | solution.py:99
  139.7 1.6 collective-permute-done.15
  141.4 12.7 %collective-permute-start.12 = (f32[128,128]{1,0:T(8,128)S(1)}, f32[128,128]{1,0:T(8,128)S(1)}, u32[]{:S(2)}, u32[]{:S(2)}) collective-permute-start(f32[128,128]{1,0:T(8,128)S(1)} %get-tuple-element.31), channel_id=1, source_target_pairs={{0,0},{1,192},{2,34},{3,226},{4,68},{5,4},{6,102},{7,38},{8,136},{... | collective-permute-start | bytes 196616 | tf_op jit(solution)/shard_map/ppermute | solution.py:89
  154.1 3.4 %collective-permute-start.13 = (f32[128,128]{1,0:T(8,128)S(1)}, f32[128,128]{1,0:T(8,128)S(1)}, u32[]{:S(2)}, u32[]{:S(2)}) collective-permute-start(f32[128,128]{1,0:T(8,128)S(1)} %get-tuple-element.32), channel_id=1, source_target_pairs={{0,192},{1,0},{2,226},{3,34},{4,4},{5,68},{6,38},{7,102},{8,72},{9... | collective-permute-start | bytes 196616 | tf_op jit(solution)/shard_map/ppermute | solution.py:90
  157.6 0.6 fusion.5
  158.2 4.5 %collective-permute-done.13 = f32[128,128]{1,0:T(8,128)S(1)} collective-permute-done((f32[128,128]{1,0:T(8,128)S(1)}, f32[128,128]{1,0:T(8,128)S(1)}, u32[]{:S(2)}, u32[]{:S(2)}) %collective-permute-start.13) | collective-permute-done | bytes 65568 | tf_op jit(solution)/shard_map/ppermute | solution.py:90
  162.7 0.7 maximum_select_fusion.2
  (45 shorter events, 0.9 us)
Async XLA Ops:
  7.2 127.2 %reduce-scatter.2.cloned.1.call-start = ((), (), s32[]{:S(2)}) async-start(), calls=%async_computation.3 | async-start | bytes 589824 | tf_op jit(solution)/shard_map/reduce_scatter | solution.py:70
  7.2 15.3 %collective-permute-start.9 = (f32[512,128]{1,0:T(8,128)}, f32[512,128]{1,0:T(8,128)S(1)}, u32[]{:S(2)}, u32[]{:S(2)}) collective-permute-start(f32[512,128]{1,0:T(8,128)} %param.6), channel_id=1, source_target_pairs={{0,1},{1,0},{2,3},{3,2},{4,5},{5,4},{6,7},{7,6},{8,9},{9,8},{10,11... | collective-permute-start | bytes 786440 | tf_op jit(solution)/shard_map/ppermute | solution.py:55
  9.1 45.3 %collective-permute-start = (f32[512,128]{1,0:T(8,128)}, f32[512,128]{1,0:T(8,128)}, u32[]{:S(2)}, u32[]{:S(2)}) collective-permute-start(f32[512,128]{1,0:T(8,128)} %param.7), channel_id=1, source_target_pairs={{32,46},{34,32},{36,34},{38,36},{40,38},{42,40},{44,42},{46,44},{3... | collective-permute-start | bytes 786440 | tf_op jit(solution)/shard_map/ppermute | solution.py:56
  20.5 27.2 %collective-permute-start.4 = (f32[512,128]{1,0:T(8,128)}, f32[512,128]{1,0:T(8,128)}, u32[]{:S(2)}, u32[]{:S(2)}) collective-permute-start(f32[512,128]{1,0:T(8,128)} %param.7), channel_id=1, source_target_pairs={{0,32},{32,0},{1,33},{33,1},{2,34},{34,2},{3,35},{35,3},{4,36},{36... | collective-permute-start | bytes 786440 | tf_op jit(solution)/shard_map/ppermute | solution.py:57
  22.5 0.7 copy-start.8
  22.5 7.6 %copy-start = (f32[512,128]{1,0:T(8,128)S(1)}, f32[512,128]{1,0:T(8,128)}, u32[]{:S(2)}) copy-start(f32[512,128]{1,0:T(8,128)} %param.6) | copy-start | bytes 786436
  22.5 7.6 %copy-start.4 = (f32[128,256]{1,0:T(8,128)S(1)}, f32[128,256]{1,0:T(8,128)}, u32[]{:S(2)}) copy-start(f32[128,256]{1,0:T(8,128)} %param.9) | copy-start | bytes 393220
  22.5 7.6 %copy-start.7 = (f32[256]{0:T(256)S(1)}, f32[256]{0:T(256)}, u32[]{:S(2)}) copy-start(f32[256]{0:T(256)} %param.11) | copy-start | bytes 3076
  25.1 5.4 %copy-start.1 = (f32[512,128]{1,0:T(8,128)S(1)}, f32[512,128]{1,0:T(8,128)}, u32[]{:S(2)}) copy-start(f32[512,128]{1,0:T(8,128)} %param.7) | copy-start | bytes 786436
  25.1 5.4 %copy-start.5 = (f32[128,256]{1,0:T(8,128)S(1)}, f32[128,256]{1,0:T(8,128)}, u32[]{:S(2)}) copy-start(f32[128,256]{1,0:T(8,128)} %param.10) | copy-start | bytes 393220
  25.1 16.8 %collective-permute-start.10 = (f32[512,256]{1,0:T(8,128)}, f32[512,256]{1,0:T(8,128)}, u32[]{:S(2)}, u32[]{:S(2)}) collective-permute-start(f32[512,256]{1,0:T(8,128)} %fusion), channel_id=1, source_target_pairs={{0,16},{16,0},{1,17},{17,1},{2,18},{18,2},{3,19},{19,3},{4,20},{20... | collective-permute-start | bytes 1572872 | tf_op jit(solution)/shard_map/ppermute | solution.py:73
  43.7 62.8 %collective-permute-start.11 = (f32[512,512]{1,0:T(8,128)S(1)}, f32[512,512]{1,0:T(8,128)S(1)}, u32[]{:S(2)}, u32[]{:S(2)}) collective-permute-start(f32[512,512]{1,0:T(8,128)S(1)} %maximum_select_fusion), channel_id=1, source_target_pairs={{0,32},{32,0},{1,33},{33,1},{2,34},{34,2},{3,35},{35,3},{4,36},{36... | collective-permute-start | bytes 3145736 | tf_op jit(solution)/shard_map/ppermute | solution.py:74
  47.8 15.4 %collective-permute-start.5 = (f32[512,128]{1,0:T(8,128)}, f32[512,128]{1,0:T(8,128)}, u32[]{:S(2)}, u32[]{:S(2)}) collective-permute-start(f32[512,128]{1,0:T(8,128)} %collective-permute-done.4), channel_id=1, source_target_pairs={{32,46},{34,32},{36,34},{38,36},{40,38},{42,40},{44,42},{46,44},{3... | collective-permute-start | bytes 786440 | tf_op jit(solution)/shard_map/ppermute | solution.py:65
  51.8 40.8 %collective-permute-start.14 = (f32[256,512]{1,0:T(8,128)}, f32[256,512]{1,0:T(8,128)}, u32[]{:S(2)}, u32[]{:S(2)}) collective-permute-start(f32[256,512]{1,0:T(8,128)} %dynamic-slice_bitcast_fusion), channel_id=1, source_target_pairs={{0,1},{1,0},{2,3},{3,2},{4,5},{5,4},{6,7},{7,6},{8,9},{9,8},{10,11... | collective-permute-start | bytes 1572872 | tf_op jit(solution)/shard_map/ppermute | solution.py:64
  55.4 27.5 %collective-permute-start.1 = (f32[512,128]{1,0:T(8,128)S(1)}, f32[512,128]{1,0:T(8,128)}, u32[]{:S(2)}, u32[]{:S(2)}) collective-permute-start(f32[512,128]{1,0:T(8,128)S(1)} %broadcast_select_fusion.1), channel_id=1, source_target_pairs={{0,2},{32,46},{2,4},{34,32},{4,6},{36,34},{6,8},{38,36},{8,10},{40... | collective-permute-start | bytes 786440 | tf_op jit(solution)/shard_map/ppermute | solution.py:81
  64.1 18.8 %copy-start.2 = (f32[512,128]{1,0:T(8,128)}, f32[512,128]{1,0:T(8,128)S(1)}, u32[]{:S(2)}) copy-start(f32[512,128]{1,0:T(8,128)S(1)} %broadcast_select_fusion) | copy-start | bytes 786436
  64.2 24.8 %collective-permute-start.6 = (f32[512,128]{1,0:T(8,128)S(1)}, f32[512,128]{1,0:T(8,128)}, u32[]{:S(2)}, u32[]{:S(2)}) collective-permute-start(f32[512,128]{1,0:T(8,128)S(1)} %broadcast_select_fusion), channel_id=1, source_target_pairs={{0,2},{32,46},{2,4},{34,32},{4,6},{36,34},{6,8},{38,36},{8,10},{40... | collective-permute-start | bytes 786440 | tf_op jit(solution)/shard_map/ppermute | solution.py:82
  82.9 12.9 %collective-permute-start.2 = (f32[512,128]{1,0:T(8,128)}, f32[512,128]{1,0:T(8,128)}, u32[]{:S(2)}, u32[]{:S(2)}) collective-permute-start(f32[512,128]{1,0:T(8,128)} %collective-permute-done.1), channel_id=1, source_target_pairs={{0,2},{32,46},{2,4},{34,32},{4,6},{36,34},{6,8},{38,36},{8,10},{40... | collective-permute-start | bytes 786440 | tf_op jit(solution)/shard_map/ppermute | solution.py:81
  88.9 12.8 %collective-permute-start.7 = (f32[512,128]{1,0:T(8,128)}, f32[512,128]{1,0:T(8,128)}, u32[]{:S(2)}, u32[]{:S(2)}) collective-permute-start(f32[512,128]{1,0:T(8,128)} %collective-permute-done.6), channel_id=1, source_target_pairs={{0,2},{32,46},{2,4},{34,32},{4,6},{36,34},{6,8},{38,36},{8,10},{40... | collective-permute-start | bytes 786440 | tf_op jit(solution)/shard_map/ppermute | solution.py:82
  94.5 12.0 %copy-start.3 = (f32[512,128]{1,0:T(8,128)S(1)}, f32[512,128]{1,0:T(8,128)}, u32[]{:S(2)}) copy-start(f32[512,128]{1,0:T(8,128)} %copy-done.2) | copy-start | bytes 786436
  95.8 26.2 %collective-permute-start.3 = (f32[512,128]{1,0:T(8,128)}, f32[512,128]{1,0:T(8,128)S(1)}, u32[]{:S(2)}, u32[]{:S(2)}) collective-permute-start(f32[512,128]{1,0:T(8,128)} %collective-permute-done.2), channel_id=1, source_target_pairs={{0,2},{32,46},{2,4},{34,32},{4,6},{36,34},{6,8},{38,36},{8,10},{40... | collective-permute-start | bytes 786440 | tf_op jit(solution)/shard_map/ppermute | solution.py:81
  101.8 20.2 %collective-permute-start.8 = (f32[512,128]{1,0:T(8,128)}, f32[512,128]{1,0:T(8,128)S(1)}, u32[]{:S(2)}, u32[]{:S(2)}) collective-permute-start(f32[512,128]{1,0:T(8,128)} %collective-permute-done.7), channel_id=1, source_target_pairs={{0,2},{32,46},{2,4},{34,32},{4,6},{36,34},{6,8},{38,36},{8,10},{40... | collective-permute-start | bytes 786440 | tf_op jit(solution)/shard_map/ppermute | solution.py:82
  111.2 10.8 %all-to-all-start = ((f32[8,128,128]{2,1,0:T(8,128)}), f32[8,128,128]{2,1,0:T(8,128)S(1)}, u32[]{:S(2)}, u32[]{:S(2)}) async-start(f32[8,128,128]{2,1,0:T(8,128)} %pad_maximum_fusion.1), calls=%async_computation | async-start | bytes 1048576 | tf_op jit(solution)/shard_map/all_to_all | solution.py:85
  123.8 17.5 %all-to-all-start.1 = ((f32[8,128,128]{2,1,0:T(8,128)}), f32[8,128,128]{2,1,0:T(8,128)S(1)}, u32[]{:S(2)}, u32[]{:S(2)}) async-start(f32[8,128,128]{2,1,0:T(8,128)} %pad_maximum_fusion.2), calls=%async_computation.1 | async-start | bytes 1048576 | tf_op jit(solution)/shard_map/all_to_all | solution.py:88
  134.3 7.0 %copy-start.6 = (f32[32,512]{1,0:T(8,128)S(1)}, f32[32,512]{1,0:T(8,128)}, u32[]{:S(2)}) copy-start(f32[32,512]{1,0:T(8,128)} %reduce-scatter.2.cloned.1.call-done) | copy-start | bytes 196612
  135.2 6.2 %collective-permute-start.15 = (f32[16,512]{1,0:T(8,128)S(1)}, f32[16,512]{1,0:T(8,128)S(1)}, u32[]{:S(2)}, u32[]{:S(2)}) collective-permute-start(f32[16,512]{1,0:T(8,128)S(1)} %dynamic-slice_bitcast_fusion.1), channel_id=1, source_target_pairs={{0,16},{16,0},{1,17},{17,1},{2,18},{18,2},{3,19},{19,3},{4,20},{20... | collective-permute-start | bytes 98312 | tf_op jit(solution)/shard_map/ppermute | solution.py:99
  141.4 16.8 %collective-permute-start.12 = (f32[128,128]{1,0:T(8,128)S(1)}, f32[128,128]{1,0:T(8,128)S(1)}, u32[]{:S(2)}, u32[]{:S(2)}) collective-permute-start(f32[128,128]{1,0:T(8,128)S(1)} %get-tuple-element.31), channel_id=1, source_target_pairs={{0,0},{1,192},{2,34},{3,226},{4,68},{5,4},{6,102},{7,38},{8,136},{... | collective-permute-start | bytes 196616 | tf_op jit(solution)/shard_map/ppermute | solution.py:89
  154.1 8.6 %collective-permute-start.13 = (f32[128,128]{1,0:T(8,128)S(1)}, f32[128,128]{1,0:T(8,128)S(1)}, u32[]{:S(2)}, u32[]{:S(2)}) collective-permute-start(f32[128,128]{1,0:T(8,128)S(1)} %get-tuple-element.32), channel_id=1, source_target_pairs={{0,192},{1,0},{2,226},{3,34},{4,4},{5,68},{6,38},{7,102},{8,72},{9... | collective-permute-start | bytes 196616 | tf_op jit(solution)/shard_map/ppermute | solution.py:90
Sparse Core Ops, SparseCore 0:
  94.7 39.6 reduce-scatter.1

commit v5 on v2

--- a/solution.py
+++ b/solution.py
@@ -10,13 +10,7 @@
 SWAP = [(0, 1), (1, 0)]
 
 
-def _ring_pairs(up):
-    pairs = []
-    for g in range(8):
-        if up:
-            pairs.append((g, (g + 1) % 8))
-        pairs.append((8 + g, 8 + (g - 1) % 8))
-    return pairs
+RING = [(g, (g + 1) % 8) for g in range(8)] + [(8 + g, 8 + (g - 1) % 8) for g in range(8)]
 
 
 def _home_pairs(turn):
@@ -54,35 +48,38 @@
 
     scale = inv_root[None, :]
     terms = jnp.concatenate([_dot(direct, right_vecs * scale), _dot(adjoint, left_vecs * scale)], axis=1)
-    half = cells // 2
-    away = lax.ppermute(lax.dynamic_slice_in_dim(terms, (1 - h) * half, half, 0), "h", SWAP)
+    terms = terms.reshape(2, 16, cells // 32, 2 * modes).transpose(1, 0, 2, 3).reshape(cells, 2 * modes)
+    terms, kept = lax.optimization_barrier((terms, adjoint))
+    part = lax.psum_scatter(terms, ("g", "q"), scatter_dimension=0, tiled=True)
+    part = part.reshape(2, cells // 32, 2 * modes)
+
     next_direct = lax.ppermute(direct, "q", SWAP)
-    next_own = lax.ppermute(adjoint, ("c", "g"), _ring_pairs(False))
-    other = lax.ppermute(adjoint, "c", SWAP)
-    next_other = lax.ppermute(other, ("c", "g"), _ring_pairs(False))
-    own = jnp.where(c == 0, adjoint, next_own)
-    other = jnp.where(c == 0, other, next_other)
-
-    terms = away + lax.dynamic_slice_in_dim(terms, h * half, half, 0)
-    summed = lax.psum_scatter(terms, ("g", "q"), scatter_dimension=0, tiled=True)
-
+    other = lax.ppermute(kept, "c", SWAP)
     pair = _beside(q, direct, next_direct) * cell_weight[:, None]
     both = _beside(h, pair, lax.ppermute(pair, "h", SWAP))
     other_both = lax.ppermute(both, "c", SWAP)
 
-    pieces = []
-    for step in range(4):
-        product = _cross(own, both) + _cross(other, other_both)
-        piece = jnp.stack([product[:, k * cols : (k + 1) * cols] for k in range(4)])
-        if step < 3:
-            own = lax.ppermute(own, ("c", "g"), _ring_pairs(True))
-            other = lax.ppermute(other, ("c", "g"), _ring_pairs(True))
-        pieces.append(lax.optimization_barrier(piece))
-        if step == 2:
-            early = lax.all_to_all(jnp.concatenate(pieces[:2]), ("x", "l"), 0, 0, tiled=True).sum(0)
-            own, other, pieces, early = lax.optimization_barrier((own, other, pieces, early))
+    def product(mine, theirs):
+        return _cross(mine, both) + _cross(theirs, other_both)
 
-    late = lax.all_to_all(jnp.concatenate(pieces[2:]), ("x", "l"), 0, 0, tiled=True).sum(0)
+    def pieces(below, above):
+        rows = jnp.where(c == 0, below, above)
+        return lax.optimization_barrier(jnp.stack([rows[:, k * cols : (k + 1) * cols] for k in range(4)]))
+
+    own = adjoint
+    products = [product(own, other)]
+    for _ in range(3):
+        own = lax.ppermute(own, ("c", "g"), RING)
+        other = lax.ppermute(other, ("c", "g"), RING)
+        products.append(product(own, other))
+    own = lax.ppermute(own, ("c", "g"), RING)
+    first = jnp.concatenate([pieces(products[0], products[1]), pieces(products[1], products[2])])
+    early = lax.all_to_all(first, ("x", "l"), 0, 0, tiled=True).sum(0)
+    own, early = lax.optimization_barrier((own, early))
+    opposite = _cross(own, both)
+    opposite = opposite + lax.ppermute(opposite, "c", SWAP)
+    second = jnp.concatenate([pieces(products[2], products[3]), pieces(products[3], opposite)])
+    late = lax.all_to_all(second, ("x", "l"), 0, 0, tiled=True).sum(0)
     home0 = lax.ppermute(jnp.where(q == 0, early, late), AXES, _home_pairs(0))
     home1 = lax.ppermute(jnp.where(q == 0, late, early), AXES, _home_pairs(1))
 
@@ -90,6 +87,10 @@
     behind = (lax.axis_index("g") - low) % 8
     arrival = jnp.where(behind < 4, behind, 7 - behind)
     gram = jnp.where(arrival < 2, jnp.concatenate([home0, home1]), jnp.concatenate([home1, home0]))
+
+    keep = lax.dynamic_index_in_dim(part, h, 0, keepdims=False)
+    away = lax.dynamic_index_in_dim(part, 1 - h, 0, keepdims=False)
+    summed = keep + lax.ppermute(away, "h", SWAP)
     return (gram, summed[:, :modes], summed[:, modes:])
 
 

time: 155 us -> 161 us (1.039)
  the two profiles are of different devices: /device:TPU:12 before, /device:TPU:24 now
where the time goes in v5:
time: 161 us; the launch traced here: 160 us
  waiting for transfers between devices  63.4 us (39%)
  starting transfers between devices  60.6 us (38%)
  matrix products  14.5 us (9%)
  between operations  14.5 us (9%)
  local copies, waits for them, and re-layouts  3.74 us (2%)
  other arithmetic  3.29 us (2%)
    reduce_scatter x1, waiting for transfers between devices, local(): part = lax.psum_scatter(terms, ('g', 'q'), scatter_dimension=0, tiled=True)  18.2 us
    dot_general x9, matrix products, _cross(): lax.dot_general(a, b, (((0,), (0,)), ((), ())), precision=PREC, preferred...  13.7 us
    ppermute x3, starting transfers between devices, local(): other = lax.ppermute(other, ('c', 'g'), RING)  13 us
    ppermute x4, starting transfers between devices, local(): own = lax.ppermute(own, ('c', 'g'), RING)  11.9 us
    ppermute x3, waiting for transfers between devices, local(): other = lax.ppermute(other, ('c', 'g'), RING)  10.6 us
    ppermute x4, waiting for transfers between devices, local(): own = lax.ppermute(own, ('c', 'g'), RING)  9.75 us
    ppermute x1, waiting for transfers between devices, local(): both = _beside(h, pair, lax.ppermute(pair, 'h', SWAP))  8.74 us
    ppermute x1, waiting for transfers between devices, local(): home1 = lax.ppermute(jnp.where(q == 0, late, early), AXES, _home_pairs(1))  5.85 us
  transfers between devices with their start and end apart: 18, of which 11 were waited for; matrix products, arithmetic and copies ran while one was open for 13% of the time, Pallas kernels for 0%

profile of v5, /device:TPU:24, one launch (start us, length us, event | category | flops | bytes accessed | tf_op | source)
XLA Modules:
  0.0 160.1 jit_solution(10114222864611680233)
XLA Ops:
  7.2 3.8 %collective-permute-start.4 = (f32[512,128]{1,0:T(8,128)}, f32[512,128]{1,0:T(8,128)S(1)}, u32[]{:S(2)}, u32[]{:S(2)}) collective-permute-start(f32[512,128]{1,0:T(8,128)} %param.6), channel_id=1, source_target_pairs={{0,1},{1,0},{2,3},{3,2},{4,5},{5,4},{6,7},{7,6},{8,9},{9,8},{10,11... | collective-permute-start | bytes 786440 | tf_op jit(solution)/shard_map/ppermute | solution.py:56
  11.0 5.2 %collective-permute-start = (f32[512,128]{1,0:T(8,128)}, f32[512,128]{1,0:T(8,128)}, u32[]{:S(2)}, u32[]{:S(2)}) collective-permute-start(f32[512,128]{1,0:T(8,128)} %param.7), channel_id=1, source_target_pairs={{0,2},{2,4},{4,6},{6,8},{8,10},{10,12},{12,14},{14,0},{32,46},{34,... | collective-permute-start | bytes 786440 | tf_op jit(solution)/shard_map/ppermute | solution.py:72
  16.3 4.1 %collective-permute-done.4 = f32[512,128]{1,0:T(8,128)S(1)} collective-permute-done((f32[512,128]{1,0:T(8,128)}, f32[512,128]{1,0:T(8,128)S(1)}, u32[]{:S(2)}, u32[]{:S(2)}) %collective-permute-start.4) | collective-permute-done | bytes 262176 | tf_op jit(solution)/shard_map/ppermute | solution.py:56
  20.4 1.2 fusion.2
  21.6 3.3 %collective-permute-start.5 = (f32[512,256]{1,0:T(8,128)S(1)}, f32[512,256]{1,0:T(8,128)S(1)}, u32[]{:S(2)}, u32[]{:S(2)}) collective-permute-start(f32[512,256]{1,0:T(8,128)S(1)} %fusion.2), channel_id=1, source_target_pairs={{0,16},{16,0},{1,17},{17,1},{2,18},{18,2},{3,19},{19,3},{4,20},{20... | collective-permute-start | bytes 1572872 | tf_op jit(solution)/shard_map/ppermute | solution.py:59
  24.9 0.4 convolution_bitcast_fusion.1
  25.3 0.4 convolution_bitcast_fusion
  25.8 0.3 copy.23
  26.2 1.1 copy.24
  27.3 3.2 %collective-permute-start.6 = (f32[512,128]{1,0:T(8,128)S(1)}, f32[512,128]{1,0:T(8,128)}, u32[]{:S(2)}, u32[]{:S(2)}) collective-permute-start(f32[512,128]{1,0:T(8,128)S(1)} %copy-done), channel_id=1, source_target_pairs={{0,32},{32,0},{1,33},{33,1},{2,34},{34,2},{3,35},{35,3},{4,36},{36... | collective-permute-start | bytes 786440 | tf_op jit(solution)/shard_map/ppermute | solution.py:57
  30.5 8.7 %collective-permute-done.5 = f32[512,256]{1,0:T(8,128)S(1)} collective-permute-done((f32[512,256]{1,0:T(8,128)S(1)}, f32[512,256]{1,0:T(8,128)S(1)}, u32[]{:S(2)}, u32[]{:S(2)}) %collective-permute-start.5) | collective-permute-done | bytes 524320 | tf_op jit(solution)/shard_map/ppermute | solution.py:59
  39.3 0.2 maximum_select_fusion
  39.5 2.4 %collective-permute-start.7 = (f32[512,512]{1,0:T(8,128)S(1)}, f32[512,512]{1,0:T(8,128)S(1)}, u32[]{:S(2)}, u32[]{:S(2)}) collective-permute-start(f32[512,512]{1,0:T(8,128)S(1)} %maximum_select_fusion), channel_id=1, source_target_pairs={{0,32},{32,0},{1,33},{33,1},{2,34},{34,2},{3,35},{35,3},{4,36},{36... | collective-permute-start | bytes 3145736 | tf_op jit(solution)/shard_map/ppermute | solution.py:60
  41.8 1.9 %collective-permute-start.1 = (f32[512,128]{1,0:T(8,128)}, f32[512,128]{1,0:T(8,128)}, u32[]{:S(2)}, u32[]{:S(2)}) collective-permute-start(f32[512,128]{1,0:T(8,128)} %collective-permute-done), channel_id=1, source_target_pairs={{0,2},{2,4},{4,6},{6,8},{8,10},{10,12},{12,14},{14,0},{32,46},{34,... | collective-permute-start | bytes 786440 | tf_op jit(solution)/shard_map/ppermute | solution.py:72
  43.8 5.2 %collective-permute-start.8 = (f32[512,128]{1,0:T(8,128)}, f32[512,128]{1,0:T(8,128)S(1)}, u32[]{:S(2)}, u32[]{:S(2)}) collective-permute-start(f32[512,128]{1,0:T(8,128)} %collective-permute-done.6), channel_id=1, source_target_pairs={{0,2},{2,4},{4,6},{6,8},{8,10},{10,12},{12,14},{14,0},{32,46},{34,... | collective-permute-start | bytes 786440 | tf_op jit(solution)/shard_map/ppermute | solution.py:73
  49.0 6.5 %collective-permute-done.1 = f32[512,128]{1,0:T(8,128)} collective-permute-done((f32[512,128]{1,0:T(8,128)}, f32[512,128]{1,0:T(8,128)}, u32[]{:S(2)}, u32[]{:S(2)}) %collective-permute-start.1) | collective-permute-done | bytes 262176 | tf_op jit(solution)/shard_map/ppermute | solution.py:72
  55.5 1.9 %collective-permute-start.2 = (f32[512,128]{1,0:T(8,128)}, f32[512,128]{1,0:T(8,128)}, u32[]{:S(2)}, u32[]{:S(2)}) collective-permute-start(f32[512,128]{1,0:T(8,128)} %collective-permute-done.1), channel_id=1, source_target_pairs={{0,2},{2,4},{4,6},{6,8},{8,10},{10,12},{12,14},{14,0},{32,46},{34,... | collective-permute-start | bytes 786440 | tf_op jit(solution)/shard_map/ppermute | solution.py:72
  57.5 4.5 %collective-permute-done.8 = f32[512,128]{1,0:T(8,128)S(1)} collective-permute-done((f32[512,128]{1,0:T(8,128)}, f32[512,128]{1,0:T(8,128)S(1)}, u32[]{:S(2)}, u32[]{:S(2)}) %collective-permute-start.8) | collective-permute-done | bytes 262176 | tf_op jit(solution)/shard_map/ppermute | solution.py:73
  62.0 1.9 %collective-permute-start.9 = (f32[512,128]{1,0:T(8,128)S(1)}, f32[512,128]{1,0:T(8,128)S(1)}, u32[]{:S(2)}, u32[]{:S(2)}) collective-permute-start(f32[512,128]{1,0:T(8,128)S(1)} %collective-permute-done.8), channel_id=1, source_target_pairs={{0,2},{2,4},{4,6},{6,8},{8,10},{10,12},{12,14},{14,0},{32,46},{34,... | collective-permute-start | bytes 786440 | tf_op jit(solution)/shard_map/ppermute | solution.py:73
  63.9 1.9 %convolution_bitcast_fusion.3 = f32[128,512]{0,1:T(8,128)S(1)} fusion(f32[512,512]{1,0:T(8,128)S(1)} %maximum_select_fusion, f32[512,128]{1,0:T(8,128)} %collective-permute-done.1), kind=kOutput, calls=%fused_computation.3 | convolution fusion | flops 201326592 | bytes 1572864 | tf_op jit(solution)/shard_map/dot_general | solution.py:35
  65.9 1.9 %convolution_bitcast_fusion.4 = f32[128,512]{0,1:T(8,128)S(1)} fusion(f32[512,512]{1,0:T(8,128)S(1)} %maximum_select_fusion, f32[512,128]{1,0:T(8,128)} %collective-permute-done), kind=kOutput, calls=%fused_computation.4 | convolution fusion | flops 201326592 | bytes 1572864 | tf_op jit(solution)/shard_map/dot_general | solution.py:35
  67.8 1.9 %fusion.8 = f32[128,512]{0,1:T(8,128)S(1)} fusion(f32[512,128]{1,0:T(8,128)} %collective-permute-done.6, f32[512,512]{1,0:T(8,128)S(1)} %collective-permute-done.7), kind=kOutput, calls=%fused_computation.50 | convolution fusion | flops 201326592 | bytes 1572864 | tf_op jit(solution)/shard_map/dot_general | solution.py:35
  69.8 6.0 %collective-permute-done.9 = f32[512,128]{1,0:T(8,128)S(1)} collective-permute-done((f32[512,128]{1,0:T(8,128)S(1)}, f32[512,128]{1,0:T(8,128)S(1)}, u32[]{:S(2)}, u32[]{:S(2)}) %collective-permute-start.9) | collective-permute-done | bytes 262176 | tf_op jit(solution)/shard_map/ppermute | solution.py:73
  75.8 1.0 convolution_add_fusion.1
  76.8 1.0 broadcast_select_fusion.1
  77.8 1.0 fusion.1
  78.9 0.8 pad_maximum_fusion.1
  79.8 5.8 %all-to-all-start = ((f32[8,128,128]{1,2,0:T(8,128)}), f32[8,128,128]{1,2,0:T(8,128)S(1)}, u32[]{:S(2)}, u32[]{:S(2)}) async-start(f32[8,128,128]{1,2,0:T(8,128)} %pad_maximum_fusion.1), calls=%async_computation | async-start | bytes 1048576 | tf_op jit(solution)/shard_map/all_to_all | solution.py:77
  85.6 2.9 %collective-permute-start.3 = (f32[512,128]{1,0:T(8,128)}, f32[512,128]{1,0:T(8,128)}, u32[]{:S(2)}, u32[]{:S(2)}) collective-permute-start(f32[512,128]{1,0:T(8,128)} %collective-permute-done.2), channel_id=1, source_target_pairs={{0,2},{2,4},{4,6},{6,8},{8,10},{10,12},{12,14},{14,0},{32,46},{34,... | collective-permute-start | bytes 786440 | tf_op jit(solution)/shard_map/ppermute | solution.py:75
  88.4 5.9 %collective-permute-start.10 = (f32[512,128]{1,0:T(8,128)S(1)}, f32[512,128]{1,0:T(8,128)S(1)}, u32[]{:S(2)}, u32[]{:S(2)}) collective-permute-start(f32[512,128]{1,0:T(8,128)S(1)} %collective-permute-done.9), channel_id=1, source_target_pairs={{0,2},{2,4},{4,6},{6,8},{8,10},{10,12},{12,14},{14,0},{32,46},{34,... | collective-permute-start | bytes 786440 | tf_op jit(solution)/shard_map/ppermute | solution.py:73
  94.3 0.2 all-to-all-done
  94.6 3.2 %collective-permute-done.3 = f32[512,128]{1,0:T(8,128)} collective-permute-done((f32[512,128]{1,0:T(8,128)}, f32[512,128]{1,0:T(8,128)}, u32[]{:S(2)}, u32[]{:S(2)}) %collective-permute-start.3) | collective-permute-done | bytes 262176 | tf_op jit(solution)/shard_map/ppermute | solution.py:75
  97.8 1.9 %fusion.9 = f32[128,512]{0,1:T(8,128)S(1)} fusion(f32[512,128]{1,0:T(8,128)} %collective-permute-done.3, f32[512,512]{1,0:T(8,128)S(1)} %maximum_select_fusion), kind=kOutput, calls=%fused_computation.51 | convolution fusion | flops 201326592 | bytes 1572864 | tf_op jit(solution)/shard_map/dot_general | solution.py:35
  99.8 1.9 %collective-permute-start.11 = (f32[128,512]{0,1:T(8,128)S(1)}, f32[128,512]{0,1:T(8,128)S(1)}, u32[]{:S(2)}, u32[]{:S(2)}) collective-permute-start(f32[128,512]{0,1:T(8,128)S(1)} %fusion.9), channel_id=1, source_target_pairs={{0,32},{32,0},{1,33},{33,1},{2,34},{34,2},{3,35},{35,3},{4,36},{36... | collective-permute-start | bytes 786440 | tf_op jit(solution)/shard_map/ppermute | solution.py:80
  101.7 1.9 %convolution_bitcast_fusion.2 = f32[128,512]{0,1:T(8,128)S(1)} fusion(f32[512,512]{1,0:T(8,128)S(1)} %maximum_select_fusion, f32[512,128]{1,0:T(8,128)} %collective-permute-done.2), kind=kOutput, calls=%fused_computation.2 | convolution fusion | flops 201326592 | bytes 1572864 | tf_op jit(solution)/shard_map/dot_general | solution.py:35
  103.7 1.0 broadcast_select_fusion
  104.8 0.8 pad_maximum_fusion.2
  105.6 5.7 %all-to-all-start.1 = ((f32[8,128,128]{1,2,0:T(8,128)}), f32[8,128,128]{1,2,0:T(8,128)S(1)}, u32[]{:S(2)}, u32[]{:S(2)}) async-start(f32[8,128,128]{1,2,0:T(8,128)} %pad_maximum_fusion.2), calls=%async_computation.1 | async-start | bytes 1048576 | tf_op jit(solution)/shard_map/all_to_all | solution.py:82
  111.3 18.2 %reduce-scatter.2.cloned.1.call-done = f32[32,512]{1,0:T(8,128)} async-done(((f32[512,512]{1,0:T(8,128)}), f32[32,512]{1,0:T(8,128)}) %reduce-scatter.2.cloned.1.call-update) | async-done | bytes 65552 | tf_op jit(solution)/shard_map/reduce_scatter | solution.py:53
  129.5 0.8 dynamic-slice_bitcast_fusion
  130.4 2.7 %collective-permute-start.14 = (f32[16,512]{1,0:T(8,128)S(1)}, f32[16,512]{1,0:T(8,128)S(1)}, u32[]{:S(2)}, u32[]{:S(2)}) collective-permute-start(f32[16,512]{1,0:T(8,128)S(1)} %dynamic-slice_bitcast_fusion), channel_id=1, source_target_pairs={{0,16},{16,0},{1,17},{17,1},{2,18},{18,2},{3,19},{19,3},{4,20},{20... | collective-permute-start | bytes 98312 | tf_op jit(solution)/shard_map/ppermute | solution.py:93
  133.1 4.6 %collective-permute-done.14 = f32[16,512]{1,0:T(8,128)S(1)} collective-permute-done((f32[16,512]{1,0:T(8,128)S(1)}, f32[16,512]{1,0:T(8,128)S(1)}, u32[]{:S(2)}, u32[]{:S(2)}) %collective-permute-start.14) | collective-permute-done | bytes 32800 | tf_op jit(solution)/shard_map/ppermute | solution.py:93
  137.7 4.9 %collective-permute-start.12 = (f32[128,128]{0,1:T(8,128)S(1)}, f32[128,128]{0,1:T(8,128)S(1)}, u32[]{:S(2)}, u32[]{:S(2)}) collective-permute-start(f32[128,128]{0,1:T(8,128)S(1)} %get-tuple-element.32), channel_id=1, source_target_pairs={{0,0},{1,192},{2,34},{3,226},{4,68},{5,4},{6,102},{7,38},{8,136},{... | collective-permute-start | bytes 196616 | tf_op jit(solution)/shard_map/ppermute | solution.py:83
  142.7 1.9 %collective-permute-start.13 = (f32[128,128]{0,1:T(8,128)S(1)}, f32[128,128]{0,1:T(8,128)S(1)}, u32[]{:S(2)}, u32[]{:S(2)}) collective-permute-start(f32[128,128]{0,1:T(8,128)S(1)} %get-tuple-element.33), channel_id=1, source_target_pairs={{0,192},{1,0},{2,226},{3,34},{4,4},{5,68},{6,38},{7,102},{8,72},{9... | collective-permute-start | bytes 196616 | tf_op jit(solution)/shard_map/ppermute | solution.py:84
  144.6 0.6 fusion.7
  145.2 1.4 collective-permute-done.12
  146.7 5.8 %collective-permute-done.13 = f32[128,128]{0,1:T(8,128)S(1)} collective-permute-done((f32[128,128]{0,1:T(8,128)S(1)}, f32[128,128]{0,1:T(8,128)S(1)}, u32[]{:S(2)}, u32[]{:S(2)}) %collective-permute-start.13) | collective-permute-done | bytes 65568 | tf_op jit(solution)/shard_map/ppermute | solution.py:84
  152.5 0.8 copy.31
  (36 shorter events, 0.4 us)
Async XLA Ops:
  7.2 122.4 %reduce-scatter.2.cloned.1.call-start = ((), (), s32[]{:S(2)}) async-start(), calls=%async_computation.3 | async-start | bytes 1114112 | tf_op jit(solution)/shard_map/reduce_scatter | solution.py:53
  7.2 13.1 %collective-permute-start.4 = (f32[512,128]{1,0:T(8,128)}, f32[512,128]{1,0:T(8,128)S(1)}, u32[]{:S(2)}, u32[]{:S(2)}) collective-permute-start(f32[512,128]{1,0:T(8,128)} %param.6), channel_id=1, source_target_pairs={{0,1},{1,0},{2,3},{3,2},{4,5},{5,4},{6,7},{7,6},{8,9},{9,8},{10,11... | collective-permute-start | bytes 786440 | tf_op jit(solution)/shard_map/ppermute | solution.py:56
  11.0 30.8 %collective-permute-start = (f32[512,128]{1,0:T(8,128)}, f32[512,128]{1,0:T(8,128)}, u32[]{:S(2)}, u32[]{:S(2)}) collective-permute-start(f32[512,128]{1,0:T(8,128)} %param.7), channel_id=1, source_target_pairs={{0,2},{2,4},{4,6},{6,8},{8,10},{10,12},{12,14},{14,0},{32,46},{34,... | collective-permute-start | bytes 786440 | tf_op jit(solution)/shard_map/ppermute | solution.py:72
  16.2 4.1 %copy-start.6 = (f32[512]{0:T(512)S(1)}, f32[512]{0:T(512)}, u32[]{:S(2)}) copy-start(f32[512]{0:T(512)} %param.8) | copy-start | bytes 6148
  16.3 8.6 %copy-start.1 = (f32[512,128]{1,0:T(8,128)S(1)}, f32[512,128]{1,0:T(8,128)}, u32[]{:S(2)}) copy-start(f32[512,128]{1,0:T(8,128)} %param.6) | copy-start | bytes 786436
  16.3 8.6 %copy-start.2 = (f32[128,256]{1,0:T(8,128)S(1)}, f32[128,256]{1,0:T(8,128)}, u32[]{:S(2)}) copy-start(f32[128,256]{1,0:T(8,128)} %param.9) | copy-start | bytes 393220
  16.3 8.6 %copy-start.5 = (f32[256]{0:T(256)S(1)}, f32[256]{0:T(256)}, u32[]{:S(2)}) copy-start(f32[256]{0:T(256)} %param.11) | copy-start | bytes 3076
  21.6 3.8 %copy-start = (f32[512,128]{1,0:T(8,128)S(1)}, f32[512,128]{1,0:T(8,128)}, u32[]{:S(2)}) copy-start(f32[512,128]{1,0:T(8,128)} %param.7) | copy-start | bytes 786436
  21.6 3.8 %copy-start.3 = (f32[128,256]{1,0:T(8,128)S(1)}, f32[128,256]{1,0:T(8,128)}, u32[]{:S(2)}) copy-start(f32[128,256]{1,0:T(8,128)} %param.10) | copy-start | bytes 393220
  21.6 17.7 %collective-permute-start.5 = (f32[512,256]{1,0:T(8,128)S(1)}, f32[512,256]{1,0:T(8,128)S(1)}, u32[]{:S(2)}, u32[]{:S(2)}) collective-permute-start(f32[512,256]{1,0:T(8,128)S(1)} %fusion.2), channel_id=1, source_target_pairs={{0,16},{16,0},{1,17},{17,1},{2,18},{18,2},{3,19},{19,3},{4,20},{20... | collective-permute-start | bytes 1572872 | tf_op jit(solution)/shard_map/ppermute | solution.py:59
  27.3 16.5 %collective-permute-start.6 = (f32[512,128]{1,0:T(8,128)S(1)}, f32[512,128]{1,0:T(8,128)}, u32[]{:S(2)}, u32[]{:S(2)}) collective-permute-start(f32[512,128]{1,0:T(8,128)S(1)} %copy-done), channel_id=1, source_target_pairs={{0,32},{32,0},{1,33},{33,1},{2,34},{34,2},{3,35},{35,3},{4,36},{36... | collective-permute-start | bytes 786440 | tf_op jit(solution)/shard_map/ppermute | solution.py:57
  39.5 28.4 %collective-permute-start.7 = (f32[512,512]{1,0:T(8,128)S(1)}, f32[512,512]{1,0:T(8,128)S(1)}, u32[]{:S(2)}, u32[]{:S(2)}) collective-permute-start(f32[512,512]{1,0:T(8,128)S(1)} %maximum_select_fusion), channel_id=1, source_target_pairs={{0,32},{32,0},{1,33},{33,1},{2,34},{34,2},{3,35},{35,3},{4,36},{36... | collective-permute-start | bytes 3145736 | tf_op jit(solution)/shard_map/ppermute | solution.py:60
  41.8 13.7 %collective-permute-start.1 = (f32[512,128]{1,0:T(8,128)}, f32[512,128]{1,0:T(8,128)}, u32[]{:S(2)}, u32[]{:S(2)}) collective-permute-start(f32[512,128]{1,0:T(8,128)} %collective-permute-done), channel_id=1, source_target_pairs={{0,2},{2,4},{4,6},{6,8},{8,10},{10,12},{12,14},{14,0},{32,46},{34,... | collective-permute-start | bytes 786440 | tf_op jit(solution)/shard_map/ppermute | solution.py:72
  43.8 18.2 %collective-permute-start.8 = (f32[512,128]{1,0:T(8,128)}, f32[512,128]{1,0:T(8,128)S(1)}, u32[]{:S(2)}, u32[]{:S(2)}) collective-permute-start(f32[512,128]{1,0:T(8,128)} %collective-permute-done.6), channel_id=1, source_target_pairs={{0,2},{2,4},{4,6},{6,8},{8,10},{10,12},{12,14},{14,0},{32,46},{34,... | collective-permute-start | bytes 786440 | tf_op jit(solution)/shard_map/ppermute | solution.py:73
  55.5 30.0 %collective-permute-start.2 = (f32[512,128]{1,0:T(8,128)}, f32[512,128]{1,0:T(8,128)}, u32[]{:S(2)}, u32[]{:S(2)}) collective-permute-start(f32[512,128]{1,0:T(8,128)} %collective-permute-done.1), channel_id=1, source_target_pairs={{0,2},{2,4},{4,6},{6,8},{8,10},{10,12},{12,14},{14,0},{32,46},{34,... | collective-permute-start | bytes 786440 | tf_op jit(solution)/shard_map/ppermute | solution.py:72
  62.0 13.8 %collective-permute-start.9 = (f32[512,128]{1,0:T(8,128)S(1)}, f32[512,128]{1,0:T(8,128)S(1)}, u32[]{:S(2)}, u32[]{:S(2)}) collective-permute-start(f32[512,128]{1,0:T(8,128)S(1)} %collective-permute-done.8), channel_id=1, source_target_pairs={{0,2},{2,4},{4,6},{6,8},{8,10},{10,12},{12,14},{14,0},{32,46},{34,... | collective-permute-start | bytes 786440 | tf_op jit(solution)/shard_map/ppermute | solution.py:73
  79.8 14.8 %all-to-all-start = ((f32[8,128,128]{1,2,0:T(8,128)}), f32[8,128,128]{1,2,0:T(8,128)S(1)}, u32[]{:S(2)}, u32[]{:S(2)}) async-start(f32[8,128,128]{1,2,0:T(8,128)} %pad_maximum_fusion.1), calls=%async_computation | async-start | bytes 1048576 | tf_op jit(solution)/shard_map/all_to_all | solution.py:77
  85.6 12.3 %collective-permute-start.3 = (f32[512,128]{1,0:T(8,128)}, f32[512,128]{1,0:T(8,128)}, u32[]{:S(2)}, u32[]{:S(2)}) collective-permute-start(f32[512,128]{1,0:T(8,128)} %collective-permute-done.2), channel_id=1, source_target_pairs={{0,2},{2,4},{4,6},{6,8},{8,10},{10,12},{12,14},{14,0},{32,46},{34,... | collective-permute-start | bytes 786440 | tf_op jit(solution)/shard_map/ppermute | solution.py:75
  88.4 15.2 %collective-permute-start.10 = (f32[512,128]{1,0:T(8,128)S(1)}, f32[512,128]{1,0:T(8,128)S(1)}, u32[]{:S(2)}, u32[]{:S(2)}) collective-permute-start(f32[512,128]{1,0:T(8,128)S(1)} %collective-permute-done.9), channel_id=1, source_target_pairs={{0,2},{2,4},{4,6},{6,8},{8,10},{10,12},{12,14},{14,0},{32,46},{34,... | collective-permute-start | bytes 786440 | tf_op jit(solution)/shard_map/ppermute | solution.py:73
  99.8 3.9 %collective-permute-start.11 = (f32[128,512]{0,1:T(8,128)S(1)}, f32[128,512]{0,1:T(8,128)S(1)}, u32[]{:S(2)}, u32[]{:S(2)}) collective-permute-start(f32[128,512]{0,1:T(8,128)S(1)} %fusion.9), channel_id=1, source_target_pairs={{0,32},{32,0},{1,33},{33,1},{2,34},{34,2},{3,35},{35,3},{4,36},{36... | collective-permute-start | bytes 786440 | tf_op jit(solution)/shard_map/ppermute | solution.py:80
  105.6 32.1 %all-to-all-start.1 = ((f32[8,128,128]{1,2,0:T(8,128)}), f32[8,128,128]{1,2,0:T(8,128)S(1)}, u32[]{:S(2)}, u32[]{:S(2)}) async-start(f32[8,128,128]{1,2,0:T(8,128)} %pad_maximum_fusion.2), calls=%async_computation.1 | async-start | bytes 1048576 | tf_op jit(solution)/shard_map/all_to_all | solution.py:82
  129.5 8.1 %copy-start.4 = (f32[32,512]{1,0:T(8,128)S(1)}, f32[32,512]{1,0:T(8,128)}, u32[]{:S(2)}) copy-start(f32[32,512]{1,0:T(8,128)} %reduce-scatter.2.cloned.1.call-done) | copy-start | bytes 196612
  130.4 7.3 %collective-permute-start.14 = (f32[16,512]{1,0:T(8,128)S(1)}, f32[16,512]{1,0:T(8,128)S(1)}, u32[]{:S(2)}, u32[]{:S(2)}) collective-permute-start(f32[16,512]{1,0:T(8,128)S(1)} %dynamic-slice_bitcast_fusion), channel_id=1, source_target_pairs={{0,16},{16,0},{1,17},{17,1},{2,18},{18,2},{3,19},{19,3},{4,20},{20... | collective-permute-start | bytes 98312 | tf_op jit(solution)/shard_map/ppermute | solution.py:93
  137.7 8.9 %collective-permute-start.12 = (f32[128,128]{0,1:T(8,128)S(1)}, f32[128,128]{0,1:T(8,128)S(1)}, u32[]{:S(2)}, u32[]{:S(2)}) collective-permute-start(f32[128,128]{0,1:T(8,128)S(1)} %get-tuple-element.32), channel_id=1, source_target_pairs={{0,0},{1,192},{2,34},{3,226},{4,68},{5,4},{6,102},{7,38},{8,136},{... | collective-permute-start | bytes 196616 | tf_op jit(solution)/shard_map/ppermute | solution.py:83
  142.7 9.8 %collective-permute-start.13 = (f32[128,128]{0,1:T(8,128)S(1)}, f32[128,128]{0,1:T(8,128)S(1)}, u32[]{:S(2)}, u32[]{:S(2)}) collective-permute-start(f32[128,128]{0,1:T(8,128)S(1)} %get-tuple-element.33), channel_id=1, source_target_pairs={{0,192},{1,0},{2,226},{3,34},{4,4},{5,68},{6,38},{7,102},{8,72},{9... | collective-permute-start | bytes 196616 | tf_op jit(solution)/shard_map/ppermute | solution.py:84
Sparse Core Ops, SparseCore 0:
  49.2 80.3 reduce-scatter.1

commit v6 on v4

--- a/solution.py
+++ b/solution.py
@@ -57,17 +57,14 @@
     other = lax.ppermute(adjoint, "c", SWAP)
     scale = inv_root[None, :]
     terms = jnp.concatenate([_dot(direct, right_vecs * scale), _dot(adjoint, left_vecs * scale)], axis=1)
-    rows = cells // 32
-    terms = terms.reshape(2, 8, 2, rows, 2 * modes).transpose(2, 1, 0, 3, 4).reshape(2, cells // 2, 2 * modes)
-    away = lax.dynamic_index_in_dim(terms, 1 - q, 0, keepdims=False)
-    away, other = lax.optimization_barrier((away, other))
-    away = lax.ppermute(away, "q", SWAP)
+    terms = terms.reshape(2, 16, cells // 32, 2 * modes).transpose(1, 0, 2, 3).reshape(cells, 2 * modes)
+    terms, other = lax.optimization_barrier((terms, other))
+    part = lax.psum_scatter(terms, ("g", "q"), scatter_dimension=0, tiled=True)
+    part = part.reshape(2, cells // 32, 2 * modes)
+
     next_other = lax.ppermute(other, ("c", "g"), _ring_pairs(False))
     own = jnp.where(c == 0, adjoint, next_own)
     other = jnp.where(c == 0, other, next_other)
-
-    terms = away + lax.dynamic_index_in_dim(terms, q, 0, keepdims=False)
-    part = lax.psum_scatter(terms, "g", scatter_dimension=0, tiled=True).reshape(2, rows, 2 * modes)
 
     pair = _beside(q, direct, next_direct) * cell_weight[:, None]
     both = _beside(h, pair, lax.ppermute(pair, "h", SWAP))

time: 171 us -> 176 us (1.029)
  the two profiles are of different devices: /device:TPU:39 before, /device:TPU:89 now
where the time goes in v6:
time: 176 us; the launch traced here: 175 us
  starting transfers between devices  89.5 us (51%)
  waiting for transfers between devices  52.1 us (30%)
  between operations  14.5 us (8%)
  matrix products  7.24 us (4%)
  local copies, waits for them, and re-layouts  6.34 us (4%)
  other arithmetic  5.01 us (3%)
    ppermute x3, starting transfers between devices, local(): own = lax.ppermute(own, ('c', 'g'), _ring_pairs(True))  23.6 us
    reduce_scatter x1, waiting for transfers between devices, local(): part = lax.psum_scatter(terms, ('g', 'q'), scatter_dimension=0, tiled=True)  22.1 us
    ppermute x1, starting transfers between devices, local(): home0 = lax.ppermute(jnp.where(q == 0, early, late), AXES, _home_pairs(0))  19 us
    ppermute x3, starting transfers between devices, local(): other = lax.ppermute(other, ('c', 'g'), _ring_pairs(True))  15 us
    dot_general x8, matrix products, _cross(): lax.dot_general(a, b, (((0,), (0,)), ((), ())), precision=PREC, preferred...  6.42 us
    ppermute x1, waiting for transfers between devices, local(): next_direct = lax.ppermute(direct, 'q', SWAP)  6.06 us
    ppermute x1, waiting for transfers between devices, local(): home1 = lax.ppermute(jnp.where(q == 0, late, early), AXES, _home_pairs(1))  6 us
    ppermute x1, waiting for transfers between devices, local(): both = _beside(h, pair, lax.ppermute(pair, 'h', SWAP))  5.74 us
  transfers between devices with their start and end apart: 18, of which 9 were waited for; matrix products, arithmetic and copies ran while one was open for 9% of the time, Pallas kernels for 0%

profile of v6, /device:TPU:89, one launch (start us, length us, event | category | flops | bytes accessed | tf_op | source)
XLA Modules:
  0.0 174.6 jit_solution(14729511285545121774)
XLA Ops:
  7.2 3.5 %collective-permute-start.9 = (f32[512,128]{1,0:T(8,128)}, f32[512,128]{1,0:T(8,128)S(1)}, u32[]{:S(2)}, u32[]{:S(2)}) collective-permute-start(f32[512,128]{1,0:T(8,128)} %param.6), channel_id=1, source_target_pairs={{0,1},{1,0},{2,3},{3,2},{4,5},{5,4},{6,7},{7,6},{8,9},{9,8},{10,11... | collective-permute-start | bytes 786440 | tf_op jit(solution)/shard_map/ppermute | solution.py:55
  10.8 6.1 %collective-permute-done.9 = f32[512,128]{1,0:T(8,128)S(1)} collective-permute-done((f32[512,128]{1,0:T(8,128)}, f32[512,128]{1,0:T(8,128)S(1)}, u32[]{:S(2)}, u32[]{:S(2)}) %collective-permute-start.9) | collective-permute-done | bytes 262176 | tf_op jit(solution)/shard_map/ppermute | solution.py:55
  16.9 1.2 fusion
  18.1 2.9 %collective-permute-start.10 = (f32[512,256]{1,0:T(8,128)S(1)}, f32[512,256]{1,0:T(8,128)S(1)}, u32[]{:S(2)}, u32[]{:S(2)}) collective-permute-start(f32[512,256]{1,0:T(8,128)S(1)} %fusion), channel_id=1, source_target_pairs={{0,16},{16,0},{1,17},{17,1},{2,18},{18,2},{3,19},{19,3},{4,20},{20... | collective-permute-start | bytes 1572872 | tf_op jit(solution)/shard_map/ppermute | solution.py:70
  21.0 1.9 %collective-permute-start = (f32[512,128]{1,0:T(8,128)S(1)}, f32[512,128]{1,0:T(8,128)}, u32[]{:S(2)}, u32[]{:S(2)}) collective-permute-start(f32[512,128]{1,0:T(8,128)S(1)} %copy-done.1), channel_id=1, source_target_pairs={{32,46},{34,32},{36,34},{38,36},{40,38},{42,40},{44,42},{46,44},{3... | collective-permute-start | bytes 786440 | tf_op jit(solution)/shard_map/ppermute | solution.py:56
  22.9 3.0 %collective-permute-start.4 = (f32[512,128]{1,0:T(8,128)S(1)}, f32[512,128]{1,0:T(8,128)}, u32[]{:S(2)}, u32[]{:S(2)}) collective-permute-start(f32[512,128]{1,0:T(8,128)S(1)} %copy-done.1), channel_id=1, source_target_pairs={{0,32},{32,0},{1,33},{33,1},{2,34},{34,2},{3,35},{35,3},{4,36},{36... | collective-permute-start | bytes 786440 | tf_op jit(solution)/shard_map/ppermute | solution.py:57
  25.9 0.6 copy-done.5
  26.6 0.4 convolution_bitcast_fusion.1
  27.0 0.5 copy-done.3
  27.5 0.4 convolution_bitcast_fusion
  27.9 5.7 %collective-permute-done.10 = f32[512,256]{1,0:T(8,128)S(1)} collective-permute-done((f32[512,256]{1,0:T(8,128)S(1)}, f32[512,256]{1,0:T(8,128)S(1)}, u32[]{:S(2)}, u32[]{:S(2)}) %collective-permute-start.10) | collective-permute-done | bytes 524320 | tf_op jit(solution)/shard_map/ppermute | solution.py:70
  33.6 0.2 maximum_select_fusion
  33.8 4.1 %collective-permute-start.11 = (f32[512,512]{1,0:T(8,128)S(1)}, f32[512,512]{1,0:T(8,128)S(1)}, u32[]{:S(2)}, u32[]{:S(2)}) collective-permute-start(f32[512,512]{1,0:T(8,128)S(1)} %maximum_select_fusion), channel_id=1, source_target_pairs={{0,32},{32,0},{1,33},{33,1},{2,34},{34,2},{3,35},{35,3},{4,36},{36... | collective-permute-start | bytes 3145736 | tf_op jit(solution)/shard_map/ppermute | solution.py:71
  38.0 1.3 copy.9
  39.3 2.4 %copy.10 = f32[16,2,16,512]{3,2,1,0:T(8,128)} copy(f32[16,2,16,512]{3,2,0,1:T(8,128)} %bitcast.64) | data formatting | bytes 2097152 | tf_op jit(solution)/shard_map/transpose | solution.py:60
  41.6 2.1 %collective-permute-start.5 = (f32[512,128]{1,0:T(8,128)}, f32[512,128]{1,0:T(8,128)S(1)}, u32[]{:S(2)}, u32[]{:S(2)}) collective-permute-start(f32[512,128]{1,0:T(8,128)} %collective-permute-done.4), channel_id=1, source_target_pairs={{32,46},{34,32},{36,34},{38,36},{40,38},{42,40},{44,42},{46,44},{3... | collective-permute-start | bytes 786440 | tf_op jit(solution)/shard_map/ppermute | solution.py:65
  43.8 1.0 broadcast_select_fusion.1
  44.7 10.4 %collective-permute-start.1 = (f32[512,128]{1,0:T(8,128)S(1)}, f32[512,128]{1,0:T(8,128)S(1)}, u32[]{:S(2)}, u32[]{:S(2)}) collective-permute-start(f32[512,128]{1,0:T(8,128)S(1)} %broadcast_select_fusion.1), channel_id=1, source_target_pairs={{0,2},{32,46},{2,4},{34,32},{4,6},{36,34},{6,8},{38,36},{8,10},{40... | collective-permute-start | bytes 786440 | tf_op jit(solution)/shard_map/ppermute | solution.py:78
  55.1 1.0 collective-permute-done.5
  56.2 5.8 %collective-permute-start.6 = (f32[512,128]{1,0:T(8,128)S(1)}, f32[512,128]{1,0:T(8,128)}, u32[]{:S(2)}, u32[]{:S(2)}) collective-permute-start(f32[512,128]{1,0:T(8,128)S(1)} %broadcast_select_fusion), channel_id=1, source_target_pairs={{0,2},{32,46},{2,4},{34,32},{4,6},{36,34},{6,8},{38,36},{8,10},{40... | collective-permute-start | bytes 786440 | tf_op jit(solution)/shard_map/ppermute | solution.py:79
  62.0 6.9 %collective-permute-start.2 = (f32[512,128]{1,0:T(8,128)S(1)}, f32[512,128]{1,0:T(8,128)S(1)}, u32[]{:S(2)}, u32[]{:S(2)}) collective-permute-start(f32[512,128]{1,0:T(8,128)S(1)} %collective-permute-done.1), channel_id=1, source_target_pairs={{0,2},{32,46},{2,4},{34,32},{4,6},{36,34},{6,8},{38,36},{8,10},{40... | collective-permute-start | bytes 786440 | tf_op jit(solution)/shard_map/ppermute | solution.py:78
  68.9 2.0 %collective-permute-done.6 = f32[512,128]{1,0:T(8,128)} collective-permute-done((f32[512,128]{1,0:T(8,128)S(1)}, f32[512,128]{1,0:T(8,128)}, u32[]{:S(2)}, u32[]{:S(2)}) %collective-permute-start.6) | collective-permute-done | bytes 262176 | tf_op jit(solution)/shard_map/ppermute | solution.py:79
  70.8 4.0 %collective-permute-start.7 = (f32[512,128]{1,0:T(8,128)}, f32[512,128]{1,0:T(8,128)}, u32[]{:S(2)}, u32[]{:S(2)}) collective-permute-start(f32[512,128]{1,0:T(8,128)} %collective-permute-done.6), channel_id=1, source_target_pairs={{0,2},{32,46},{2,4},{34,32},{4,6},{36,34},{6,8},{38,36},{8,10},{40... | collective-permute-start | bytes 786440 | tf_op jit(solution)/shard_map/ppermute | solution.py:79
  74.9 6.3 %collective-permute-start.3 = (f32[512,128]{1,0:T(8,128)S(1)}, f32[512,128]{1,0:T(8,128)S(1)}, u32[]{:S(2)}, u32[]{:S(2)}) collective-permute-start(f32[512,128]{1,0:T(8,128)S(1)} %collective-permute-done.2), channel_id=1, source_target_pairs={{0,2},{32,46},{2,4},{34,32},{4,6},{36,34},{6,8},{38,36},{8,10},{40... | collective-permute-start | bytes 786440 | tf_op jit(solution)/shard_map/ppermute | solution.py:78
  81.2 0.7 collective-permute-done.7
  81.9 5.2 %collective-permute-start.8 = (f32[512,128]{1,0:T(8,128)}, f32[512,128]{1,0:T(8,128)}, u32[]{:S(2)}, u32[]{:S(2)}) collective-permute-start(f32[512,128]{1,0:T(8,128)} %collective-permute-done.7), channel_id=1, source_target_pairs={{0,2},{32,46},{2,4},{34,32},{4,6},{36,34},{6,8},{38,36},{8,10},{40... | collective-permute-start | bytes 786440 | tf_op jit(solution)/shard_map/ppermute | solution.py:79
  87.2 0.4 fusion.6
  87.6 0.4 convolution_add_fusion.3
  88.1 1.4 fusion.7
  89.5 0.4 convolution_add_fusion.2
  90.0 0.9 pad_maximum_fusion.1
  90.9 5.2 %all-to-all-start = ((f32[8,128,128]{2,1,0:T(8,128)}), f32[8,128,128]{2,1,0:T(8,128)S(1)}, u32[]{:S(2)}, u32[]{:S(2)}) async-start(f32[8,128,128]{2,1,0:T(8,128)} %pad_maximum_fusion.1), calls=%async_computation | async-start | bytes 1048576 | tf_op jit(solution)/shard_map/all_to_all | solution.py:82
  96.1 1.4 fusion.8
  97.5 0.4 convolution_add_fusion.1
  98.0 5.0 %all-to-all-done = f32[8,128,128]{2,1,0:T(8,128)S(1)} async-done(((f32[8,128,128]{2,1,0:T(8,128)}), f32[8,128,128]{2,1,0:T(8,128)S(1)}, u32[]{:S(2)}, u32[]{:S(2)}) %all-to-all-start) | async-done | bytes 524320 | tf_op jit(solution)/shard_map/all_to_all | solution.py:82
  103.1 1.4 fusion.9
  104.5 0.4 convolution_add_fusion
  105.0 0.9 pad_maximum_fusion.2
  105.8 3.9 %all-to-all-start.1 = ((f32[8,128,128]{2,1,0:T(8,128)}), f32[8,128,128]{2,1,0:T(8,128)S(1)}, u32[]{:S(2)}, u32[]{:S(2)}) async-start(f32[8,128,128]{2,1,0:T(8,128)} %pad_maximum_fusion.2), calls=%async_computation.1 | async-start | bytes 1048576 | tf_op jit(solution)/shard_map/all_to_all | solution.py:85
  109.7 22.1 %reduce-scatter.2.cloned.1.call-done = f32[32,512]{1,0:T(8,128)} async-done(((f32[512,512]{1,0:T(8,128)}), f32[32,512]{1,0:T(8,128)}) %reduce-scatter.2.cloned.1.call-update) | async-done | bytes 65552 | tf_op jit(solution)/shard_map/reduce_scatter | solution.py:62
  131.8 0.8 dynamic-slice_bitcast_fusion
  132.6 2.6 %collective-permute-start.14 = (f32[16,512]{1,0:T(8,128)S(1)}, f32[16,512]{1,0:T(8,128)S(1)}, u32[]{:S(2)}, u32[]{:S(2)}) collective-permute-start(f32[16,512]{1,0:T(8,128)S(1)} %dynamic-slice_bitcast_fusion), channel_id=1, source_target_pairs={{0,16},{16,0},{1,17},{17,1},{2,18},{18,2},{3,19},{19,3},{4,20},{20... | collective-permute-start | bytes 98312 | tf_op jit(solution)/shard_map/ppermute | solution.py:96
  135.3 3.5 %collective-permute-done.14 = f32[16,512]{1,0:T(8,128)S(1)} collective-permute-done((f32[16,512]{1,0:T(8,128)S(1)}, f32[16,512]{1,0:T(8,128)S(1)}, u32[]{:S(2)}, u32[]{:S(2)}) %collective-permute-start.14) | collective-permute-done | bytes 32800 | tf_op jit(solution)/shard_map/ppermute | solution.py:96
  138.9 19.0 %collective-permute-start.12 = (f32[128,128]{1,0:T(8,128)S(1)}, f32[128,128]{1,0:T(8,128)S(1)}, u32[]{:S(2)}, u32[]{:S(2)}) collective-permute-start(f32[128,128]{1,0:T(8,128)S(1)} %get-tuple-element.31), channel_id=1, source_target_pairs={{0,0},{1,192},{2,34},{3,226},{4,68},{5,4},{6,102},{7,38},{8,136},{... | collective-permute-start | bytes 196616 | tf_op jit(solution)/shard_map/ppermute | solution.py:86
  157.9 2.6 %collective-permute-start.13 = (f32[128,128]{1,0:T(8,128)S(1)}, f32[128,128]{1,0:T(8,128)S(1)}, u32[]{:S(2)}, u32[]{:S(2)}) collective-permute-start(f32[128,128]{1,0:T(8,128)S(1)} %get-tuple-element.32), channel_id=1, source_target_pairs={{0,192},{1,0},{2,226},{3,34},{4,4},{5,68},{6,38},{7,102},{8,72},{9... | collective-permute-start | bytes 196616 | tf_op jit(solution)/shard_map/ppermute | solution.py:87
  160.5 0.6 fusion.5
  161.1 6.0 %collective-permute-done.13 = f32[128,128]{1,0:T(8,128)S(1)} collective-permute-done((f32[128,128]{1,0:T(8,128)S(1)}, f32[128,128]{1,0:T(8,128)S(1)}, u32[]{:S(2)}, u32[]{:S(2)}) %collective-permute-start.13) | collective-permute-done | bytes 65568 | tf_op jit(solution)/shard_map/ppermute | solution.py:87
  167.1 0.7 maximum_select_fusion.2
  (37 shorter events, 0.4 us)
Async XLA Ops:
  7.2 124.6 %reduce-scatter.2.cloned.1.call-start = ((), (), s32[]{:S(2)}) async-start(), calls=%async_computation.3 | async-start | bytes 1114112 | tf_op jit(solution)/shard_map/reduce_scatter | solution.py:62
  7.2 9.7 %collective-permute-start.9 = (f32[512,128]{1,0:T(8,128)}, f32[512,128]{1,0:T(8,128)S(1)}, u32[]{:S(2)}, u32[]{:S(2)}) collective-permute-start(f32[512,128]{1,0:T(8,128)} %param.6), channel_id=1, source_target_pairs={{0,1},{1,0},{2,3},{3,2},{4,5},{5,4},{6,7},{7,6},{8,9},{9,8},{10,11... | collective-permute-start | bytes 786440 | tf_op jit(solution)/shard_map/ppermute | solution.py:55
  10.8 6.1 %copy-start.6 = (f32[512]{0:T(512)S(1)}, f32[512]{0:T(512)}, u32[]{:S(2)}) copy-start(f32[512]{0:T(512)} %param.8) | copy-start | bytes 6148
  10.8 10.2 %copy-start.1 = (f32[512,128]{1,0:T(8,128)S(1)}, f32[512,128]{1,0:T(8,128)}, u32[]{:S(2)}) copy-start(f32[512,128]{1,0:T(8,128)} %param.7) | copy-start | bytes 786436
  10.8 15.1 %copy-start = (f32[512,128]{1,0:T(8,128)S(1)}, f32[512,128]{1,0:T(8,128)}, u32[]{:S(2)}) copy-start(f32[512,128]{1,0:T(8,128)} %param.6) | copy-start | bytes 786436
  10.8 15.1 %copy-start.2 = (f32[128,256]{1,0:T(8,128)S(1)}, f32[128,256]{1,0:T(8,128)}, u32[]{:S(2)}) copy-start(f32[128,256]{1,0:T(8,128)} %param.9) | copy-start | bytes 393220
  18.1 15.5 %collective-permute-start.10 = (f32[512,256]{1,0:T(8,128)S(1)}, f32[512,256]{1,0:T(8,128)S(1)}, u32[]{:S(2)}, u32[]{:S(2)}) collective-permute-start(f32[512,256]{1,0:T(8,128)S(1)} %fusion), channel_id=1, source_target_pairs={{0,16},{16,0},{1,17},{17,1},{2,18},{18,2},{3,19},{19,3},{4,20},{20... | collective-permute-start | bytes 1572872 | tf_op jit(solution)/shard_map/ppermute | solution.py:70
  21.0 22.8 %collective-permute-start = (f32[512,128]{1,0:T(8,128)S(1)}, f32[512,128]{1,0:T(8,128)}, u32[]{:S(2)}, u32[]{:S(2)}) collective-permute-start(f32[512,128]{1,0:T(8,128)S(1)} %copy-done.1), channel_id=1, source_target_pairs={{32,46},{34,32},{36,34},{38,36},{40,38},{42,40},{44,42},{46,44},{3... | collective-permute-start | bytes 786440 | tf_op jit(solution)/shard_map/ppermute | solution.py:56
  22.9 18.8 %collective-permute-start.4 = (f32[512,128]{1,0:T(8,128)S(1)}, f32[512,128]{1,0:T(8,128)}, u32[]{:S(2)}, u32[]{:S(2)}) collective-permute-start(f32[512,128]{1,0:T(8,128)S(1)} %copy-done.1), channel_id=1, source_target_pairs={{0,32},{32,0},{1,33},{33,1},{2,34},{34,2},{3,35},{35,3},{4,36},{36... | collective-permute-start | bytes 786440 | tf_op jit(solution)/shard_map/ppermute | solution.py:57
  25.9 0.7 copy-start.5
  26.6 0.9 copy-start.3
  33.8 53.4 %collective-permute-start.11 = (f32[512,512]{1,0:T(8,128)S(1)}, f32[512,512]{1,0:T(8,128)S(1)}, u32[]{:S(2)}, u32[]{:S(2)}) collective-permute-start(f32[512,512]{1,0:T(8,128)S(1)} %maximum_select_fusion), channel_id=1, source_target_pairs={{0,32},{32,0},{1,33},{33,1},{2,34},{34,2},{3,35},{35,3},{4,36},{36... | collective-permute-start | bytes 3145736 | tf_op jit(solution)/shard_map/ppermute | solution.py:71
  41.6 14.5 %collective-permute-start.5 = (f32[512,128]{1,0:T(8,128)}, f32[512,128]{1,0:T(8,128)S(1)}, u32[]{:S(2)}, u32[]{:S(2)}) collective-permute-start(f32[512,128]{1,0:T(8,128)} %collective-permute-done.4), channel_id=1, source_target_pairs={{32,46},{34,32},{36,34},{38,36},{40,38},{42,40},{44,42},{46,44},{3... | collective-permute-start | bytes 786440 | tf_op jit(solution)/shard_map/ppermute | solution.py:65
  44.7 17.2 %collective-permute-start.1 = (f32[512,128]{1,0:T(8,128)S(1)}, f32[512,128]{1,0:T(8,128)S(1)}, u32[]{:S(2)}, u32[]{:S(2)}) collective-permute-start(f32[512,128]{1,0:T(8,128)S(1)} %broadcast_select_fusion.1), channel_id=1, source_target_pairs={{0,2},{32,46},{2,4},{34,32},{4,6},{36,34},{6,8},{38,36},{8,10},{40... | collective-permute-start | bytes 786440 | tf_op jit(solution)/shard_map/ppermute | solution.py:78
  56.2 14.7 %collective-permute-start.6 = (f32[512,128]{1,0:T(8,128)S(1)}, f32[512,128]{1,0:T(8,128)}, u32[]{:S(2)}, u32[]{:S(2)}) collective-permute-start(f32[512,128]{1,0:T(8,128)S(1)} %broadcast_select_fusion), channel_id=1, source_target_pairs={{0,2},{32,46},{2,4},{34,32},{4,6},{36,34},{6,8},{38,36},{8,10},{40... | collective-permute-start | bytes 786440 | tf_op jit(solution)/shard_map/ppermute | solution.py:79
  62.0 12.9 %collective-permute-start.2 = (f32[512,128]{1,0:T(8,128)S(1)}, f32[512,128]{1,0:T(8,128)S(1)}, u32[]{:S(2)}, u32[]{:S(2)}) collective-permute-start(f32[512,128]{1,0:T(8,128)S(1)} %collective-permute-done.1), channel_id=1, source_target_pairs={{0,2},{32,46},{2,4},{34,32},{4,6},{36,34},{6,8},{38,36},{8,10},{40... | collective-permute-start | bytes 786440 | tf_op jit(solution)/shard_map/ppermute | solution.py:78
  70.8 11.1 %collective-permute-start.7 = (f32[512,128]{1,0:T(8,128)}, f32[512,128]{1,0:T(8,128)}, u32[]{:S(2)}, u32[]{:S(2)}) collective-permute-start(f32[512,128]{1,0:T(8,128)} %collective-permute-done.6), channel_id=1, source_target_pairs={{0,2},{32,46},{2,4},{34,32},{4,6},{36,34},{6,8},{38,36},{8,10},{40... | collective-permute-start | bytes 786440 | tf_op jit(solution)/shard_map/ppermute | solution.py:79
  74.9 28.2 %collective-permute-start.3 = (f32[512,128]{1,0:T(8,128)S(1)}, f32[512,128]{1,0:T(8,128)S(1)}, u32[]{:S(2)}, u32[]{:S(2)}) collective-permute-start(f32[512,128]{1,0:T(8,128)S(1)} %collective-permute-done.2), channel_id=1, source_target_pairs={{0,2},{32,46},{2,4},{34,32},{4,6},{36,34},{6,8},{38,36},{8,10},{40... | collective-permute-start | bytes 786440 | tf_op jit(solution)/shard_map/ppermute | solution.py:78
  81.9 21.1 %collective-permute-start.8 = (f32[512,128]{1,0:T(8,128)}, f32[512,128]{1,0:T(8,128)}, u32[]{:S(2)}, u32[]{:S(2)}) collective-permute-start(f32[512,128]{1,0:T(8,128)} %collective-permute-done.7), channel_id=1, source_target_pairs={{0,2},{32,46},{2,4},{34,32},{4,6},{36,34},{6,8},{38,36},{8,10},{40... | collective-permute-start | bytes 786440 | tf_op jit(solution)/shard_map/ppermute | solution.py:79
  90.9 12.1 %all-to-all-start = ((f32[8,128,128]{2,1,0:T(8,128)}), f32[8,128,128]{2,1,0:T(8,128)S(1)}, u32[]{:S(2)}, u32[]{:S(2)}) async-start(f32[8,128,128]{2,1,0:T(8,128)} %pad_maximum_fusion.1), calls=%async_computation | async-start | bytes 1048576 | tf_op jit(solution)/shard_map/all_to_all | solution.py:82
  105.8 32.9 %all-to-all-start.1 = ((f32[8,128,128]{2,1,0:T(8,128)}), f32[8,128,128]{2,1,0:T(8,128)S(1)}, u32[]{:S(2)}, u32[]{:S(2)}) async-start(f32[8,128,128]{2,1,0:T(8,128)} %pad_maximum_fusion.2), calls=%async_computation.1 | async-start | bytes 1048576 | tf_op jit(solution)/shard_map/all_to_all | solution.py:85
  131.8 7.0 %copy-start.4 = (f32[32,512]{1,0:T(8,128)S(1)}, f32[32,512]{1,0:T(8,128)}, u32[]{:S(2)}) copy-start(f32[32,512]{1,0:T(8,128)} %reduce-scatter.2.cloned.1.call-done) | copy-start | bytes 196612
  132.6 6.2 %collective-permute-start.14 = (f32[16,512]{1,0:T(8,128)S(1)}, f32[16,512]{1,0:T(8,128)S(1)}, u32[]{:S(2)}, u32[]{:S(2)}) collective-permute-start(f32[16,512]{1,0:T(8,128)S(1)} %dynamic-slice_bitcast_fusion), channel_id=1, source_target_pairs={{0,16},{16,0},{1,17},{17,1},{2,18},{18,2},{3,19},{19,3},{4,20},{20... | collective-permute-start | bytes 98312 | tf_op jit(solution)/shard_map/ppermute | solution.py:96
  138.9 22.3 %collective-permute-start.12 = (f32[128,128]{1,0:T(8,128)S(1)}, f32[128,128]{1,0:T(8,128)S(1)}, u32[]{:S(2)}, u32[]{:S(2)}) collective-permute-start(f32[128,128]{1,0:T(8,128)S(1)} %get-tuple-element.31), channel_id=1, source_target_pairs={{0,0},{1,192},{2,34},{3,226},{4,68},{5,4},{6,102},{7,38},{8,136},{... | collective-permute-start | bytes 196616 | tf_op jit(solution)/shard_map/ppermute | solution.py:86
  157.9 9.2 %collective-permute-start.13 = (f32[128,128]{1,0:T(8,128)S(1)}, f32[128,128]{1,0:T(8,128)S(1)}, u32[]{:S(2)}, u32[]{:S(2)}) collective-permute-start(f32[128,128]{1,0:T(8,128)S(1)} %get-tuple-element.32), channel_id=1, source_target_pairs={{0,192},{1,0},{2,226},{3,34},{4,4},{5,68},{6,38},{7,102},{8,72},{9... | collective-permute-start | bytes 196616 | tf_op jit(solution)/shard_map/ppermute | solution.py:87
Sparse Core Ops, SparseCore 0:
  75.0 56.7 reduce-scatter.1
